TPU v7x, 512 devices: a whole 4x4x16 slice. The times are simulated.
512 devices in a mesh: site: 64 (over y, z), vec: 8 (over x, core).
Axes of the slice: x: 4, y: 4, z: 16, core: 2. Of those that a mesh axis runs over, the one named last changes fastest.
Arguments:
- diag_blocks: float32 [512, 64, 128], P('site'), as said below
- hop_blocks: float32 [512, 4, 64, 128], P('site'), may hold values from -0.1875 to 0.1875
- neighbors: int32 [512, 8], P('site'), may hold values from 0 to 511, as said below
- start_basis: float32 [512, 128, 512], P('site', None, 'vec'), may hold values from -6 to 6
Outputs:
- basis: float32 [512, 128, 512], P('site', None, 'vec')
- projected: float32 [512, 512], P(None, 'vec')
Inputs may be any that keep to these rules, and one draw needn't show every extreme that they name: neighbors[s, d] is the site one step forward (d = 0, 1, 2, 3 along x, y, z, t) or back (d = 4 + k along the same k) of site s on a periodic 2 x 2 x 2 x 64 lattice; rows j * 8 to (j + 1) * 8 - 1 hold time slice j in an arbitrary order, so the t neighbours lie in the next and previous slice (wrapping) and the others in the same slice. `diag_blocks`: each diagonal block is Hermitian: its left half is symmetric and its right half antisymmetric.
All inputs are finite; a program needn't handle non-finite values.
Results may differ from a plain program's by a relative error of at most 0.00021.
Values sent between devices are 32-bit elements; how exact they have to be, the bound alone decides.
No kernel may reach another device: no remote copies, remote signals or barrier semaphores. Data moves between devices by JAX's collectives and lax.ppermute only.
A program may use at most 64 MiB of HBM per device.

v0:
```python
import jax
import jax.numpy as jnp
from jax import lax
from jax.sharding import PartitionSpec as P

DEGREE = 4


filter_center = 3.7
filter_radius = 3.1
highest = lax.Precision.HIGHEST


def passed_along(x, axis, by):
    size = lax.axis_size(axis)
    return lax.ppermute(x, axis, [(i, (i + by) % size) for i in range(size)])


def embed(weights):
    half_size = weights.shape[-2]
    real_part = weights[..., :half_size]
    imag_part = weights[..., half_size:]
    upper_rows = jnp.concatenate([real_part, -imag_part], -1)
    lower_rows = jnp.concatenate([imag_part, real_part], -1)
    return jnp.concatenate([upper_rows, lower_rows], -2)


def operate(vectors, matrices, pool_index, time_back):
    ahead_block = passed_along(vectors, "site", -1)
    pool = jnp.concatenate([vectors, ahead_block], 0)
    sources = jnp.take(pool, pool_index[:, :8], axis=0)
    summed = jnp.einsum("sjab,sjbc->sac", matrices, sources, precision=highest)
    backward = jnp.einsum("sba,sbc->sac", time_back, vectors, precision=highest)
    backward = passed_along(backward, "site", 1)
    return summed + jnp.take(backward, pool_index[:, 8], axis=0)


def filtered(start_block, operator_apply):
    previous = start_block
    current = (operator_apply(start_block) - filter_center * start_block) / filter_radius
    for order_step in range(DEGREE - 1):
        following = (
            2.0 * (operator_apply(current) - filter_center * current) / filter_radius - previous
        )
        previous, current = (current, following)
    return current


def factor_inverse(gram_matrix):
    lower_factor = jnp.linalg.cholesky(gram_matrix)
    identity = jnp.eye(gram_matrix.shape[0], dtype=jnp.float32)
    return jax.scipy.linalg.solve_triangular(lower_factor, identity, lower=True)


def local(diag_blocks, hop_blocks, neighbors, start_basis):
    site_count = start_basis.shape[0]
    local_cols = start_basis.shape[2]
    all_cols = local_cols * lax.axis_size("vec")
    total_rows = site_count * start_basis.shape[1] * lax.axis_size("site")
    col_start = lax.axis_index("vec") * local_cols
    row_index = neighbors % site_count
    own_index = jnp.arange(site_count, dtype=jnp.int32)
    diag_full = embed(diag_blocks)
    hop_full = embed(hop_blocks)
    back_list = []
    for direction in range(3):
        chosen = jnp.take(hop_full[:, direction], row_index[:, 4 + direction], axis=0)
        back_list.append(jnp.swapaxes(chosen, 1, 2))
    matrices = jnp.stack(
        [diag_full, hop_full[:, 0], hop_full[:, 1], hop_full[:, 2], hop_full[:, 3]] + back_list, 1
    )
    pool_index = jnp.stack(
        [
            own_index,
            row_index[:, 0],
            row_index[:, 1],
            row_index[:, 2],
            row_index[:, 3] + site_count,
            row_index[:, 4],
            row_index[:, 5],
            row_index[:, 6],
            row_index[:, 7],
        ],
        1,
    )
    time_back = hop_full[:, 3]

    def operator_apply(vectors):
        return operate(vectors, matrices, pool_index, time_back)

    basis = start_basis
    filtered_block = filtered(basis, operator_apply)
    everything = lax.all_gather(filtered_block, "vec", axis=2, tiled=True).reshape(-1, all_cols)
    own_block = filtered_block.reshape(-1, local_cols)
    gram_part = jnp.einsum("rc,rk->ck", everything, own_block, precision=highest)
    gram_part = lax.psum(gram_part, "site")
    gram_whole = lax.all_gather(gram_part, "vec", axis=1, tiled=True)
    inverse = factor_inverse(gram_whole / total_rows)
    own_rows = lax.dynamic_slice_in_dim(inverse, col_start, local_cols, 0)
    basis_flat = jnp.einsum("rc,kc->rk", everything, own_rows, precision=highest)
    image_block = operator_apply(basis_flat.reshape(filtered_block.shape)).reshape(-1, local_cols)
    moment = jnp.einsum("rc,rk->ck", everything, image_block, precision=highest)
    moment = lax.psum(moment, "site")
    projected = jnp.dot(inverse, moment, precision=highest) / total_rows
    basis = basis_flat.reshape(filtered_block.shape)
    return (basis, projected)


def solution(mesh):
    placed = (
        P("site", None, None),
        P("site", None, None, None),
        P("site", None),
        P("site", None, "vec"),
    )
    return jax.shard_map(
        local,
        mesh=mesh,
        in_specs=placed,
        out_specs=(P("site", None, "vec"), P(None, "vec")),
        check_vma=False,
    )
```

profile of v0, /device:TPU:1, one launch (start us, length us, event | category | flops | bytes accessed | tf_op | source)
XLA Modules:
  0.0 900.5 jit_solution(3755153946303805086)
XLA Ops:
  7.2 14.5 %collective-permute-start = (f32[8,128,64]{1,2,0:T(8,128)}, f32[8,128,64]{1,2,0:T(8,128)}, u32[]{:S(2)}, u32[]{:S(2)}) collective-permute-start(f32[8,128,64]{1,2,0:T(8,128)} %param.13), channel_id=1, source_target_pairs={{0,504},{8,0},{16,8},{24,16},{32,24},{40,32},{48,40},{56,48},{64,5... | collective-permute-start | bytes 786440 | tf_op jit(solution)/shard_map/ppermute | solution.py:16
  46.1 7.6 broadcast_multiply_fusion.1
  53.8 6.7 collective-permute-start.2
  66.9 6.7 collective-permute-done.3
  75.1 7.6 fusion.61
  85.9 3.3 collective-permute-start.5
  91.9 4.7 collective-permute-done.5
  97.1 7.6 fusion.49
  107.3 3.4 collective-permute-start.7
  113.9 3.9 collective-permute-done.7
  119.3 8.3 fusion.37
  127.7 26.0 %all-gather.3.cloned.1.call-done = f32[8,128,512]{1,2,0:T(8,128)} async-done(((f32[8,128,64]{1,2,0:T(8,128)}), f32[8,128,512]{1,2,0:T(8,128)}) %all-gather.3.cloned.1.call-update) | async-done | bytes 2097168 | tf_op jit(solution)/shard_map/all_gather | solution.py:93
  153.7 4.4 convolution_bitcast_fusion.1
  158.2 250.4 %all-reduce.4.cloned.1.call-done = f32[512,64]{0,1:T(8,128)} async-done(((f32[512,64]{0,1:T(8,128)}), f32[512,64]{0,1:T(8,128)}) %all-reduce.4.cloned.1.call-update) | async-done | bytes 131088 | tf_op jit(solution)/shard_map/psum | solution.py:96
  411.0 36.2 %all-gather.5.cloned.1.call-done = f32[512,512]{0,1:T(8,128)} async-done(((f32[512,64]{0,1:T(8,128)}), f32[512,512]{0,1:T(8,128)}) %all-gather.5.cloned.1.call-update) | async-done | bytes 1048592 | tf_op jit(solution)/shard_map/all_gather | solution.py:97
  454.6 11.7 %cholesky.104 = f32[128,128]{1,0:T(8,128)S(1)} custom-call(f32[128,128]{1,0:T(8,128)S(1)} %cholesky.266), custom_call_target="Cholesky" | custom-call | tf_op jit(solution)/shard_map/jit(cholesky)/cholesky | solution.py:50
  466.5 9.8 %custom-call.31 = f32[1,128,128]{1,2,0:T(8,128)S(1)} custom-call(f32[1,128,128]{2,1,0:T(8,128)S(1)} %get-tuple-element.47), custom_call_target="InvertDiagBlocksLowerTriangular" | custom-call | tf_op jit(solution)/shard_map/jit(cholesky)/cholesky | solution.py:50
  478.9 11.7 %cholesky.217 = f32[128,128]{1,0:T(8,128)S(1)} custom-call(f32[128,128]{1,0:T(8,128)S(1)} %cholesky.270), custom_call_target="Cholesky" | custom-call | tf_op jit(solution)/shard_map/jit(cholesky)/cholesky | solution.py:50
  492.0 9.9 %custom-call.32 = f32[1,128,128]{1,2,0:T(8,128)S(1)} custom-call(f32[1,128,128]{2,1,0:T(8,128)S(1)} %get-tuple-element.44), custom_call_target="InvertDiagBlocksLowerTriangular" | custom-call | tf_op jit(solution)/shard_map/jit(cholesky)/cholesky | solution.py:50
  503.5 11.7 %cholesky.238 = f32[128,128]{1,0:T(8,128)S(1)} custom-call(f32[128,128]{1,0:T(8,128)S(1)} %cholesky.275), custom_call_target="Cholesky" | custom-call | tf_op jit(solution)/shard_map/jit(cholesky)/cholesky | solution.py:50
  515.9 9.8 %custom-call.33 = f32[1,128,128]{1,2,0:T(8,128)S(1)} custom-call(f32[1,128,128]{2,1,0:T(8,128)S(1)} %get-tuple-element.41), custom_call_target="InvertDiagBlocksLowerTriangular" | custom-call | tf_op jit(solution)/shard_map/jit(cholesky)/cholesky | solution.py:50
  527.1 11.9 %cholesky.255 = f32[128,128]{1,0:T(8,128)S(1)} custom-call(f32[128,128]{1,0:T(8,128)S(1)} %convolution_subtract_fusion.5), custom_call_target="Cholesky" | custom-call | tf_op jit(solution)/shard_map/jit(cholesky)/cholesky | solution.py:50
  543.5 14.3 %while.1 = (s32[]{:T(128)}, f32[512,512]{1,0:T(8,128)}, s32[4,2]{0,1:T(2,128)S(1)}, f32[4,128,128]{2,1,0:T(8,128)}, s32[]{:T(128)}) while((s32[]{:T(128)}, f32[512,512]{1,0:T(8,128)}, s32[4,2]{0,1:T(2,128)S(1)}, f32[4,128,128]{2,1,0:T(8,128)}, s32[]{:T(128)}) %tuple.47), condition=%wide.while_cond, body=%wide.while_body.sunk | while | flops 2 | bytes 132705 | solution.py:52
  544.1 2.9 bitcast_dynamic-update-slice_fusion.5
  547.7 2.9 bitcast_dynamic-update-slice_fusion.5
  551.3 2.9 bitcast_dynamic-update-slice_fusion.5
  554.9 2.9 bitcast_dynamic-update-slice_fusion.5
  557.8 40.1 %custom-call.34 = f32[4,128,128]{1,2,0:T(8,128)S(1)} custom-call(f32[4,128,128]{2,1,0:T(8,128)} %get-tuple-element.12), custom_call_target="InvertDiagBlocksLowerTriangular" | custom-call | tf_op jit(solution)/shard_map/jit(_solve_triangular)/triangular_solve | solution.py:52
  607.4 7.7 collective-permute-start.8
  622.6 12.7 %collective-permute-done.9 = f32[8,128,64]{2,1,0:T(8,128)S(1)} collective-permute-done((f32[8,128,64]{2,1,0:T(8,128)}, f32[8,128,64]{2,1,0:T(8,128)S(1)}, u32[]{:S(2)}, u32[]{:S(2)}) %collective-permute-start.9) | collective-permute-done | bytes 262176 | tf_op jit(solution)/shard_map/ppermute | solution.py:16
  636.7 6.8 fusion.13
  646.1 244.8 %all-reduce.6.cloned.1.call-done = f32[512,64]{1,0:T(8,128)} async-done(((f32[512,64]{1,0:T(8,128)}), f32[512,64]{1,0:T(8,128)}) %all-reduce.6.cloned.1.call-update) | async-done | bytes 131088 | tf_op jit(solution)/shard_map/psum | solution.py:103
  (140 shorter events, 91.5 us)
Async XLA Ops:
  7.2 15.8 %copy-start.4 = (f32[8,4,64,128]{3,2,1,0:T(8,128)S(1)}, f32[8,4,64,128]{3,2,1,0:T(8,128)}, u32[]{:S(2)}) copy-start(f32[8,4,64,128]{3,2,1,0:T(8,128)} %param.11) | copy-start | bytes 3145732
  7.2 146.6 %all-gather.3.cloned.1.call-start = ((), (), s32[]{:S(2)}) async-start(), calls=%async_computation | async-start | bytes 2359296 | tf_op jit(solution)/shard_map/all_gather | solution.py:93
  7.2 34.4 %collective-permute-start = (f32[8,128,64]{1,2,0:T(8,128)}, f32[8,128,64]{1,2,0:T(8,128)}, u32[]{:S(2)}, u32[]{:S(2)}) collective-permute-start(f32[8,128,64]{1,2,0:T(8,128)} %param.13), channel_id=1, source_target_pairs={{0,504},{8,0},{16,8},{24,16},{32,24},{40,32},{48,40},{56,48},{64,5... | collective-permute-start | bytes 786440 | tf_op jit(solution)/shard_map/ppermute | solution.py:16
  23.6 1.0 copy-start.5
  24.2 5.1 copy-start
  24.5 4.8 copy-start.10
  26.3 18.3 %collective-permute-start.1 = (f32[8,128,64]{1,2,0:T(8,128)}, f32[8,128,64]{1,2,0:T(8,128)}, u32[]{:S(2)}, u32[]{:S(2)}) collective-permute-start(f32[8,128,64]{1,2,0:T(8,128)} %fusion.94), channel_id=1, source_target_pairs={{0,8},{8,16},{16,24},{24,32},{32,40},{40,48},{48,56},{56,64},{64,7... | collective-permute-start | bytes 786440 | tf_op jit(solution)/shard_map/ppermute | solution.py:16
  38.7 1.9 copy-start.8
  53.8 11.0 %collective-permute-start.2 = (f32[8,128,64]{1,2,0:T(8,128)S(1)}, f32[8,128,64]{1,2,0:T(8,128)S(1)}, u32[]{:S(2)}, u32[]{:S(2)}) collective-permute-start(f32[8,128,64]{1,2,0:T(8,128)S(1)} %get-tuple-element.49), channel_id=1, source_target_pairs={{0,504},{8,0},{16,8},{24,16},{32,24},{40,32},{48,40},{56,48},{64,5... | collective-permute-start | bytes 786440 | tf_op jit(solution)/shard_map/ppermute | solution.py:16
  61.8 11.8 %collective-permute-start.3 = (f32[8,128,64]{1,2,0:T(8,128)}, f32[8,128,64]{1,2,0:T(8,128)}, u32[]{:S(2)}, u32[]{:S(2)}) collective-permute-start(f32[8,128,64]{1,2,0:T(8,128)} %fusion.93), channel_id=1, source_target_pairs={{0,8},{8,16},{16,24},{24,32},{32,40},{40,48},{48,56},{56,64},{64,7... | collective-permute-start | bytes 786440 | tf_op jit(solution)/shard_map/ppermute | solution.py:16
  82.7 7.1 collective-permute-start.4
  85.9 10.6 %collective-permute-start.5 = (f32[8,128,64]{1,2,0:T(8,128)}, f32[8,128,64]{1,2,0:T(8,128)S(1)}, u32[]{:S(2)}, u32[]{:S(2)}) collective-permute-start(f32[8,128,64]{1,2,0:T(8,128)} %fusion.92), channel_id=1, source_target_pairs={{0,8},{8,16},{16,24},{24,32},{32,40},{40,48},{48,56},{56,64},{64,7... | collective-permute-start | bytes 786440 | tf_op jit(solution)/shard_map/ppermute | solution.py:16
  104.8 7.1 collective-permute-start.6
  107.3 10.5 %collective-permute-start.7 = (f32[8,128,64]{1,2,0:T(8,128)S(1)}, f32[8,128,64]{1,2,0:T(8,128)}, u32[]{:S(2)}, u32[]{:S(2)}) collective-permute-start(f32[8,128,64]{1,2,0:T(8,128)S(1)} %fusion.91), channel_id=1, source_target_pairs={{0,8},{8,16},{16,24},{24,32},{32,40},{40,48},{48,56},{56,64},{64,7... | collective-permute-start | bytes 786440 | tf_op jit(solution)/shard_map/ppermute | solution.py:16
  127.7 280.9 %all-reduce.4.cloned.1.call-start = ((), (), s32[]{:S(2)}) async-start(), calls=%async_computation.1 | async-start | bytes 262144 | tf_op jit(solution)/shard_map/psum | solution.py:96
  158.1 289.0 %all-gather.5.cloned.1.call-start = ((), (), s32[]{:S(2)}) async-start(), calls=%async_computation.2 | async-start | bytes 1179648 | tf_op jit(solution)/shard_map/all_gather | solution.py:97
  408.6 482.4 %all-reduce.6.cloned.1.call-start = ((), (), s32[]{:S(2)}) async-start(), calls=%async_computation.3 | async-start | bytes 524288 | tf_op jit(solution)/shard_map/psum | solution.py:103
  447.2 5.0 copy-start.3
  453.6 1.0 copy-start.6
  597.9 4.9 copy-start.9
  602.8 3.2 copy-start.1
  607.4 15.2 %copy-start.7 = (f32[8,128,64]{1,2,0:T(8,128)}, f32[8,128,64]{1,2,0:T(8,128)S(1)}, u32[]{:S(2)}) copy-start(f32[8,128,64]{1,2,0:T(8,128)S(1)} %fusion.106) | copy-start | bytes 786436
  607.4 13.1 %collective-permute-start.8 = (f32[8,128,64]{1,2,0:T(8,128)S(1)}, f32[8,128,64]{1,2,0:T(8,128)S(1)}, u32[]{:S(2)}, u32[]{:S(2)}) collective-permute-start(f32[8,128,64]{1,2,0:T(8,128)S(1)} %fusion.106), channel_id=1, source_target_pairs={{0,504},{8,0},{16,8},{24,16},{32,24},{40,32},{48,40},{56,48},{64,5... | collective-permute-start | bytes 786440 | tf_op jit(solution)/shard_map/ppermute | solution.py:16
  617.0 18.4 %collective-permute-start.9 = (f32[8,128,64]{2,1,0:T(8,128)}, f32[8,128,64]{2,1,0:T(8,128)S(1)}, u32[]{:S(2)}, u32[]{:S(2)}) collective-permute-start(f32[8,128,64]{2,1,0:T(8,128)} %fusion.90), channel_id=1, source_target_pairs={{0,8},{8,16},{16,24},{24,32},{32,40},{40,48},{48,56},{56,64},{64,7... | collective-permute-start | bytes 786440 | tf_op jit(solution)/shard_map/ppermute | solution.py:16
  636.7 6.9 copy-start.2
Sparse Core Ops, SparseCore 0:
  127.8 25.8 all-gather.2
  158.3 250.2 all-reduce.3
  410.7 36.3 all-gather.4
  646.3 244.6 all-reduce.5
where the time goes:
time: 918 us; the launch traced here: 901 us
  waiting for transfers between devices  590 us (64%)
  other arithmetic  133 us (14%)
  matrix products  69.3 us (8%)
  starting transfers between devices  46.2 us (5%)
  local copies, waits for them, and re-layouts  45.1 us (5%)
  between operations  17.2 us (2%)
    psum x1, waiting for transfers between devices, local(): gram_part = lax.psum(gram_part, 'site')  250 us
    psum x1, waiting for transfers between devices, local(): moment = lax.psum(moment, 'site')  245 us
    another operation x15, other arithmetic, factor_inverse(): lower_factor = jnp.linalg.cholesky(gram_matrix)  79.4 us
    ppermute x10, starting transfers between devices, passed_along(): return lax.ppermute(x, axis, [(i, (i + by) % size) for i in range(size)])  45.6 us
    another operation x4, other arithmetic, factor_inverse(): return jax.scipy.linalg.solve_triangular(lower_factor, identity, lower=True)  41.3 us
    dot_general x5, matrix products, operate(): summed = jnp.einsum('sjab,sjbc->sac', matrices, sources, precision=highest)  38.1 us
    all_gather x1, waiting for transfers between devices, local(): gram_whole = lax.all_gather(gram_part, 'vec', axis=1, tiled=True)  36.2 us
    ppermute x10, waiting for transfers between devices, passed_along(): return lax.ppermute(x, axis, [(i, (i + by) % size) for i in range(size)])  32.2 us
  transfers between devices with their start and end apart: 14, of which 12 were waited for; matrix products, arithmetic and copies ran while one was open for 4% of the time, Pallas kernels for 0%

commit v1 on v0

v1 whole, which is shorter than its diff:
```python
import functools

import jax
import jax.numpy as jnp
from jax import lax
from jax.experimental import pallas as pl
from jax.experimental.pallas import tpu as pltpu
from jax.sharding import PartitionSpec as P

DEGREE = 4
CENTER = 3.7
RADIUS = 3.1
NEWTON_LIMIT = 12
NEWTON_DONE = 1e-6
VMEM_LIMIT = 44 * 1024 * 1024

f32 = jnp.float32
bf16 = jnp.bfloat16
VMEM_SPEC = pl.BlockSpec(memory_space=pltpu.VMEM)
SMEM_SPEC = pl.BlockSpec(memory_space=pltpu.SMEM)


def call(kernel, out_shape, n_smem, n_vmem, scratch=(), flops=0, moved=0, name=None):
    return pl.pallas_call(
        kernel,
        out_shape=out_shape,
        in_specs=[SMEM_SPEC] * n_smem + [VMEM_SPEC] * n_vmem,
        out_specs=jax.tree.map(lambda _: VMEM_SPEC, out_shape),
        scratch_shapes=list(scratch),
        compiler_params=pltpu.CompilerParams(vmem_limit_bytes=VMEM_LIMIT),
        cost_estimate=pl.CostEstimate(flops=flops, bytes_accessed=moved, transcendentals=0),
        name=name,
    )


def split(x):
    high = x.astype(bf16)
    return high, (x - high.astype(f32)).astype(bf16)


def left_operand(x):
    high, low = split(x)
    return jnp.concatenate([high, low, high], axis=1)


def adjoint(block):
    turned = block.T
    half = turned.shape[0] // 2
    return jnp.concatenate([turned[:half], -turned[half:]], axis=1)


def low_lanes(shape):
    return lax.broadcasted_iota(jnp.int32, shape, len(shape) - 1) < shape[-1] // 2


def swapped(x):
    return pltpu.roll(x, x.shape[-1] // 2, axis=x.ndim - 1)


def prepare_kernel(near, diag, hop, hop_back, own_ref, time_ref):
    sites, half, wide = diag.shape
    rows = lax.broadcasted_iota(jnp.int32, (half, wide), 0)
    cols = lax.broadcasted_iota(jnp.int32, (half, wide), 1)
    unit = jnp.where(rows == cols, CENTER, 0.0)
    for s in range(sites):
        parts = [diag[s] - unit]
        for d in range(3):
            parts.append(hop[s, d] + adjoint(hop[near[s, 4 + d] % sites, d]))
        own_ref[s] = left_operand(jnp.concatenate(parts, axis=1) * (1.0 / RADIUS))
        parts = [hop[s, 3], adjoint(hop_back[near[s, 7] % sites])]
        time_ref[s] = left_operand(jnp.concatenate(parts, axis=1) * (1.0 / RADIUS))


def spread(x, high_ref, low_ref):
    for n in range(x.shape[0]):
        xp = x[n]
        half = xp.shape[0]
        xs = swapped(xp)
        xq = jnp.where(low_lanes(xp.shape), -xs, xs)
        high_ref[n, :half], low_ref[n, :half] = split(xp)
        high_ref[n, half:], low_ref[n, half:] = split(xq)


def own_kernel(near, x, mats, out, high, low):
    sites = x.shape[0]
    spread(x, high, low)
    for s in range(sites):
        index = [s] + [near[s, d] % sites for d in range(3)]
        h = jnp.concatenate([high[n] for n in index], axis=0)
        l = jnp.concatenate([low[n] for n in index], axis=0)
        out[s] = jnp.dot(
            mats[s], jnp.concatenate([h, h, l], axis=0), preferred_element_type=f32
        )


def time_kernel(mode, near, own, ahead, behind, mats, *rest):
    *more, out, ahigh, alow, bhigh, blow = rest
    sites = own.shape[0]
    spread(ahead, ahigh, alow)
    spread(behind, bhigh, blow)
    for s in range(sites):
        n, m = near[s, 3] % sites, near[s, 7] % sites
        h = jnp.concatenate([ahigh[n], bhigh[m]], axis=0)
        l = jnp.concatenate([alow[n], blow[m]], axis=0)
        applied = own[s] + jnp.dot(
            mats[s], jnp.concatenate([h, h, l], axis=0), preferred_element_type=f32
        )
        if mode == "first":
            out[s] = applied
        elif mode == "next":
            out[s] = 2.0 * applied - more[0][s]
        else:
            out[s] = RADIUS * applied + CENTER * more[0][s]


def product_kernel(everything, own, image, out):
    low = low_lanes(own.shape)
    f, h = own[...], image[...]
    real = jnp.where(low, f, swapped(h))
    imag = jnp.where(low, swapped(f), h)
    left = left_operand(jnp.concatenate([real.T, imag.T], axis=1))
    for p in range(out.shape[0]):
        a, b = everything[2 * p], everything[2 * p + 1]
        both = jnp.concatenate(
            [jnp.where(low, a, swapped(b)), jnp.where(low, swapped(a), b)], axis=0
        )
        high, small = split(both)
        out[p] = jnp.dot(
            left, jnp.concatenate([high, high, small], axis=0), preferred_element_type=f32
        )


def sum_kernel(parts, out):
    total = parts[0]
    for i in range(1, parts.shape[0]):
        total = total + parts[i]
    for i in range(out.shape[0]):
        out[i] = total


NT = (((1,), (1,)), ((), ()))
NN = (((1,), (0,)), ((), ()))


def multiply(a, b, dims):
    ah, al = split(a)
    bh, bl = split(b)
    dot = functools.partial(lax.dot_general, dimension_numbers=dims, preferred_element_type=f32)
    return dot(ah, bh) + (dot(al, bh) + dot(ah, bl))


def inverse_kernel(count, gathered, out, scaled, factor, product):
    n = out.shape[0]
    devices, quarters, rows_each, lanes = gathered.shape
    for v in range(devices):
        for b in range(quarters):
            scaled[v * rows_each : (v + 1) * rows_each, b * lanes : (b + 1) * lanes] = (
                gathered[v, b] * (1.0 / count)
            )
    rows = lax.broadcasted_iota(jnp.int32, (n, n), 0)
    cols = lax.broadcasted_iota(jnp.int32, (n, n), 1)
    on_diag = rows == cols
    weight = jnp.where(rows > cols, 1.0, jnp.where(on_diag, 0.5, 0.0))
    unit = jnp.where(on_diag, 1.0, 0.0)
    matrix = scaled[...]
    only_diag = jnp.where(on_diag, matrix, 0.0)
    scale_row = lax.rsqrt(jnp.sum(only_diag, axis=0, keepdims=True))
    scale_col = lax.rsqrt(jnp.sum(only_diag, axis=1, keepdims=True))
    matrix = matrix * scale_row * scale_col
    scaled[...] = matrix
    factor[...] = unit - weight * (matrix - unit)

    def go_on(state):
        step, size = state
        return jnp.logical_and(step < NEWTON_LIMIT, jnp.logical_not(size < NEWTON_DONE))

    def improve(state):
        step, _ = state
        current = factor[...]
        product[...] = multiply(current, scaled[...], NN)
        error = multiply(product[...], current, NT) - unit
        size = jnp.sum(error * error)
        factor[...] = current - multiply(weight * error, current, NN)
        return step + 1, size

    _, size = lax.while_loop(go_on, improve, (jnp.int32(0), jnp.float32(1.0)))

    @pl.when(jnp.logical_not(size < NEWTON_DONE))
    def _():
        factor[...] = unit

        def eliminate(j, carry):
            pivot_row = scaled[pl.ds(j, 1), :]
            here = lax.broadcasted_iota(jnp.int32, (1, n), 1) == j
            pivot = jnp.sum(jnp.where(here, pivot_row, 0.0))
            a = scaled[...]
            column = jnp.sum(jnp.where(cols == j, a, 0.0), axis=1, keepdims=True) / pivot
            below = lax.broadcasted_iota(jnp.int32, (n, 1), 0) > j
            column = jnp.where(below, column, 0.0)
            r_row = factor[pl.ds(j, 1), :]
            scaled[...] = a - column * pivot_row
            factor[...] = factor[...] - column * r_row
            factor[pl.ds(j, 1), :] = r_row * lax.rsqrt(jnp.full_like(r_row, pivot))
            return carry

        lax.fori_loop(0, n, eliminate, 0)

    out[...] = factor[...] * scale_row


def basis_kernel(place, everything, inverse, out):
    devices, _, wide = everything.shape
    half = wide // 2
    mine = inverse[pl.ds(pl.multiple_of(place[0] * half, half), half), :]
    low = low_lanes((half, wide))
    top, bottom = [], []
    for p in range(devices // 2):
        r = mine[:, p * wide : (p + 1) * wide]
        rs = swapped(r)
        top += [jnp.where(low, r, 0.0), jnp.where(low, rs, 0.0)]
        bottom += [jnp.where(low, 0.0, rs), jnp.where(low, 0.0, r)]
    right = jnp.concatenate(
        [jnp.concatenate(top, axis=1), jnp.concatenate(bottom, axis=1)], axis=0
    )
    left = jnp.concatenate([everything[u] for u in range(devices)], axis=1)
    packed = multiply(left, right, NT)
    sites = out.shape[0]
    for s in range(sites):
        block = packed[s * half : (s + 1) * half]
        out[s, :half] = block[:, :half]
        out[s, half:] = block[:, half:]


def projected_kernel(count, place, moments, inverse, out):
    devices, quarters, rows_each, _ = moments.shape
    mine = inverse[pl.ds(pl.multiple_of(place[0] * rows_each, rows_each), rows_each), :]
    moment = jnp.concatenate(
        [
            jnp.concatenate([moments[v, b] for b in range(quarters)], axis=1)
            for v in range(devices)
        ],
        axis=0,
    )
    half_way = multiply(mine, moment, NN)
    out[...] = multiply(inverse[...], half_way, NT) * (1.0 / count)


def passed_along(x, by):
    size = lax.axis_size("site")
    return lax.ppermute(x, "site", [(i, (i + by) % size) for i in range(size)])


def local(diag_blocks, hop_blocks, neighbors, start_basis):
    sites, both, cols = start_basis.shape
    half = both // 2
    wide = 2 * cols
    devices = lax.axis_size("vec")
    slices = lax.axis_size("site")
    all_cols = cols * devices
    count = sites * both * slices
    place = lax.axis_index("vec").astype(jnp.int32).reshape(1)
    shape = jax.ShapeDtypeStruct
    block = shape((sites, half, wide), f32)

    current = jnp.concatenate([start_basis[:, :half], start_basis[:, half:]], axis=-1)
    hop_back = passed_along(hop_blocks[:, 3], 1)
    own_mats, time_mats = call(
        prepare_kernel,
        (
            shape((sites, half, 3 * 4 * both), bf16),
            shape((sites, half, 3 * 2 * both), bf16),
        ),
        1,
        3,
        flops=1 << 24,
        moved=1 << 22,
        name="prepare",
    )(neighbors, diag_blocks, hop_blocks, hop_back)

    stack = pltpu.VMEM((sites, both, wide), bf16)

    def apply(vectors, mode, *more):
        ahead = passed_along(vectors, -1)
        behind = passed_along(vectors, 1)
        own = call(
            own_kernel,
            block,
            1,
            2,
            scratch=[stack] * 2,
            flops=sites * half * 12 * both * wide * 2,
            moved=1 << 21,
            name="own_slice",
        )(neighbors, vectors, own_mats)
        return call(
            functools.partial(time_kernel, mode),
            block,
            1,
            4 + len(more),
            scratch=[stack] * 4,
            flops=sites * half * 6 * both * wide * 2,
            moved=1 << 21,
            name="next_slices",
        )(neighbors, own, ahead, behind, time_mats, *more)

    previous = current
    current = apply(current, "first")
    for _ in range(DEGREE - 1):
        previous, current = current, apply(current, "next", previous)

    flat = current.reshape(sites * half, wide)
    everything = lax.all_gather(flat, "vec", axis=0)
    image = apply(current, "image", current).reshape(sites * half, wide)
    quarters = all_cols // wide
    products = call(
        product_kernel,
        shape((quarters, wide, wide), f32),
        0,
        3,
        flops=6 * all_cols * wide * sites * both,
        moved=1 << 22,
        name="products",
    )(everything, flat, image)

    chunk = quarters * wide // slices
    parts = lax.all_to_all(
        products.reshape(slices, chunk, wide), "site", 0, 0, tiled=True
    )
    summed = call(
        sum_kernel,
        shape((slices, chunk, wide), f32),
        0,
        1,
        moved=1 << 19,
        name="sum_parts",
    )(parts)
    whole = lax.all_to_all(summed, "site", 0, 0, tiled=True).reshape(quarters, wide, wide)
    gram = lax.all_gather(whole[:, :cols], "vec", axis=0)
    moments = lax.all_gather(whole[:, cols:], "vec", axis=0)

    inverse = call(
        functools.partial(inverse_kernel, float(count)),
        shape((all_cols, all_cols), f32),
        0,
        1,
        scratch=[pltpu.VMEM((all_cols, all_cols), f32)] * 3,
        flops=9 * 6 * all_cols**3,
        moved=1 << 21,
        name="inverse_factor",
    )(gram)
    basis = call(
        basis_kernel,
        shape((sites, both, cols), f32),
        1,
        2,
        flops=12 * all_cols * wide * sites * half,
        moved=1 << 22,
        name="basis",
    )(place, everything, inverse)
    projected = call(
        functools.partial(projected_kernel, float(count)),
        shape((all_cols, cols), f32),
        1,
        2,
        flops=12 * all_cols * all_cols * cols,
        moved=1 << 22,
        name="projected",
    )(place, moments, inverse)
    return basis, projected


def solution(mesh):
    placed = (
        P("site", None, None),
        P("site", None, None, None),
        P("site", None),
        P("site", None, "vec"),
    )
    return jax.shard_map(
        local,
        mesh=mesh,
        in_specs=placed,
        out_specs=(P("site", None, "vec"), P(None, "vec")),
        check_vma=False,
    )
```

time: 918 us -> 462 us (0.50); the launches traced: 901 us -> 461 us
  waiting for transfers between devices: 590 us -> 63.3 us
  Pallas kernels: 0 us -> 267 us
  other arithmetic: 133 us -> 0.14 us
  matrix products: 69.3 us -> 0 us
  blocking collectives: 0 us -> 59.9 us
  local copies, waits for them, and re-layouts: 45.1 us -> 13.5 us
    psum x2 -> x0, waiting for transfers between devices: 495 us -> none  [the longest x1 250 us: local(): gram_part = lax.psum(gram_part, 'site')]
    pallas_call x0 -> x16, Pallas kernels: none -> 267 us  [the longest x1 247 us: local(): call(functools.partial(inverse_kernel, float(count)), shape((all_cols, al...]
    another operation x21 -> x0, other arithmetic: 122 us -> none  [the longest x15 79.4 us: factor_inverse(): lower_factor = jnp.linalg.cholesky(gram_matrix)]
    all_to_all x0 -> x2, blocking collectives: none -> 59.9 us  [the longest x1 35 us: local(): lax.all_to_all(products.reshape(slices, chunk, wide), 'site', 0, 0, tiled...]
    dot_general x14 -> x0, matrix products: 55.9 us -> none  [the longest x5 38.1 us: operate(): summed = jnp.einsum('sjab,sjbc->sac', matrices, sources, precision=highest)]
    gather x16 -> x0, local copies, waits for them, and re-layouts: 25.4 us -> none  [the longest x5 10 us: operate(): sources = jnp.take(pool, pool_index[:, :8], axis=0)]
    all_gather x2 -> x3, waiting for transfers between devices: 62.2 us -> 37.8 us  [the longest x1 25.3 us: local(): gram = lax.all_gather(whole[:, :cols], 'vec', axis=0)]
    another operation x17 -> x0, local copies, waits for them, and re-layouts: 14.4 us -> none
  transfers between devices with their start and end apart: 14 -> 14, of which waited for: 12 -> 12; matrix products, arithmetic and copies ran while one was open for 4% -> 0% of each run, Pallas kernels for 0% -> 56%
where the time goes in v1:
time: 462 us; the launch traced here: 461 us
  Pallas kernels  267 us (58%)
  waiting for transfers between devices  63.3 us (14%)
  blocking collectives  59.9 us (13%)
  starting transfers between devices  42.8 us (9%)
  between operations  14 us (3%)
  local copies, waits for them, and re-layouts  13.5 us (3%)
    pallas_call x1, Pallas kernels, local(): call(functools.partial(inverse_kernel, float(count)), shape((all_cols, al...  247 us
    ppermute x11, starting transfers between devices, passed_along(): return lax.ppermute(x, 'site', [(i, (i + by) % size) for i in range(size)])  42.7 us
    all_to_all x1, blocking collectives, local(): lax.all_to_all(products.reshape(slices, chunk, wide), 'site', 0, 0, tiled...  35 us
    all_gather x1, waiting for transfers between devices, local(): gram = lax.all_gather(whole[:, :cols], 'vec', axis=0)  25.3 us
    all_to_all x1, blocking collectives, local(): lax.all_to_all(summed, 'site', 0, 0, tiled=True)  24.9 us
    ppermute x11, waiting for transfers between devices, passed_along(): return lax.ppermute(x, 'site', [(i, (i + by) % size) for i in range(size)])  24.8 us
    all_gather x1, waiting for transfers between devices, local(): everything = lax.all_gather(flat, 'vec', axis=0)  12.4 us
    unnamed x24, local copies, waits for them, and re-layouts  10.6 us
  transfers between devices with their start and end apart: 14, of which 12 were waited for; matrix products, arithmetic and copies ran while one was open for 0% of the time, Pallas kernels for 56%

profile of v1, /device:TPU:1, one launch (start us, length us, event | category | flops | bytes accessed | tf_op | source)
XLA Modules:
  0.0 461.0 jit_solution(11601039443583752201)
XLA Ops:
  8.3 4.4 collective-permute-start
  14.3 11.9 %collective-permute-start.1 = (f32[8,64,128]{2,1,0:T(8,128)S(1)}, f32[8,64,128]{2,1,0:T(8,128)S(1)}, u32[]{:S(2)}, u32[]{:S(2)}) collective-permute-start(f32[8,64,128]{2,1,0:T(8,128)S(1)} %pad_maximum_fusion.x.rest_0_), channel_id=1, source_target_pairs={{0,504},{8,0},{16,8},{24,16},{32,24},{40,32},{48,40},{56,48},{64,5... | collective-permute-start | bytes 786440 | tf_op jit(solution)/shard_map/ppermute | solution.py:250
  26.2 1.9 collective-permute-start.2
  31.3 1.6 prepare.1
  32.9 1.3 own_slice.5.own
  34.2 4.1 collective-permute-done.2.behind
  39.5 2.1 collective-permute-start.3
  41.6 3.2 collective-permute-start.4
  44.8 1.3 own_slice.6.own
  47.3 5.5 %collective-permute-done.4.behind = f32[8,64,128]{2,1,0:T(8,128)S(1)} collective-permute-done((f32[8,64,128]{2,1,0:T(8,128)S(1)}, f32[8,64,128]{2,1,0:T(8,128)S(1)}, u32[]{:S(2)}, u32[]{:S(2)}) %collective-permute-start.4) | collective-permute-done | bytes 262176 | tf_op jit(solution)/shard_map/ppermute | solution.py:250
  54.0 1.9 collective-permute-start.5
  56.0 3.4 collective-permute-start.6
  59.3 1.3 own_slice.7.own
  61.1 5.2 %collective-permute-done.6.behind = f32[8,64,128]{2,1,0:T(8,128)S(1)} collective-permute-done((f32[8,64,128]{2,1,0:T(8,128)S(1)}, f32[8,64,128]{2,1,0:T(8,128)S(1)}, u32[]{:S(2)}, u32[]{:S(2)}) %collective-permute-start.6) | collective-permute-done | bytes 262176 | tf_op jit(solution)/shard_map/ppermute | solution.py:250
  67.6 1.9 collective-permute-start.7
  69.5 3.4 collective-permute-start.8
  74.7 5.2 %collective-permute-done.8.behind = f32[8,64,128]{2,1,0:T(8,128)S(1)} collective-permute-done((f32[8,64,128]{2,1,0:T(8,128)S(1)}, f32[8,64,128]{2,1,0:T(8,128)S(1)}, u32[]{:S(2)}, u32[]{:S(2)}) %collective-permute-start.8) | collective-permute-done | bytes 262176 | tf_op jit(solution)/shard_map/ppermute | solution.py:250
  79.9 1.9 next_slices.8.x.rest_0_
  81.9 1.9 collective-permute-start.10
  83.8 6.7 %collective-permute-start.9 = (f32[8,64,128]{2,1,0:T(8,128)}, f32[8,64,128]{2,1,0:T(8,128)S(1)}, u32[]{:S(2)}, u32[]{:S(2)}) collective-permute-start(f32[8,64,128]{2,1,0:T(8,128)} %next_slices.8.x.rest_0_), channel_id=1, source_target_pairs={{0,504},{8,0},{16,8},{24,16},{32,24},{40,32},{48,40},{56,48},{64,5... | collective-permute-start | bytes 786440 | tf_op jit(solution)/shard_map/ppermute | solution.py:250
  90.5 1.7 own_slice.9.own
  92.5 1.6 collective-permute-done.9.ahead
  94.1 1.5 next_slices.9
  95.6 12.4 %all-gather.6.cloned.1.call-done.everything = f32[8,512,128]{2,1,0:T(8,128)} async-done(((f32[1,512,128]{2,1,0:T(8,128)}), f32[8,512,128]{2,1,0:T(8,128)}) %all-gather.6.cloned.1.call-update) | async-done | bytes 2097168 | tf_op jit(solution)/shard_map/all_gather | solution.py:312
  108.1 1.6 copy-done
  109.7 2.3 products.1
  112.0 35.0 %all_to_all.10.parts = f32[64,8,128]{2,1,0:T(8,128)S(1)} all-to-all(f32[64,8,128]{2,1,0:T(8,128)S(1)} %bitcast.13), channel_id=1, replica_groups=mesh['site'=64,'vec'=8] {'site'}, dimensions={0} | all-to-all | bytes 524288 | tf_op jit(solution)/shard_map/all_to_all | solution.py:326
  147.1 24.9 %all_to_all.11 = f32[64,8,128]{2,1,0:T(8,128)S(1)} all-to-all(f32[64,8,128]{2,1,0:T(8,128)S(1)} %sum_parts.1), channel_id=1, replica_groups=mesh['site'=64,'vec'=8] {'site'}, dimensions={0} | all-to-all | bytes 524288 | tf_op jit(solution)/shard_map/all_to_all | solution.py:337
  173.5 25.3 %all-gather.8.cloned.1.call-done = f32[32,64,128]{2,1,0:T(8,128)} async-done(((f32[4,64,128]{2,1,0:T(8,128)}), f32[32,64,128]{2,1,0:T(8,128)}) %all-gather.8.cloned.1.call-update) | async-done | bytes 1048592 | tf_op jit(solution)/shard_map/all_gather | solution.py:338
  200.0 247.4 %inverse_factor.1.inverse = f32[512,512]{1,0:T(8,128)S(1)} custom-call(f32[8,4,64,128]{3,2,1,0:T(8,128)S(1)} %bitcast.15), custom_call_target="tpu_custom_call" | custom-call | flops 7247757312 | bytes 2097152 | tf_op jit(solution)/shard_map/inverse_factor/pallas_call | solution.py:341
  447.5 1.4 copy-done.4
  452.6 1.9 copy.14
  (45 shorter events, 19.8 us)
Async XLA Ops:
  7.2 22.3 %copy-start.3 = (f32[8,4,64,128]{3,2,1,0:T(8,128)S(1)}, f32[8,4,64,128]{3,2,1,0:T(8,128)}, u32[]{:S(2)}) copy-start(f32[8,4,64,128]{3,2,1,0:T(8,128)} %hop.1) | copy-start | bytes 3145732
  7.2 22.2 %copy-start.5 = (s32[8,8]{1,0:T(8,128)S(1)}, s32[8,8]{1,0:T(8,128)}, u32[]{:S(2)}) copy-start(s32[8,8]{1,0:T(8,128)} %near.21) | copy-start | bytes 772
  7.2 100.9 %all-gather.6.cloned.1.call-start = ((), (), s32[]{:S(2)}) async-start(), calls=%async_computation.2 | async-start | bytes 2359296 | tf_op jit(solution)/shard_map/all_gather | solution.py:312
  8.3 20.4 %collective-permute-start = (f32[8,64,128]{2,1,0:T(8,128)S(1)}, f32[8,64,128]{2,1,0:T(8,128)S(1)}, u32[]{:S(2)}, u32[]{:S(2)}) collective-permute-start(f32[8,64,128]{2,1,0:T(8,128)S(1)} %slice_bitcast_fusion), channel_id=1, source_target_pairs={{0,8},{8,16},{16,24},{24,32},{32,40},{40,48},{48,56},{56,64},{64,7... | collective-permute-start | bytes 786440 | tf_op jit(solution)/shard_map/ppermute | solution.py:250
  14.3 19.9 %collective-permute-start.1 = (f32[8,64,128]{2,1,0:T(8,128)S(1)}, f32[8,64,128]{2,1,0:T(8,128)S(1)}, u32[]{:S(2)}, u32[]{:S(2)}) collective-permute-start(f32[8,64,128]{2,1,0:T(8,128)S(1)} %pad_maximum_fusion.x.rest_0_), channel_id=1, source_target_pairs={{0,504},{8,0},{16,8},{24,16},{32,24},{40,32},{48,40},{56,48},{64,5... | collective-permute-start | bytes 786440 | tf_op jit(solution)/shard_map/ppermute | solution.py:250
  26.2 12.1 %collective-permute-start.2 = (f32[8,64,128]{2,1,0:T(8,128)S(1)}, f32[8,64,128]{2,1,0:T(8,128)S(1)}, u32[]{:S(2)}, u32[]{:S(2)}) collective-permute-start(f32[8,64,128]{2,1,0:T(8,128)S(1)} %pad_maximum_fusion.x.rest_0_), channel_id=1, source_target_pairs={{0,8},{8,16},{16,24},{24,32},{32,40},{40,48},{48,56},{56,64},{64,7... | collective-permute-start | bytes 786440 | tf_op jit(solution)/shard_map/ppermute | solution.py:250
  28.7 0.7 copy-start.7
  29.4 1.0 copy-start.6
  30.4 0.9 copy-start.8
  39.5 7.8 %collective-permute-start.3 = (f32[8,64,128]{2,1,0:T(8,128)S(1)}, f32[8,64,128]{2,1,0:T(8,128)S(1)}, u32[]{:S(2)}, u32[]{:S(2)}) collective-permute-start(f32[8,64,128]{2,1,0:T(8,128)S(1)} %next_slices.5.x.rest_0_), channel_id=1, source_target_pairs={{0,504},{8,0},{16,8},{24,16},{32,24},{40,32},{48,40},{56,48},{64,5... | collective-permute-start | bytes 786440 | tf_op jit(solution)/shard_map/ppermute | solution.py:250
  41.6 11.3 %collective-permute-start.4 = (f32[8,64,128]{2,1,0:T(8,128)S(1)}, f32[8,64,128]{2,1,0:T(8,128)S(1)}, u32[]{:S(2)}, u32[]{:S(2)}) collective-permute-start(f32[8,64,128]{2,1,0:T(8,128)S(1)} %next_slices.5.x.rest_0_), channel_id=1, source_target_pairs={{0,8},{8,16},{16,24},{24,32},{32,40},{40,48},{48,56},{56,64},{64,7... | collective-permute-start | bytes 786440 | tf_op jit(solution)/shard_map/ppermute | solution.py:250
  54.0 7.1 %collective-permute-start.5 = (f32[8,64,128]{2,1,0:T(8,128)S(1)}, f32[8,64,128]{2,1,0:T(8,128)S(1)}, u32[]{:S(2)}, u32[]{:S(2)}) collective-permute-start(f32[8,64,128]{2,1,0:T(8,128)S(1)} %next_slices.6.x.rest_0_), channel_id=1, source_target_pairs={{0,504},{8,0},{16,8},{24,16},{32,24},{40,32},{48,40},{56,48},{64,5... | collective-permute-start | bytes 786440 | tf_op jit(solution)/shard_map/ppermute | solution.py:250
  56.0 10.4 %collective-permute-start.6 = (f32[8,64,128]{2,1,0:T(8,128)S(1)}, f32[8,64,128]{2,1,0:T(8,128)S(1)}, u32[]{:S(2)}, u32[]{:S(2)}) collective-permute-start(f32[8,64,128]{2,1,0:T(8,128)S(1)} %next_slices.6.x.rest_0_), channel_id=1, source_target_pairs={{0,8},{8,16},{16,24},{24,32},{32,40},{40,48},{48,56},{56,64},{64,7... | collective-permute-start | bytes 786440 | tf_op jit(solution)/shard_map/ppermute | solution.py:250
  67.6 7.1 %collective-permute-start.7 = (f32[8,64,128]{2,1,0:T(8,128)S(1)}, f32[8,64,128]{2,1,0:T(8,128)S(1)}, u32[]{:S(2)}, u32[]{:S(2)}) collective-permute-start(f32[8,64,128]{2,1,0:T(8,128)S(1)} %next_slices.7.x), channel_id=1, source_target_pairs={{0,504},{8,0},{16,8},{24,16},{32,24},{40,32},{48,40},{56,48},{64,5... | collective-permute-start | bytes 786440 | tf_op jit(solution)/shard_map/ppermute | solution.py:250
  69.5 10.4 %collective-permute-start.8 = (f32[8,64,128]{2,1,0:T(8,128)S(1)}, f32[8,64,128]{2,1,0:T(8,128)S(1)}, u32[]{:S(2)}, u32[]{:S(2)}) collective-permute-start(f32[8,64,128]{2,1,0:T(8,128)S(1)} %next_slices.7.x), channel_id=1, source_target_pairs={{0,8},{8,16},{16,24},{24,32},{32,40},{40,48},{48,56},{56,64},{64,7... | collective-permute-start | bytes 786440 | tf_op jit(solution)/shard_map/ppermute | solution.py:250
  81.8 117.0 %all-gather.8.cloned.1.call-start = ((), (), s32[]{:S(2)}) async-start(), calls=%async_computation.3 | async-start | bytes 1179648 | tf_op jit(solution)/shard_map/all_gather | solution.py:338
  81.9 10.6 %collective-permute-start.10 = (f32[8,64,128]{2,1,0:T(8,128)}, f32[8,64,128]{2,1,0:T(8,128)S(1)}, u32[]{:S(2)}, u32[]{:S(2)}) collective-permute-start(f32[8,64,128]{2,1,0:T(8,128)} %next_slices.8.x.rest_0_), channel_id=1, source_target_pairs={{0,8},{8,16},{16,24},{24,32},{32,40},{40,48},{48,56},{56,64},{64,7... | collective-permute-start | bytes 786440 | tf_op jit(solution)/shard_map/ppermute | solution.py:250
  83.8 10.3 %collective-permute-start.9 = (f32[8,64,128]{2,1,0:T(8,128)}, f32[8,64,128]{2,1,0:T(8,128)S(1)}, u32[]{:S(2)}, u32[]{:S(2)}) collective-permute-start(f32[8,64,128]{2,1,0:T(8,128)} %next_slices.8.x.rest_0_), channel_id=1, source_target_pairs={{0,504},{8,0},{16,8},{24,16},{32,24},{40,32},{48,40},{56,48},{64,5... | collective-permute-start | bytes 786440 | tf_op jit(solution)/shard_map/ppermute | solution.py:250
  108.1 1.6 copy-start
  172.8 274.7 %all-gather.10.cloned.1.call-start = ((), (), s32[]{:S(2)}) async-start(), calls=%async_computation.4 | async-start | bytes 1179648 | tf_op jit(solution)/shard_map/all_gather | solution.py:339
  198.8 1.2 copy-start.9
  447.5 3.2 copy-start.1
  447.5 1.4 copy-start.4
  451.8 0.8 copy-start.2
Sparse Core Ops, SparseCore 0:
  82.0 26.0 all-gather.5
  172.9 25.8 all-gather.7
  201.5 30.9 all-gather.9

commit v2 on v1

v2 whole, which is shorter than its diff:
```python
import functools

import jax
import jax.numpy as jnp
from jax import lax
from jax.experimental import pallas as pl
from jax.experimental.pallas import tpu as pltpu
from jax.sharding import PartitionSpec as P

DEGREE = 4
CENTER = 3.7
RADIUS = 3.1
NEWTON_LIMIT = 12
NEWTON_DONE = 1e-6
VMEM_LIMIT = 44 * 1024 * 1024

f32 = jnp.float32
bf16 = jnp.bfloat16
VMEM_SPEC = pl.BlockSpec(memory_space=pltpu.VMEM)
SMEM_SPEC = pl.BlockSpec(memory_space=pltpu.SMEM)


def call(kernel, out_shape, n_smem, n_vmem, scratch=(), flops=0, moved=0, name=None):
    return pl.pallas_call(
        kernel,
        out_shape=out_shape,
        in_specs=[SMEM_SPEC] * n_smem + [VMEM_SPEC] * n_vmem,
        out_specs=jax.tree.map(lambda _: VMEM_SPEC, out_shape),
        scratch_shapes=list(scratch),
        compiler_params=pltpu.CompilerParams(vmem_limit_bytes=VMEM_LIMIT),
        cost_estimate=pl.CostEstimate(flops=flops, bytes_accessed=moved, transcendentals=0),
        name=name,
    )


def split(x):
    high = x.astype(bf16)
    return high, (x - high.astype(f32)).astype(bf16)


NT = (((1,), (1,)), ((), ()))
NN = (((1,), (0,)), ((), ()))


def left_operand(x):
    high, low = split(x)
    return jnp.concatenate([high, low, high], axis=1)


def low_lanes(shape):
    return lax.broadcasted_iota(jnp.int32, shape, len(shape) - 1) < shape[-1] // 2


def swapped(x):
    return pltpu.roll(x, x.shape[-1] // 2, axis=x.ndim - 1)


def transposed(block):
    turned = block.T
    half = turned.shape[0] // 2
    return jnp.concatenate([turned[:half], turned[half:]], axis=1)


def conjugated(block):
    return jnp.where(low_lanes(block.shape), block, -block)


def right_operand(block):
    turned = swapped(block)
    full = jnp.concatenate([block, jnp.where(low_lanes(block.shape), -turned, turned)], axis=0)
    high, low = split(full * (1.0 / RADIUS))
    return jnp.concatenate([high, high, low], axis=0)


def backward_kernel(near, x, hop, out, hop_out):
    for s in range(x.shape[0]):
        block = hop[s, 0]
        hop_out[s] = block
        out[s] = jnp.dot(
            left_operand(x[s]), right_operand(conjugated(block)), preferred_element_type=f32
        )


def prepare_kernel(near, diag, hop, own_ref, ahead_ref):
    sites, half, wide = diag.shape
    rows = lax.broadcasted_iota(jnp.int32, (half, wide), 0)
    cols = lax.broadcasted_iota(jnp.int32, (half, wide), 1)
    unit = jnp.where(rows == cols, CENTER, 0.0)
    for s in range(sites):
        parts = [right_operand(transposed(diag[s]) - unit)]
        for d in range(3):
            other = hop[lax.rem(near[s, 4 + d], sites), d]
            parts.append(right_operand(transposed(hop[s, d]) + conjugated(other)))
        own_ref[s] = jnp.concatenate(parts, axis=0)
        ahead_ref[s] = right_operand(transposed(hop[s, 3]))


def prepare_back_kernel(near, hop_back, back_ref):
    sites = hop_back.shape[0]
    for s in range(sites):
        back_ref[s] = right_operand(conjugated(hop_back[lax.rem(near[s, 7], sites)]))


def own_kernel(near, x, mats, out, spread):
    sites = x.shape[0]
    for n in range(sites):
        spread[n] = left_operand(x[n])
    for s in range(sites):
        index = [s] + [lax.rem(near[s, d], sites) for d in range(3)]
        left = jnp.concatenate([spread[n] for n in index], axis=1)
        out[s] = jnp.dot(left, mats[s], preferred_element_type=f32)


def first_kernel(near, own, ahead, received, ahead_mats, out):
    sites = own.shape[0]
    for s in range(sites):
        left = left_operand(ahead[lax.rem(near[s, 3], sites)])
        part = jnp.dot(left, ahead_mats[s], preferred_element_type=f32)
        out[s] = own[s] + part + received[lax.rem(near[s, 7], sites)]


def next_kernel(mode, near, own, ahead, behind, ahead_mats, back_mats, more, out):
    sites = own.shape[0]
    for s in range(sites):
        left = left_operand(ahead[lax.rem(near[s, 3], sites)])
        right = left_operand(behind[lax.rem(near[s, 7], sites)])
        applied = own[s] + jnp.dot(
            jnp.concatenate([left, right], axis=1),
            jnp.concatenate([ahead_mats[s], back_mats[s]], axis=0),
            preferred_element_type=f32,
        )
        if mode == "next":
            out[s] = 2.0 * applied - more[s]
        else:
            out[s] = RADIUS * applied + CENTER * more[s]


def product_kernel(place, everything, own, image, out):
    devices = everything.shape[0]
    sites, cols, wide = own.shape
    f = jnp.concatenate([own[s] for s in range(sites)], axis=1)
    h = jnp.concatenate([image[s] for s in range(sites)], axis=1)
    left = left_operand(jnp.concatenate([f, h], axis=0))
    third = sites * wide
    shift = place[0]
    tiles = devices // 2
    for p in range(tiles):
        both = []
        for j in (2 * p, 2 * p + 1):
            u = lax.rem(shift + j, devices)
            both.append(
                jnp.concatenate(
                    [everything[u, s * cols : (s + 1) * cols] for s in range(sites)], axis=1
                )
            )
        high, low = split(jnp.concatenate(both, axis=0))
        dot = functools.partial(lax.dot_general, dimension_numbers=NT, preferred_element_type=f32)
        tile = dot(left[:, : 2 * third], jnp.concatenate([high, high], axis=1)) + dot(
            left[:, :third], low
        )
        if p < 2:
            out[p * cols : (p + 1) * cols] = tile[:cols]
        elif p == 2:
            out[2 * cols : 2 * cols + cols // 2] = jnp.concatenate(
                [tile[: cols // 2, :cols], tile[cols // 2 : cols, :cols]], axis=1
            )
        start = 5 * cols // 2 + p * cols
        out[start : start + cols] = tile[cols:]
    start = 5 * cols // 2 + tiles * cols
    out[start:] = jnp.zeros((out.shape[0] - start, wide), f32)


def sum_kernel(parts, out):
    total = parts[0]
    for i in range(1, parts.shape[0]):
        total = total + parts[i]
    for i in range(out.shape[0]):
        out[i] = total


def multiply(a, b, dims):
    ah, al = split(a)
    bh, bl = split(b)
    dot = functools.partial(lax.dot_general, dimension_numbers=dims, preferred_element_type=f32)
    return dot(ah, bh) + (dot(al, bh) + dot(ah, bl))


def inverse_kernel(count, gathered, out, scaled, factor, product):
    n = out.shape[0]
    devices, _, wide = gathered.shape
    half = wide // 2
    blocks = {}
    for v in range(devices):
        for j in range(5):
            if j < 4:
                rows = gathered[v, (j // 2) * half : (j // 2 + 1) * half]
                block = rows[:, (j % 2) * half : (j % 2 + 1) * half]
            else:
                rows = gathered[v, wide:]
                block = jnp.concatenate([rows[:, :half], rows[:, half:]], axis=0)
            blocks[v, (v + j) % devices] = block
            if 0 < j < 4:
                blocks[(v + j) % devices, v] = block.T
    for v in range(devices):
        line = jnp.concatenate([blocks[v, u] for u in range(devices)], axis=1)
        scaled[v * half : (v + 1) * half, :] = line * (1.0 / count)
    rows = lax.broadcasted_iota(jnp.int32, (n, n), 0)
    cols = lax.broadcasted_iota(jnp.int32, (n, n), 1)
    on_diag = rows == cols
    weight = jnp.where(rows > cols, 1.0, jnp.where(on_diag, 0.5, 0.0))
    unit = jnp.where(on_diag, 1.0, 0.0)
    matrix = scaled[...]
    only_diag = jnp.where(on_diag, matrix, 0.0)
    scale_row = lax.rsqrt(jnp.sum(only_diag, axis=0, keepdims=True))
    scale_col = lax.rsqrt(jnp.sum(only_diag, axis=1, keepdims=True))
    matrix = matrix * scale_row * scale_col
    scaled[...] = matrix
    factor[...] = unit - weight * (matrix - unit)

    def go_on(state):
        step, size = state
        return jnp.logical_and(step < NEWTON_LIMIT, jnp.logical_not(size < NEWTON_DONE))

    def improve(state):
        step, _ = state
        current = factor[...]
        product[...] = multiply(current, scaled[...], NN)
        error = multiply(product[...], current, NT) - unit
        size = jnp.sum(error * error)
        factor[...] = current - multiply(weight * error, current, NN)
        return step + 1, size

    _, size = lax.while_loop(go_on, improve, (jnp.int32(0), jnp.float32(1.0)))

    @pl.when(jnp.logical_not(size < NEWTON_DONE))
    def _():
        factor[...] = unit

        def eliminate(j, carry):
            pivot_row = scaled[pl.ds(j, 1), :]
            here = lax.broadcasted_iota(jnp.int32, (1, n), 1) == j
            pivot = jnp.sum(jnp.where(here, pivot_row, 0.0))
            a = scaled[...]
            column = jnp.sum(jnp.where(cols == j, a, 0.0), axis=1, keepdims=True) / pivot
            below = lax.broadcasted_iota(jnp.int32, (n, 1), 0) > j
            column = jnp.where(below, column, 0.0)
            r_row = factor[pl.ds(j, 1), :]
            scaled[...] = a - column * pivot_row
            factor[...] = factor[...] - column * r_row
            factor[pl.ds(j, 1), :] = r_row * lax.rsqrt(jnp.full_like(r_row, pivot))
            return carry

        lax.fori_loop(0, n, eliminate, 0)

    out[...] = factor[...] * scale_row


def basis_kernel(place, everything, inverse, out):
    devices = everything.shape[0]
    sites, cols, wide = out.shape
    mine = inverse[pl.ds(pl.multiple_of(place[0] * cols, cols), cols), :]
    right = jnp.concatenate(
        [
            jnp.concatenate(
                [everything[u, s * cols : (s + 1) * cols] for s in range(sites)], axis=1
            )
            for u in range(devices)
        ],
        axis=0,
    )
    result = multiply(mine, right, NN)
    for s in range(sites):
        out[s] = result[:, s * wide : (s + 1) * wide]


def projected_kernel(count, place, moments, inverse, out):
    devices, _, wide = moments.shape
    half = wide // 2
    tiles = devices // 2
    low = low_lanes((half, wide))
    lines = []
    for v in range(devices):
        turned = [moments[v, p * half : (p + 1) * half] for p in range(tiles)]
        line = []
        for q in range(tiles):
            j = (2 * q - v) % devices
            if v % 2 == 0:
                line.append(turned[j // 2])
            else:
                line.append(swapped(jnp.where(low, turned[(j // 2 + 1) % tiles], turned[j // 2])))
        lines.append(jnp.concatenate(line, axis=1))
    moment = jnp.concatenate(lines, axis=0)
    mine = inverse[pl.ds(pl.multiple_of(place[0] * half, half), half), :]
    half_way = multiply(mine, moment, NN)
    out[...] = multiply(half_way, inverse[...], NT) * (1.0 / count)


def passed_along(x, by):
    size = lax.axis_size("site")
    return lax.ppermute(x, "site", [(i, (i + by) % size) for i in range(size)])


def local(diag_blocks, hop_blocks, neighbors, start_basis):
    sites, both, cols = start_basis.shape
    half = both // 2
    devices = lax.axis_size("vec")
    slices = lax.axis_size("site")
    all_cols = cols * devices
    count = float(sites * both * slices)
    place = lax.axis_index("vec").astype(jnp.int32).reshape(1)
    shape = jax.ShapeDtypeStruct
    block = shape((sites, cols, both), f32)
    size = sites * cols * both * 4

    def matrices(blocks):
        return shape((sites, 3 * blocks * both, both), bf16)

    def work(blocks):
        return sites * cols * blocks * 3 * both * both * 2

    current = jnp.swapaxes(start_basis, 1, 2)
    ahead = passed_along(current, -1)
    back, links = pl.pallas_call(
        backward_kernel,
        out_shape=(block, shape((sites, half, both), f32)),
        grid=(1,),
        in_specs=[
            SMEM_SPEC,
            pl.BlockSpec((sites, cols, both), lambda i: (0, 0, 0)),
            pl.BlockSpec((sites, 1, half, both), lambda i: (0, 3, 0, 0)),
        ],
        out_specs=(
            pl.BlockSpec((sites, cols, both), lambda i: (0, 0, 0)),
            pl.BlockSpec((sites, half, both), lambda i: (0, 0, 0)),
        ),
        compiler_params=pltpu.CompilerParams(vmem_limit_bytes=VMEM_LIMIT),
        cost_estimate=pl.CostEstimate(
            flops=work(1), bytes_accessed=4 * size, transcendentals=0
        ),
        name="backward",
    )(neighbors, current, hop_blocks)
    received = passed_along(back, 1)
    links_back = passed_along(links, 1)
    own_mats, ahead_mats = call(
        prepare_kernel,
        (matrices(4), matrices(1)),
        1,
        2,
        flops=1 << 24,
        moved=1 << 23,
        name="prepare",
    )(neighbors, diag_blocks, hop_blocks)
    back_mats = call(
        prepare_back_kernel, matrices(1), 1, 1, flops=1 << 22, moved=1 << 21, name="prepare_back"
    )(neighbors, links_back)

    def own_part(vectors):
        return call(
            own_kernel,
            block,
            1,
            2,
            scratch=[pltpu.VMEM((sites, cols, 3 * both), bf16)],
            flops=work(4),
            moved=8 * size,
            name="own_slice",
        )(neighbors, vectors, own_mats)

    def apply(vectors, mode, more):
        ahead = passed_along(vectors, -1)
        behind = passed_along(vectors, 1)
        return call(
            functools.partial(next_kernel, mode),
            block,
            1,
            6,
            flops=work(2),
            moved=8 * size,
            name="next_slices",
        )(neighbors, own_part(vectors), ahead, behind, ahead_mats, back_mats, more)

    previous = current
    current = call(first_kernel, block, 1, 4, flops=work(1), moved=6 * size, name="first_step")(
        neighbors, own_part(current), ahead, received, ahead_mats
    )
    for _ in range(DEGREE - 1):
        previous, current = current, apply(current, "next", previous)

    everything = lax.all_gather(current.reshape(sites * cols, both), "vec", axis=0)
    image = apply(current, "image", current)
    kept = 5 * cols // 2
    products = call(
        product_kernel,
        shape((slices * 8, both), f32),
        1,
        3,
        flops=6 * all_cols * 2 * cols * sites * both,
        moved=1 << 22,
        name="products",
    )(place, everything, current, image)

    parts = lax.all_to_all(products.reshape(slices, 8, both), "site", 0, 0, tiled=True)
    summed = call(
        sum_kernel, shape((slices, 8, both), f32), 0, 1, moved=1 << 19, name="sum_parts"
    )(parts)
    whole = lax.all_to_all(summed, "site", 0, 0, tiled=True).reshape(slices * 8, both)
    moments = lax.all_gather(whole[kept : kept + all_cols // 2], "vec", axis=0)
    gram = lax.all_gather(whole[:kept], "vec", axis=0)

    inverse = call(
        functools.partial(inverse_kernel, count),
        shape((all_cols, all_cols), f32),
        0,
        1,
        scratch=[pltpu.VMEM((all_cols, all_cols), f32)] * 3,
        flops=9 * 6 * all_cols**3,
        moved=1 << 21,
        name="inverse_factor",
    )(gram)
    basis = call(
        basis_kernel,
        block,
        1,
        2,
        flops=6 * all_cols * cols * sites * both,
        moved=1 << 22,
        name="basis",
    )(place, everything, inverse)
    projected = call(
        functools.partial(projected_kernel, count),
        shape((cols, all_cols), f32),
        1,
        2,
        flops=12 * all_cols * all_cols * cols,
        moved=1 << 22,
        name="projected",
    )(place, moments, inverse)
    return jnp.swapaxes(basis, 1, 2), projected.T


def solution(mesh):
    placed = (
        P("site", None, None),
        P("site", None, None, None),
        P("site", None),
        P("site", None, "vec"),
    )
    return jax.shard_map(
        local,
        mesh=mesh,
        in_specs=placed,
        out_specs=(P("site", None, "vec"), P(None, "vec")),
        check_vma=False,
    )
```

time: 462 us -> 451 us (0.976)
  waiting for transfers between devices: 63.3 us -> 33.1 us
  blocking collectives: 59.9 us -> 77.6 us
  local copies, waits for them, and re-layouts: 13.5 us -> 7.59 us
  Pallas kernels: 267 us -> 272 us
    all_gather x3 -> x2, waiting for transfers between devices: 37.8 us -> 12.3 us  [the longest x1 12.3 us: local(): lax.all_gather(current.reshape(sites * cols, both), 'vec', axis=0)]
    all_gather x0 -> x1, blocking collectives: none -> 17.7 us  [local(): gram = lax.all_gather(whole[:kept], 'vec', axis=0)]
    pallas_call x16 -> x18, Pallas kernels: 267 us -> 272 us  [the longest x1 248 us: local(): call(functools.partial(inverse_kernel, count), shape((all_cols, all_cols)...]
  transfers between devices with their start and end apart: 14 -> 13, of which waited for: 12 -> 9; matrix products, arithmetic and copies ran while one was open for 0% -> 0% of each run, Pallas kernels for 56% -> 58%
where the time goes in v2:
time: 451 us; the launch traced here: 450 us
  Pallas kernels  272 us (60%)
  blocking collectives  77.6 us (17%)
  starting transfers between devices  46.1 us (10%)
  waiting for transfers between devices  33.1 us (7%)
  between operations  14.3 us (3%)
  local copies, waits for them, and re-layouts  7.59 us (2%)
    pallas_call x1, Pallas kernels, local(): call(functools.partial(inverse_kernel, count), shape((all_cols, all_cols)...  248 us
    ppermute x11, starting transfers between devices, passed_along(): return lax.ppermute(x, 'site', [(i, (i + by) % size) for i in range(size)])  46 us
    all_to_all x1, blocking collectives, local(): lax.all_to_all(products.reshape(slices, 8, both), 'site', 0, 0, tiled=True)  35 us
    all_to_all x1, blocking collectives, local(): lax.all_to_all(summed, 'site', 0, 0, tiled=True).reshape(slices * 8, both)  24.9 us
    ppermute x11, waiting for transfers between devices, passed_along(): return lax.ppermute(x, 'site', [(i, (i + by) % size) for i in range(size)])  20.8 us
    all_gather x1, blocking collectives, local(): gram = lax.all_gather(whole[:kept], 'vec', axis=0)  17.7 us
    all_gather x1, waiting for transfers between devices, local(): lax.all_gather(current.reshape(sites * cols, both), 'vec', axis=0)  12.3 us
  transfers between devices with their start and end apart: 13, of which 9 were waited for; matrix products, arithmetic and copies ran while one was open for 0% of the time, Pallas kernels for 58%

profile of v2, /device:TPU:1, one launch (start us, length us, event | category | flops | bytes accessed | tf_op | source)
XLA Modules:
  0.0 450.5 jit_solution(9211620988318453748)
XLA Ops:
  9.1 1.3 backward.1
  10.5 4.4 collective-permute-start.1
  14.8 11.9 %collective-permute-start = (f32[8,64,128]{2,1,0:T(8,128)}, f32[8,64,128]{2,1,0:T(8,128)S(1)}, u32[]{:S(2)}, u32[]{:S(2)}) collective-permute-start(f32[8,64,128]{2,1,0:T(8,128)} %bitcast.1.x.more), channel_id=1, source_target_pairs={{0,504},{8,0},{16,8},{24,16},{32,24},{40,32},{48,40},{56,48},{64,5... | collective-permute-start | bytes 786440 | tf_op jit(solution)/shard_map/ppermute | solution.py:300
  26.8 1.9 collective-permute-start.4
  30.9 3.1 prepare.1
  34.0 1.9 own_slice.5.own
  36.8 6.7 %collective-permute-start.2 = (f32[8,64,128]{2,1,0:T(8,128)S(1)}, f32[8,64,128]{2,1,0:T(8,128)S(1)}, u32[]{:S(2)}, u32[]{:S(2)}) collective-permute-start(f32[8,64,128]{2,1,0:T(8,128)S(1)} %first_step.1.x.more), channel_id=1, source_target_pairs={{0,504},{8,0},{16,8},{24,16},{32,24},{40,32},{48,40},{56,48},{64,5... | collective-permute-start | bytes 786440 | tf_op jit(solution)/shard_map/ppermute | solution.py:300
  43.5 1.9 collective-permute-start.3
  46.2 1.3 own_slice.6.own
  47.8 7.2 %collective-permute-done.3.behind = f32[8,64,128]{2,1,0:T(8,128)S(1)} collective-permute-done((f32[8,64,128]{2,1,0:T(8,128)S(1)}, f32[8,64,128]{2,1,0:T(8,128)S(1)}, u32[]{:S(2)}, u32[]{:S(2)}) %collective-permute-start.3) | collective-permute-done | bytes 262176 | tf_op jit(solution)/shard_map/ppermute | solution.py:300
  55.0 1.3 next_slices.4.x.more
  56.3 1.9 collective-permute-start.5
  58.3 3.4 collective-permute-start.6
  63.4 5.2 %collective-permute-done.6.behind = f32[8,64,128]{2,1,0:T(8,128)S(1)} collective-permute-done((f32[8,64,128]{2,1,0:T(8,128)S(1)}, f32[8,64,128]{2,1,0:T(8,128)S(1)}, u32[]{:S(2)}, u32[]{:S(2)}) %collective-permute-start.6) | collective-permute-done | bytes 262176 | tf_op jit(solution)/shard_map/ppermute | solution.py:300
  69.7 1.9 collective-permute-start.7
  71.6 3.4 collective-permute-start.8
  76.8 5.2 %collective-permute-done.8.behind = f32[8,64,128]{2,1,0:T(8,128)S(1)} collective-permute-done((f32[8,64,128]{2,1,0:T(8,128)S(1)}, f32[8,64,128]{2,1,0:T(8,128)S(1)}, u32[]{:S(2)}, u32[]{:S(2)}) %collective-permute-start.8) | collective-permute-done | bytes 262176 | tf_op jit(solution)/shard_map/ppermute | solution.py:300
  82.1 1.7 next_slices.6.x.more.own
  83.8 1.9 collective-permute-start.10
  85.7 6.7 %collective-permute-start.9 = (f32[8,64,128]{2,1,0:T(8,128)}, f32[8,64,128]{2,1,0:T(8,128)}, u32[]{:S(2)}, u32[]{:S(2)}) collective-permute-start(f32[8,64,128]{2,1,0:T(8,128)} %next_slices.6.x.more.own), channel_id=1, source_target_pairs={{0,504},{8,0},{16,8},{24,16},{32,24},{40,32},{48,40},{56,48},{64,5... | collective-permute-start | bytes 786440 | tf_op jit(solution)/shard_map/ppermute | solution.py:300
  92.5 1.8 own_slice.9.own
  94.5 1.6 collective-permute-done.9.ahead
  96.1 1.4 next_slices.7.image
  97.5 12.3 %all-gather.3.cloned.1.call-done.everything = f32[8,512,128]{2,1,0:T(8,128)} async-done(((f32[1,512,128]{2,1,0:T(8,128)}), f32[8,512,128]{2,1,0:T(8,128)}) %all-gather.3.cloned.1.call-update) | async-done | bytes 2097168 | tf_op jit(solution)/shard_map/all_gather | solution.py:389
  109.8 1.6 copy-done.4
  111.4 2.0 products.1
  113.4 35.0 %all_to_all.10.parts = f32[64,8,128]{2,1,0:T(8,128)S(1)} all-to-all(f32[64,8,128]{2,1,0:T(8,128)S(1)} %bitcast.10), channel_id=1, replica_groups=mesh['site'=64,'vec'=8] {'site'}, dimensions={0} | all-to-all | bytes 524288 | tf_op jit(solution)/shard_map/all_to_all | solution.py:402
  148.5 24.9 %all_to_all.11 = f32[64,8,128]{2,1,0:T(8,128)S(1)} all-to-all(f32[64,8,128]{2,1,0:T(8,128)S(1)} %sum_parts.1), channel_id=1, replica_groups=mesh['site'=64,'vec'=8] {'site'}, dimensions={0} | all-to-all | bytes 524288 | tf_op jit(solution)/shard_map/all_to_all | solution.py:406
  174.1 17.7 %all_gather.17.gathered = f32[8,160,128]{2,1,0:T(8,128)S(1)} all-gather(f32[1,160,128]{2,1,0:T(8,128)S(1)} %slice_bitcast_fusion.1), channel_id=1, replica_groups=mesh['site'=64,'vec'=8] {'vec'}, dimensions={0}, use_global_device_ids=true | all-gather | bytes 737280 | tf_op jit(solution)/shard_map/all_gather | solution.py:408
  191.8 247.5 %inverse_factor.1.inverse = f32[512,512]{1,0:T(8,128)S(1)} custom-call(f32[8,160,128]{2,1,0:T(8,128)S(1)} %all_gather.17.gathered), custom_call_target="tpu_custom_call" | custom-call | flops 7247757312 | bytes 2097152 | tf_op jit(solution)/shard_map/inverse_factor/pallas_call | solution.py:410
  439.4 1.5 basis.1
  442.1 1.6 projected.1
  (43 shorter events, 12.9 us)
Async XLA Ops:
  7.2 102.7 %all-gather.3.cloned.1.call-start = ((), (), s32[]{:S(2)}) async-start(), calls=%async_computation.2 | async-start | bytes 2359296 | tf_op jit(solution)/shard_map/all_gather | solution.py:389
  7.2 1.2 copy-start.6
  8.4 0.7 copy-start.9
  10.5 25.4 %collective-permute-start.1 = (f32[8,64,128]{2,1,0:T(8,128)S(1)}, f32[8,64,128]{2,1,0:T(8,128)S(1)}, u32[]{:S(2)}, u32[]{:S(2)}) collective-permute-start(f32[8,64,128]{2,1,0:T(8,128)S(1)} %get-tuple-element.7), channel_id=1, source_target_pairs={{0,8},{8,16},{16,24},{24,32},{32,40},{40,48},{48,56},{56,64},{64,7... | collective-permute-start | bytes 786440 | tf_op jit(solution)/shard_map/ppermute | solution.py:300
  14.8 21.1 %collective-permute-start = (f32[8,64,128]{2,1,0:T(8,128)}, f32[8,64,128]{2,1,0:T(8,128)S(1)}, u32[]{:S(2)}, u32[]{:S(2)}) collective-permute-start(f32[8,64,128]{2,1,0:T(8,128)} %bitcast.1.x.more), channel_id=1, source_target_pairs={{0,504},{8,0},{16,8},{24,16},{32,24},{40,32},{48,40},{56,48},{64,5... | collective-permute-start | bytes 786440 | tf_op jit(solution)/shard_map/ppermute | solution.py:300
  26.8 18.6 %collective-permute-start.4 = (f32[8,64,128]{2,1,0:T(8,128)S(1)}, f32[8,64,128]{2,1,0:T(8,128)S(1)}, u32[]{:S(2)}, u32[]{:S(2)}) collective-permute-start(f32[8,64,128]{2,1,0:T(8,128)S(1)} %get-tuple-element.9), channel_id=1, source_target_pairs={{0,8},{8,16},{16,24},{24,32},{32,40},{40,48},{48,56},{56,64},{64,7... | collective-permute-start | bytes 786440 | tf_op jit(solution)/shard_map/ppermute | solution.py:300
  28.7 1.2 copy-start.7
  29.9 0.9 copy-start.11
  34.0 48.0 %copy-start = (bf16[8,384,128]{2,1,0:T(8,128)(2,1)}, bf16[8,384,128]{2,1,0:T(8,128)(2,1)S(1)}, u32[]{:S(2)}) copy-start(bf16[8,384,128]{2,1,0:T(8,128)(2,1)S(1)} %get-tuple-element.8.ahead_mats) | copy-start | bytes 2359300
  36.8 11.0 %collective-permute-start.2 = (f32[8,64,128]{2,1,0:T(8,128)S(1)}, f32[8,64,128]{2,1,0:T(8,128)S(1)}, u32[]{:S(2)}, u32[]{:S(2)}) collective-permute-start(f32[8,64,128]{2,1,0:T(8,128)S(1)} %first_step.1.x.more), channel_id=1, source_target_pairs={{0,504},{8,0},{16,8},{24,16},{32,24},{40,32},{48,40},{56,48},{64,5... | collective-permute-start | bytes 786440 | tf_op jit(solution)/shard_map/ppermute | solution.py:300
  43.5 11.5 %collective-permute-start.3 = (f32[8,64,128]{2,1,0:T(8,128)S(1)}, f32[8,64,128]{2,1,0:T(8,128)S(1)}, u32[]{:S(2)}, u32[]{:S(2)}) collective-permute-start(f32[8,64,128]{2,1,0:T(8,128)S(1)} %first_step.1.x.more), channel_id=1, source_target_pairs={{0,8},{8,16},{16,24},{24,32},{32,40},{40,48},{48,56},{56,64},{64,7... | collective-permute-start | bytes 786440 | tf_op jit(solution)/shard_map/ppermute | solution.py:300
  46.2 35.9 %copy-start.2 = (bf16[8,384,128]{2,1,0:T(8,128)(2,1)}, bf16[8,384,128]{2,1,0:T(8,128)(2,1)S(1)}, u32[]{:S(2)}) copy-start(bf16[8,384,128]{2,1,0:T(8,128)(2,1)S(1)} %prepare_back.1.back_mats) | copy-start | bytes 2359300
  56.3 7.1 %collective-permute-start.5 = (f32[8,64,128]{2,1,0:T(8,128)S(1)}, f32[8,64,128]{2,1,0:T(8,128)S(1)}, u32[]{:S(2)}, u32[]{:S(2)}) collective-permute-start(f32[8,64,128]{2,1,0:T(8,128)S(1)} %next_slices.4.x.more), channel_id=1, source_target_pairs={{0,504},{8,0},{16,8},{24,16},{32,24},{40,32},{48,40},{56,48},{64,5... | collective-permute-start | bytes 786440 | tf_op jit(solution)/shard_map/ppermute | solution.py:300
  58.3 10.4 %collective-permute-start.6 = (f32[8,64,128]{2,1,0:T(8,128)S(1)}, f32[8,64,128]{2,1,0:T(8,128)S(1)}, u32[]{:S(2)}, u32[]{:S(2)}) collective-permute-start(f32[8,64,128]{2,1,0:T(8,128)S(1)} %next_slices.4.x.more), channel_id=1, source_target_pairs={{0,8},{8,16},{16,24},{24,32},{32,40},{40,48},{48,56},{56,64},{64,7... | collective-permute-start | bytes 786440 | tf_op jit(solution)/shard_map/ppermute | solution.py:300
  69.7 22.8 %copy-start.10 = (s32[8,8]{1,0:T(8,128)S(1)}, s32[8,8]{1,0:T(8,128)}, u32[]{:S(2)}) copy-start(s32[8,8]{1,0:T(8,128)} %near.25) | copy-start | bytes 772
  69.7 7.1 %collective-permute-start.7 = (f32[8,64,128]{2,1,0:T(8,128)S(1)}, f32[8,64,128]{2,1,0:T(8,128)S(1)}, u32[]{:S(2)}, u32[]{:S(2)}) collective-permute-start(f32[8,64,128]{2,1,0:T(8,128)S(1)} %next_slices.5.x), channel_id=1, source_target_pairs={{0,504},{8,0},{16,8},{24,16},{32,24},{40,32},{48,40},{56,48},{64,5... | collective-permute-start | bytes 786440 | tf_op jit(solution)/shard_map/ppermute | solution.py:300
  71.6 10.4 %collective-permute-start.8 = (f32[8,64,128]{2,1,0:T(8,128)S(1)}, f32[8,64,128]{2,1,0:T(8,128)S(1)}, u32[]{:S(2)}, u32[]{:S(2)}) collective-permute-start(f32[8,64,128]{2,1,0:T(8,128)S(1)} %next_slices.5.x), channel_id=1, source_target_pairs={{0,8},{8,16},{16,24},{24,32},{32,40},{40,48},{48,56},{56,64},{64,7... | collective-permute-start | bytes 786440 | tf_op jit(solution)/shard_map/ppermute | solution.py:300
  83.8 357.1 %all-gather.5.cloned.1.call-start = ((), (), s32[]{:S(2)}) async-start(), calls=%async_computation.3 | async-start | bytes 1179648 | tf_op jit(solution)/shard_map/all_gather | solution.py:407
  83.8 10.6 %collective-permute-start.10 = (f32[8,64,128]{2,1,0:T(8,128)}, f32[8,64,128]{2,1,0:T(8,128)S(1)}, u32[]{:S(2)}, u32[]{:S(2)}) collective-permute-start(f32[8,64,128]{2,1,0:T(8,128)} %next_slices.6.x.more.own), channel_id=1, source_target_pairs={{0,8},{8,16},{16,24},{24,32},{32,40},{40,48},{48,56},{56,64},{64,7... | collective-permute-start | bytes 786440 | tf_op jit(solution)/shard_map/ppermute | solution.py:300
  85.7 10.3 %collective-permute-start.9 = (f32[8,64,128]{2,1,0:T(8,128)}, f32[8,64,128]{2,1,0:T(8,128)}, u32[]{:S(2)}, u32[]{:S(2)}) collective-permute-start(f32[8,64,128]{2,1,0:T(8,128)} %next_slices.6.x.more.own), channel_id=1, source_target_pairs={{0,504},{8,0},{16,8},{24,16},{32,24},{40,32},{48,40},{56,48},{64,5... | collective-permute-start | bytes 786440 | tf_op jit(solution)/shard_map/ppermute | solution.py:300
  92.5 3.6 copy-start.1
  92.5 3.6 copy-start.3
  109.8 1.6 copy-start.4
  191.8 247.5 %copy-start.5 = (f32[8,512,128]{2,1,0:T(8,128)S(1)}, f32[8,512,128]{2,1,0:T(8,128)}, u32[]{:S(2)}) copy-start(f32[8,512,128]{2,1,0:T(8,128)} %all-gather.3.cloned.1.call-done.everything) | copy-start | bytes 6291460
  440.8 1.2 copy-start.8
Sparse Core Ops, SparseCore 0:
  83.9 25.8 all-gather.2
  174.2 25.9 all-gather.4

commit v3 on v2

--- a/solution.py
+++ b/solution.py
@@ -72,13 +72,11 @@
     return jnp.concatenate([high, high, low], axis=0)
 
 
-def backward_kernel(near, x, hop, out, hop_out):
+def backward_kernel(x, hop, out, back_ref):
     for s in range(x.shape[0]):
-        block = hop[s, 0]
-        hop_out[s] = block
-        out[s] = jnp.dot(
-            left_operand(x[s]), right_operand(conjugated(block)), preferred_element_type=f32
-        )
+        back = right_operand(conjugated(hop[s, 0]))
+        back_ref[s] = back
+        out[s] = jnp.dot(left_operand(x[s]), back, preferred_element_type=f32)
 
 
 def prepare_kernel(near, diag, hop, own_ref, ahead_ref):
@@ -95,12 +93,6 @@
         ahead_ref[s] = right_operand(transposed(hop[s, 3]))
 
 
-def prepare_back_kernel(near, hop_back, back_ref):
-    sites = hop_back.shape[0]
-    for s in range(sites):
-        back_ref[s] = right_operand(conjugated(hop_back[lax.rem(near[s, 7], sites)]))
-
-
 def own_kernel(near, x, mats, out, spread):
     sites = x.shape[0]
     for n in range(sites):
@@ -111,28 +103,23 @@
         out[s] = jnp.dot(left, mats[s], preferred_element_type=f32)
 
 
-def first_kernel(near, own, ahead, received, ahead_mats, out):
+def step_kernel(mode, near, own, ahead, received, ahead_mats, *rest):
     sites = own.shape[0]
+    more = rest[0] if mode != "first" else None
+    back_mats, out, back = rest[-3:] if mode != "image" else (None, rest[-1], None)
     for s in range(sites):
         left = left_operand(ahead[lax.rem(near[s, 3], sites)])
         part = jnp.dot(left, ahead_mats[s], preferred_element_type=f32)
-        out[s] = own[s] + part + received[lax.rem(near[s, 7], sites)]
-
-
-def next_kernel(mode, near, own, ahead, behind, ahead_mats, back_mats, more, out):
-    sites = own.shape[0]
-    for s in range(sites):
-        left = left_operand(ahead[lax.rem(near[s, 3], sites)])
-        right = left_operand(behind[lax.rem(near[s, 7], sites)])
-        applied = own[s] + jnp.dot(
-            jnp.concatenate([left, right], axis=1),
-            jnp.concatenate([ahead_mats[s], back_mats[s]], axis=0),
-            preferred_element_type=f32,
-        )
-        if mode == "next":
-            out[s] = 2.0 * applied - more[s]
+        applied = own[s] + (part + received[lax.rem(near[s, 7], sites)])
+        if mode == "first":
+            result = applied
+        elif mode == "next":
+            result = 2.0 * applied - more[s]
         else:
-            out[s] = RADIUS * applied + CENTER * more[s]
+            result = RADIUS * applied + CENTER * more[s]
+        out[s] = result
+        if mode != "image":
+            back[s] = jnp.dot(left_operand(result), back_mats[s], preferred_element_type=f32)
 
 
 def product_kernel(place, everything, own, image, out):
@@ -319,28 +306,24 @@
         return sites * cols * blocks * 3 * both * both * 2
 
     current = jnp.swapaxes(start_basis, 1, 2)
-    ahead = passed_along(current, -1)
-    back, links = pl.pallas_call(
+    back, back_mats = pl.pallas_call(
         backward_kernel,
-        out_shape=(block, shape((sites, half, both), f32)),
+        out_shape=(block, matrices(1)),
         grid=(1,),
         in_specs=[
-            SMEM_SPEC,
             pl.BlockSpec((sites, cols, both), lambda i: (0, 0, 0)),
             pl.BlockSpec((sites, 1, half, both), lambda i: (0, 3, 0, 0)),
         ],
         out_specs=(
             pl.BlockSpec((sites, cols, both), lambda i: (0, 0, 0)),
-            pl.BlockSpec((sites, half, both), lambda i: (0, 0, 0)),
+            pl.BlockSpec((sites, 3 * both, both), lambda i: (0, 0, 0)),
         ),
         compiler_params=pltpu.CompilerParams(vmem_limit_bytes=VMEM_LIMIT),
         cost_estimate=pl.CostEstimate(
             flops=work(1), bytes_accessed=4 * size, transcendentals=0
         ),
         name="backward",
-    )(neighbors, current, hop_blocks)
-    received = passed_along(back, 1)
-    links_back = passed_along(links, 1)
+    )(current, hop_blocks)
     own_mats, ahead_mats = call(
         prepare_kernel,
         (matrices(4), matrices(1)),
@@ -350,12 +333,11 @@
         moved=1 << 23,
         name="prepare",
     )(neighbors, diag_blocks, hop_blocks)
-    back_mats = call(
-        prepare_back_kernel, matrices(1), 1, 1, flops=1 << 22, moved=1 << 21, name="prepare_back"
-    )(neighbors, links_back)
-
-    def own_part(vectors):
-        return call(
+
+    def apply(vectors, back, mode, *more):
+        ahead = passed_along(vectors, -1)
+        received = passed_along(back, 1)
+        own = call(
             own_kernel,
             block,
             1,
@@ -365,29 +347,26 @@
             moved=8 * size,
             name="own_slice",
         )(neighbors, vectors, own_mats)
-
-    def apply(vectors, mode, more):
-        ahead = passed_along(vectors, -1)
-        behind = passed_along(vectors, 1)
+        if mode != "image":
+            more = (*more, back_mats)
         return call(
-            functools.partial(next_kernel, mode),
-            block,
+            functools.partial(step_kernel, mode),
+            block if mode == "image" else (block, block),
             1,
-            6,
+            4 + len(more),
             flops=work(2),
             moved=8 * size,
             name="next_slices",
-        )(neighbors, own_part(vectors), ahead, behind, ahead_mats, back_mats, more)
+        )(neighbors, own, ahead, received, ahead_mats, *more)
 
     previous = current
-    current = call(first_kernel, block, 1, 4, flops=work(1), moved=6 * size, name="first_step")(
-        neighbors, own_part(current), ahead, received, ahead_mats
-    )
+    current, back = apply(current, back, "first")
     for _ in range(DEGREE - 1):
-        previous, current = current, apply(current, "next", previous)
+        following, back = apply(current, back, "next", previous)
+        previous, current = current, following
 
     everything = lax.all_gather(current.reshape(sites * cols, both), "vec", axis=0)
-    image = apply(current, "image", current)
+    image = apply(current, back, "image", current)
     kept = 5 * cols // 2
     products = call(
         product_kernel,

time: 451 us -> 452 us (level)
  starting transfers between devices: 46.1 us -> 38.9 us
    ppermute x11 -> x10, starting transfers between devices: 46 us -> 38.8 us  [passed_along(): return lax.ppermute(x, 'site', [(i, (i + by) % size) for i in range(size)])]
    ppermute x11 -> x10, waiting for transfers between devices: 20.8 us -> 25 us  [passed_along(): return lax.ppermute(x, 'site', [(i, (i + by) % size) for i in range(size)])]
    pallas_call x12 -> x11, Pallas kernels: 16 us -> 18.8 us  [the longest x5 10 us: apply(): call(functools.partial(step_kernel, mode), block if mode == 'image' else...]
  transfers between devices with their start and end apart: 13 -> 12, of which waited for: 9 -> 9; matrix products, arithmetic and copies ran while one was open for 0% -> 0% of each run, Pallas kernels for 58% -> 58%
where the time goes in v3:
time: 452 us; the launch traced here: 451 us
  Pallas kernels  275 us (61%)
  blocking collectives  77.7 us (17%)
  starting transfers between devices  38.9 us (9%)
  waiting for transfers between devices  37.4 us (8%)
  between operations  14.3 us (3%)
  local copies, waits for them, and re-layouts  8.29 us (2%)
    pallas_call x1, Pallas kernels, local(): call(functools.partial(inverse_kernel, count), shape((all_cols, all_cols)...  248 us
    ppermute x10, starting transfers between devices, passed_along(): return lax.ppermute(x, 'site', [(i, (i + by) % size) for i in range(size)])  38.8 us
    all_to_all x1, blocking collectives, local(): lax.all_to_all(products.reshape(slices, 8, both), 'site', 0, 0, tiled=True)  35 us
    ppermute x10, waiting for transfers between devices, passed_along(): return lax.ppermute(x, 'site', [(i, (i + by) % size) for i in range(size)])  25 us
    all_to_all x1, blocking collectives, local(): lax.all_to_all(summed, 'site', 0, 0, tiled=True).reshape(slices * 8, both)  24.9 us
    all_gather x1, blocking collectives, local(): gram = lax.all_gather(whole[:kept], 'vec', axis=0)  17.7 us
    all_gather x1, waiting for transfers between devices, local(): lax.all_gather(current.reshape(sites * cols, both), 'vec', axis=0)  12.3 us
    pallas_call x5, Pallas kernels, apply(): call(functools.partial(step_kernel, mode), block if mode == 'image' else...  10 us
  transfers between devices with their start and end apart: 12, of which 9 were waited for; matrix products, arithmetic and copies ran while one was open for 0% of the time, Pallas kernels for 58%

profile of v3, /device:TPU:1, one launch (start us, length us, event | category | flops | bytes accessed | tf_op | source)
XLA Modules:
  0.0 451.1 jit_solution(7689953351406324338)
XLA Ops:
  9.7 4.4 collective-permute-start.1
  14.1 12.0 %collective-permute-start = (f32[8,64,128]{2,1,0:T(8,128)}, f32[8,64,128]{2,1,0:T(8,128)S(1)}, u32[]{:S(2)}, u32[]{:S(2)}) collective-permute-start(f32[8,64,128]{2,1,0:T(8,128)} %bitcast.1.x.rest_0_), channel_id=1, source_target_pairs={{0,504},{8,0},{16,8},{24,16},{32,24},{40,32},{48,40},{56,48},{64,5... | collective-permute-start | bytes 786440 | tf_op jit(solution)/shard_map/ppermute | solution.py:287
  29.0 3.1 prepare.1
  32.1 1.9 own_slice.5.own
  34.0 1.9 next_slices.5
  35.9 4.7 %collective-permute-start.2 = (f32[8,64,128]{2,1,0:T(8,128)S(1)}, f32[8,64,128]{2,1,0:T(8,128)S(1)}, u32[]{:S(2)}, u32[]{:S(2)}) collective-permute-start(f32[8,64,128]{2,1,0:T(8,128)S(1)} %get-tuple-element.18.x.rest_0_), channel_id=1, source_target_pairs={{0,504},{8,0},{16,8},{24,16},{32,24},{40,32},{48,40},{56,48},{64,5... | collective-permute-start | bytes 786440 | tf_op jit(solution)/shard_map/ppermute | solution.py:287
  40.6 1.9 collective-permute-start.3
  44.7 7.2 %collective-permute-done.3.received = f32[8,64,128]{2,1,0:T(8,128)S(1)} collective-permute-done((f32[8,64,128]{2,1,0:T(8,128)S(1)}, f32[8,64,128]{2,1,0:T(8,128)S(1)}, u32[]{:S(2)}, u32[]{:S(2)}) %collective-permute-start.3) | collective-permute-done | bytes 262176 | tf_op jit(solution)/shard_map/ppermute | solution.py:287
  51.8 2.3 next_slices.6
  54.1 1.9 collective-permute-start.4
  56.0 3.4 collective-permute-start.5
  59.4 1.3 own_slice.7.own
  61.2 5.2 %collective-permute-done.5.received = f32[8,64,128]{2,1,0:T(8,128)S(1)} collective-permute-done((f32[8,64,128]{2,1,0:T(8,128)S(1)}, f32[8,64,128]{2,1,0:T(8,128)S(1)}, u32[]{:S(2)}, u32[]{:S(2)}) %collective-permute-start.5) | collective-permute-done | bytes 262176 | tf_op jit(solution)/shard_map/ppermute | solution.py:287
  66.5 1.9 next_slices.7
  68.4 1.9 collective-permute-start.6
  70.4 3.4 collective-permute-start.7
  75.5 5.3 %collective-permute-done.7.received = f32[8,64,128]{2,1,0:T(8,128)S(1)} collective-permute-done((f32[8,64,128]{2,1,0:T(8,128)S(1)}, f32[8,64,128]{2,1,0:T(8,128)S(1)}, u32[]{:S(2)}, u32[]{:S(2)}) %collective-permute-start.7) | collective-permute-done | bytes 262176 | tf_op jit(solution)/shard_map/ppermute | solution.py:287
  80.8 2.5 next_slices.8
  84.1 1.9 collective-permute-start.8
  86.0 3.4 collective-permute-start.9
  89.4 1.7 own_slice.9.own
  91.4 5.4 %collective-permute-done.9.received = f32[8,64,128]{2,1,0:T(8,128)} collective-permute-done((f32[8,64,128]{2,1,0:T(8,128)}, f32[8,64,128]{2,1,0:T(8,128)}, u32[]{:S(2)}, u32[]{:S(2)}) %collective-permute-start.9) | collective-permute-done | bytes 262176 | tf_op jit(solution)/shard_map/ppermute | solution.py:287
  96.8 1.3 next_slices.9.image
  98.1 12.3 %all-gather.3.cloned.1.call-done.everything = f32[8,512,128]{2,1,0:T(8,128)} async-done(((f32[1,512,128]{2,1,0:T(8,128)}), f32[8,512,128]{2,1,0:T(8,128)}) %all-gather.3.cloned.1.call-update) | async-done | bytes 2097168 | tf_op jit(solution)/shard_map/all_gather | solution.py:368
  110.4 1.6 copy-done.2
  112.0 2.0 products.1
  114.0 35.0 %all_to_all.10.parts = f32[64,8,128]{2,1,0:T(8,128)S(1)} all-to-all(f32[64,8,128]{2,1,0:T(8,128)S(1)} %bitcast.10), channel_id=1, replica_groups=mesh['site'=64,'vec'=8] {'site'}, dimensions={0} | all-to-all | bytes 524288 | tf_op jit(solution)/shard_map/all_to_all | solution.py:381
  149.1 24.9 %all_to_all.11 = f32[64,8,128]{2,1,0:T(8,128)S(1)} all-to-all(f32[64,8,128]{2,1,0:T(8,128)S(1)} %sum_parts.1), channel_id=1, replica_groups=mesh['site'=64,'vec'=8] {'site'}, dimensions={0} | all-to-all | bytes 524288 | tf_op jit(solution)/shard_map/all_to_all | solution.py:385
  174.7 17.7 %all_gather.17.gathered = f32[8,160,128]{2,1,0:T(8,128)S(1)} all-gather(f32[1,160,128]{2,1,0:T(8,128)S(1)} %slice_bitcast_fusion.1), channel_id=1, replica_groups=mesh['site'=64,'vec'=8] {'vec'}, dimensions={0}, use_global_device_ids=true | all-gather | bytes 737280 | tf_op jit(solution)/shard_map/all_gather | solution.py:387
  192.4 247.5 %inverse_factor.1.inverse = f32[512,512]{1,0:T(8,128)S(1)} custom-call(f32[8,160,128]{2,1,0:T(8,128)S(1)} %all_gather.17.gathered), custom_call_target="tpu_custom_call" | custom-call | flops 7247757312 | bytes 2097152 | tf_op jit(solution)/shard_map/inverse_factor/pallas_call | solution.py:389
  440.0 1.4 basis.1
  442.6 1.6 projected.1
  (38 shorter events, 12.8 us)
Async XLA Ops:
  7.2 103.2 %all-gather.3.cloned.1.call-start = ((), (), s32[]{:S(2)}) async-start(), calls=%async_computation.2 | async-start | bytes 2359296 | tf_op jit(solution)/shard_map/all_gather | solution.py:368
  7.2 1.2 copy-start.4
  9.7 24.2 %collective-permute-start.1 = (f32[8,64,128]{2,1,0:T(8,128)S(1)}, f32[8,64,128]{2,1,0:T(8,128)S(1)}, u32[]{:S(2)}, u32[]{:S(2)}) collective-permute-start(f32[8,64,128]{2,1,0:T(8,128)S(1)} %get-tuple-element.15), channel_id=1, source_target_pairs={{0,8},{8,16},{16,24},{24,32},{32,40},{40,48},{48,56},{56,64},{64,7... | collective-permute-start | bytes 786440 | tf_op jit(solution)/shard_map/ppermute | solution.py:287
  14.1 19.8 %collective-permute-start = (f32[8,64,128]{2,1,0:T(8,128)}, f32[8,64,128]{2,1,0:T(8,128)S(1)}, u32[]{:S(2)}, u32[]{:S(2)}) collective-permute-start(f32[8,64,128]{2,1,0:T(8,128)} %bitcast.1.x.rest_0_), channel_id=1, source_target_pairs={{0,504},{8,0},{16,8},{24,16},{32,24},{40,32},{48,40},{56,48},{64,5... | collective-permute-start | bytes 786440 | tf_op jit(solution)/shard_map/ppermute | solution.py:287
  26.1 1.2 copy-start.5
  27.3 0.7 copy-start.7
  28.0 0.9 copy-start.9
  32.1 48.7 %copy-start = (bf16[8,384,128]{2,1,0:T(8,128)(2,1)}, bf16[8,384,128]{2,1,0:T(8,128)(2,1)S(1)}, u32[]{:S(2)}) copy-start(bf16[8,384,128]{2,1,0:T(8,128)(2,1)S(1)} %get-tuple-element.16.ahead_mats) | copy-start | bytes 2359300
  35.9 8.8 %collective-permute-start.2 = (f32[8,64,128]{2,1,0:T(8,128)S(1)}, f32[8,64,128]{2,1,0:T(8,128)S(1)}, u32[]{:S(2)}, u32[]{:S(2)}) collective-permute-start(f32[8,64,128]{2,1,0:T(8,128)S(1)} %get-tuple-element.18.x.rest_0_), channel_id=1, source_target_pairs={{0,504},{8,0},{16,8},{24,16},{32,24},{40,32},{48,40},{56,48},{64,5... | collective-permute-start | bytes 786440 | tf_op jit(solution)/shard_map/ppermute | solution.py:287
  40.6 11.2 %collective-permute-start.3 = (f32[8,64,128]{2,1,0:T(8,128)S(1)}, f32[8,64,128]{2,1,0:T(8,128)S(1)}, u32[]{:S(2)}, u32[]{:S(2)}) collective-permute-start(f32[8,64,128]{2,1,0:T(8,128)S(1)} %get-tuple-element.19), channel_id=1, source_target_pairs={{0,8},{8,16},{16,24},{24,32},{32,40},{40,48},{48,56},{56,64},{64,7... | collective-permute-start | bytes 786440 | tf_op jit(solution)/shard_map/ppermute | solution.py:287
  54.1 7.1 %collective-permute-start.4 = (f32[8,64,128]{2,1,0:T(8,128)S(1)}, f32[8,64,128]{2,1,0:T(8,128)S(1)}, u32[]{:S(2)}, u32[]{:S(2)}) collective-permute-start(f32[8,64,128]{2,1,0:T(8,128)S(1)} %get-tuple-element.20.x.rest_0_), channel_id=1, source_target_pairs={{0,504},{8,0},{16,8},{24,16},{32,24},{40,32},{48,40},{56,48},{64,5... | collective-permute-start | bytes 786440 | tf_op jit(solution)/shard_map/ppermute | solution.py:287
  56.0 10.4 %collective-permute-start.5 = (f32[8,64,128]{2,1,0:T(8,128)S(1)}, f32[8,64,128]{2,1,0:T(8,128)S(1)}, u32[]{:S(2)}, u32[]{:S(2)}) collective-permute-start(f32[8,64,128]{2,1,0:T(8,128)S(1)} %get-tuple-element.21), channel_id=1, source_target_pairs={{0,8},{8,16},{16,24},{24,32},{32,40},{40,48},{48,56},{56,64},{64,7... | collective-permute-start | bytes 786440 | tf_op jit(solution)/shard_map/ppermute | solution.py:287
  68.4 7.1 %collective-permute-start.6 = (f32[8,64,128]{2,1,0:T(8,128)S(1)}, f32[8,64,128]{2,1,0:T(8,128)S(1)}, u32[]{:S(2)}, u32[]{:S(2)}) collective-permute-start(f32[8,64,128]{2,1,0:T(8,128)S(1)} %get-tuple-element.22.x), channel_id=1, source_target_pairs={{0,504},{8,0},{16,8},{24,16},{32,24},{40,32},{48,40},{56,48},{64,5... | collective-permute-start | bytes 786440 | tf_op jit(solution)/shard_map/ppermute | solution.py:287
  70.3 19.1 %copy-start.8 = (s32[8,8]{1,0:T(8,128)S(1)}, s32[8,8]{1,0:T(8,128)}, u32[]{:S(2)}) copy-start(s32[8,8]{1,0:T(8,128)} %near.21) | copy-start | bytes 772
  70.4 10.4 %collective-permute-start.7 = (f32[8,64,128]{2,1,0:T(8,128)S(1)}, f32[8,64,128]{2,1,0:T(8,128)S(1)}, u32[]{:S(2)}, u32[]{:S(2)}) collective-permute-start(f32[8,64,128]{2,1,0:T(8,128)S(1)} %get-tuple-element.23), channel_id=1, source_target_pairs={{0,8},{8,16},{16,24},{24,32},{32,40},{40,48},{48,56},{56,64},{64,7... | collective-permute-start | bytes 786440 | tf_op jit(solution)/shard_map/ppermute | solution.py:287
  83.3 0.7 copy-start.10
  84.1 357.4 %all-gather.5.cloned.1.call-start = ((), (), s32[]{:S(2)}) async-start(), calls=%async_computation.3 | async-start | bytes 1179648 | tf_op jit(solution)/shard_map/all_gather | solution.py:386
  84.1 7.3 %collective-permute-start.8 = (f32[8,64,128]{2,1,0:T(8,128)}, f32[8,64,128]{2,1,0:T(8,128)S(1)}, u32[]{:S(2)}, u32[]{:S(2)}) collective-permute-start(f32[8,64,128]{2,1,0:T(8,128)} %get-tuple-element.24.x.rest_0_.own), channel_id=1, source_target_pairs={{0,504},{8,0},{16,8},{24,16},{32,24},{40,32},{48,40},{56,48},{64,5... | collective-permute-start | bytes 786440 | tf_op jit(solution)/shard_map/ppermute | solution.py:287
  86.0 10.8 %collective-permute-start.9 = (f32[8,64,128]{2,1,0:T(8,128)}, f32[8,64,128]{2,1,0:T(8,128)}, u32[]{:S(2)}, u32[]{:S(2)}) collective-permute-start(f32[8,64,128]{2,1,0:T(8,128)} %copy-done.10), channel_id=1, source_target_pairs={{0,8},{8,16},{16,24},{24,32},{32,40},{40,48},{48,56},{56,64},{64,7... | collective-permute-start | bytes 786440 | tf_op jit(solution)/shard_map/ppermute | solution.py:287
  89.4 7.4 %copy-start.1 = (bf16[8,384,128]{2,1,0:T(8,128)(2,1)S(1)}, bf16[8,384,128]{2,1,0:T(8,128)(2,1)}, u32[]{:S(2)}) copy-start(bf16[8,384,128]{2,1,0:T(8,128)(2,1)} %copy-done) | copy-start | bytes 2359300
  110.4 1.6 copy-start.2
  192.4 247.5 %copy-start.3 = (f32[8,512,128]{2,1,0:T(8,128)S(1)}, f32[8,512,128]{2,1,0:T(8,128)}, u32[]{:S(2)}) copy-start(f32[8,512,128]{2,1,0:T(8,128)} %all-gather.3.cloned.1.call-done.everything) | copy-start | bytes 6291460
  441.4 1.2 copy-start.6
Sparse Core Ops, SparseCore 0:
  84.2 26.1 all-gather.2
  174.8 25.9 all-gather.4

commit v4 on v2

--- a/solution.py
+++ b/solution.py
@@ -135,39 +135,67 @@
             out[s] = RADIUS * applied + CENTER * more[s]
 
 
-def product_kernel(place, everything, own, image, out):
-    devices = everything.shape[0]
+def senders(devices):
+    chips = devices // 2
+    table = []
+    for v in range(devices):
+        x, c = v // 2, v % 2
+        opposite = (x + chips // 2) % chips
+        table.append(
+            [
+                2 * ((x - 1) % chips) + c,
+                2 * ((x + 1) % chips) + 1 - c,
+                2 * x + 1 - c,
+                2 * opposite + (1 - c if x < chips // 2 else c),
+            ]
+        )
+    return table
+
+
+def product_kernel(own, image, first, second, third, fourth, out):
     sites, cols, wide = own.shape
-    f = jnp.concatenate([own[s] for s in range(sites)], axis=1)
-    h = jnp.concatenate([image[s] for s in range(sites)], axis=1)
-    left = left_operand(jnp.concatenate([f, h], axis=0))
-    third = sites * wide
-    shift = place[0]
-    tiles = devices // 2
-    for p in range(tiles):
-        both = []
-        for j in (2 * p, 2 * p + 1):
-            u = lax.rem(shift + j, devices)
-            both.append(
-                jnp.concatenate(
-                    [everything[u, s * cols : (s + 1) * cols] for s in range(sites)], axis=1
-                )
-            )
-        high, low = split(jnp.concatenate(both, axis=0))
-        dot = functools.partial(lax.dot_general, dimension_numbers=NT, preferred_element_type=f32)
-        tile = dot(left[:, : 2 * third], jnp.concatenate([high, high], axis=1)) + dot(
-            left[:, :third], low
-        )
-        if p < 2:
-            out[p * cols : (p + 1) * cols] = tile[:cols]
-        elif p == 2:
-            out[2 * cols : 2 * cols + cols // 2] = jnp.concatenate(
-                [tile[: cols // 2, :cols], tile[cols // 2 : cols, :cols]], axis=1
-            )
-        start = 5 * cols // 2 + p * cols
-        out[start : start + cols] = tile[cols:]
-    start = 5 * cols // 2 + tiles * cols
-    out[start:] = jnp.zeros((out.shape[0] - start, wide), f32)
+
+    def flat(ref):
+        return jnp.concatenate([ref[s] for s in range(sites)], axis=1)
+
+    f = flat(own)
+    high, low = split(jnp.concatenate([f, flat(image)], axis=0))
+    left = jnp.concatenate([high, low], axis=1)
+    half = cols // 2
+    dot = functools.partial(lax.dot_general, dimension_numbers=NT, preferred_element_type=f32)
+    for p, group in enumerate(((own, first), (second, third), (fourth,))):
+        h, l = split(jnp.concatenate([f if r is own else flat(r) for r in group], axis=0))
+        tile = dot(left, jnp.concatenate([h, h], axis=1)) + dot(high, l)
+        for i in range(2):
+            part = tile[i * cols : (i + 1) * cols]
+            start = i * (5 * half) + p * cols
+            if len(group) == 2:
+                out[start : start + cols] = part
+            else:
+                out[start : start + half] = jnp.concatenate([part[:half], part[half:]], axis=1)
+    out[10 * half :] = jnp.zeros((out.shape[0] - 10 * half, wide), f32)
+
+
+def lines_of(gathered):
+    devices, _, wide = gathered.shape
+    half = wide // 2
+    blocks = {}
+    for v, others in enumerate(senders(devices)):
+        for j, u in enumerate([v, *others]):
+            if j < 4:
+                rows = gathered[v, (j // 2) * half : (j // 2 + 1) * half]
+                block = rows[:, (j % 2) * half : (j % 2 + 1) * half]
+            else:
+                rows = gathered[v, wide : wide + half // 2]
+                block = jnp.concatenate([rows[:, :half], rows[:, half:]], axis=0)
+            blocks[v, u] = block
+    for v in range(devices):
+        for u in range(devices):
+            if (v, u) not in blocks:
+                blocks[v, u] = blocks[u, v].T
+    return [
+        jnp.concatenate([blocks[v, u] for u in range(devices)], axis=1) for v in range(devices)
+    ]
 
 
 def sum_kernel(parts, out):
@@ -187,22 +215,8 @@
 
 def inverse_kernel(count, gathered, out, scaled, factor, product):
     n = out.shape[0]
-    devices, _, wide = gathered.shape
-    half = wide // 2
-    blocks = {}
-    for v in range(devices):
-        for j in range(5):
-            if j < 4:
-                rows = gathered[v, (j // 2) * half : (j // 2 + 1) * half]
-                block = rows[:, (j % 2) * half : (j % 2 + 1) * half]
-            else:
-                rows = gathered[v, wide:]
-                block = jnp.concatenate([rows[:, :half], rows[:, half:]], axis=0)
-            blocks[v, (v + j) % devices] = block
-            if 0 < j < 4:
-                blocks[(v + j) % devices, v] = block.T
-    for v in range(devices):
-        line = jnp.concatenate([blocks[v, u] for u in range(devices)], axis=1)
+    half = gathered.shape[2] // 2
+    for v, line in enumerate(lines_of(gathered)):
         scaled[v * half : (v + 1) * half, :] = line * (1.0 / count)
     rows = lax.broadcasted_iota(jnp.int32, (n, n), 0)
     cols = lax.broadcasted_iota(jnp.int32, (n, n), 1)
@@ -274,22 +288,8 @@
 
 
 def projected_kernel(count, place, moments, inverse, out):
-    devices, _, wide = moments.shape
-    half = wide // 2
-    tiles = devices // 2
-    low = low_lanes((half, wide))
-    lines = []
-    for v in range(devices):
-        turned = [moments[v, p * half : (p + 1) * half] for p in range(tiles)]
-        line = []
-        for q in range(tiles):
-            j = (2 * q - v) % devices
-            if v % 2 == 0:
-                line.append(turned[j // 2])
-            else:
-                line.append(swapped(jnp.where(low, turned[(j // 2 + 1) % tiles], turned[j // 2])))
-        lines.append(jnp.concatenate(line, axis=1))
-    moment = jnp.concatenate(lines, axis=0)
+    half = moments.shape[2] // 2
+    moment = jnp.concatenate(lines_of(moments), axis=0)
     mine = inverse[pl.ds(pl.multiple_of(place[0] * half, half), half), :]
     half_way = multiply(mine, moment, NN)
     out[...] = multiply(half_way, inverse[...], NT) * (1.0 / count)
@@ -386,18 +386,23 @@
     for _ in range(DEGREE - 1):
         previous, current = current, apply(current, "next", previous)
 
-    everything = lax.all_gather(current.reshape(sites * cols, both), "vec", axis=0)
     image = apply(current, "image", current)
+    table = senders(devices)
+    others = [
+        lax.ppermute(current, "vec", [(table[v][i], v) for v in range(devices)]) for i in range(4)
+    ]
     kept = 5 * cols // 2
     products = call(
         product_kernel,
         shape((slices * 8, both), f32),
-        1,
-        3,
-        flops=6 * all_cols * 2 * cols * sites * both,
+        0,
+        6,
+        flops=6 * 5 * cols * 2 * cols * sites * both,
         moved=1 << 22,
         name="products",
-    )(place, everything, current, image)
+    )(current, image, *others)
+    flat, _ = lax.optimization_barrier((current.reshape(sites * cols, both), products))
+    everything = lax.all_gather(flat, "vec", axis=0)
 
     parts = lax.all_to_all(products.reshape(slices, 8, both), "site", 0, 0, tiled=True)
     summed = call(

time: 451 us -> 449 us (level)
  starting transfers between devices: 46.1 us -> 63.4 us
  blocking collectives: 77.6 us -> 65.7 us
  waiting for transfers between devices: 33.1 us -> 24.6 us
    ppermute x0 -> x4, starting transfers between devices: none -> 17.3 us  [local(): lax.ppermute(current, 'vec', [(table[v][i], v) for v in range(devices)])]
    all_gather x1, waiting for transfers between devices: 12.3 us -> 0.02 us  [local(): everything = lax.all_gather(flat, 'vec', axis=0)]
    all_to_all x1, blocking collectives: 35 us -> 24.1 us  [local(): lax.all_to_all(products.reshape(slices, 8, both), 'site', 0, 0, tiled=True)]
    ppermute x0 -> x4, waiting for transfers between devices: none -> 5.57 us  [local(): lax.ppermute(current, 'vec', [(table[v][i], v) for v in range(devices)])]
  transfers between devices with their start and end apart: 13 -> 17, of which waited for: 9 -> 7; matrix products, arithmetic and copies ran while one was open for 0% -> 0% of each run, Pallas kernels for 58% -> 59%
where the time goes in v4:
time: 449 us; the launch traced here: 448 us
  Pallas kernels  272 us (61%)
  blocking collectives  65.7 us (15%)
  starting transfers between devices  63.4 us (14%)
  waiting for transfers between devices  24.6 us (5%)
  between operations  14.4 us (3%)
  local copies, waits for them, and re-layouts  7.56 us (2%)
    pallas_call x1, Pallas kernels, local(): call(functools.partial(inverse_kernel, count), shape((all_cols, all_cols)...  248 us
    ppermute x11, starting transfers between devices, passed_along(): return lax.ppermute(x, 'site', [(i, (i + by) % size) for i in range(size)])  46 us
    all_to_all x1, blocking collectives, local(): lax.all_to_all(summed, 'site', 0, 0, tiled=True).reshape(slices * 8, both)  24.5 us
    all_to_all x1, blocking collectives, local(): lax.all_to_all(products.reshape(slices, 8, both), 'site', 0, 0, tiled=True)  24.1 us
    ppermute x11, waiting for transfers between devices, passed_along(): return lax.ppermute(x, 'site', [(i, (i + by) % size) for i in range(size)])  18.9 us
    ppermute x4, starting transfers between devices, local(): lax.ppermute(current, 'vec', [(table[v][i], v) for v in range(devices)])  17.3 us
    all_gather x1, blocking collectives, local(): gram = lax.all_gather(whole[:kept], 'vec', axis=0)  17.2 us
  transfers between devices with their start and end apart: 17, of which 7 were waited for; matrix products, arithmetic and copies ran while one was open for 0% of the time, Pallas kernels for 59%

profile of v4, /device:TPU:1, one launch (start us, length us, event | category | flops | bytes accessed | tf_op | source)
XLA Modules:
  0.0 447.6 jit_solution(1032608737840019047)
XLA Ops:
  10.5 4.4 collective-permute-start.1
  14.8 11.9 %collective-permute-start = (f32[8,64,128]{2,1,0:T(8,128)}, f32[8,64,128]{2,1,0:T(8,128)S(1)}, u32[]{:S(2)}, u32[]{:S(2)}) collective-permute-start(f32[8,64,128]{2,1,0:T(8,128)} %bitcast.1.x.more), channel_id=1, source_target_pairs={{0,504},{8,0},{16,8},{24,16},{32,24},{40,32},{48,40},{56,48},{64,5... | collective-permute-start | bytes 786440 | tf_op jit(solution)/shard_map/ppermute | solution.py:300
  26.8 1.9 collective-permute-start.4
  30.9 3.1 prepare.1
  34.0 1.7 own_slice.5.own
  36.6 6.7 %collective-permute-start.2 = (f32[8,64,128]{2,1,0:T(8,128)S(1)}, f32[8,64,128]{2,1,0:T(8,128)S(1)}, u32[]{:S(2)}, u32[]{:S(2)}) collective-permute-start(f32[8,64,128]{2,1,0:T(8,128)S(1)} %first_step.1.x.more), channel_id=1, source_target_pairs={{0,504},{8,0},{16,8},{24,16},{32,24},{40,32},{48,40},{56,48},{64,5... | collective-permute-start | bytes 786440 | tf_op jit(solution)/shard_map/ppermute | solution.py:300
  43.3 1.9 collective-permute-start.3
  47.7 7.2 %collective-permute-done.3.behind = f32[8,64,128]{2,1,0:T(8,128)S(1)} collective-permute-done((f32[8,64,128]{2,1,0:T(8,128)S(1)}, f32[8,64,128]{2,1,0:T(8,128)S(1)}, u32[]{:S(2)}, u32[]{:S(2)}) %collective-permute-start.3) | collective-permute-done | bytes 262176 | tf_op jit(solution)/shard_map/ppermute | solution.py:300
  56.2 1.9 collective-permute-start.5
  58.1 3.4 collective-permute-start.6
  63.3 5.2 %collective-permute-done.6.behind = f32[8,64,128]{2,1,0:T(8,128)S(1)} collective-permute-done((f32[8,64,128]{2,1,0:T(8,128)S(1)}, f32[8,64,128]{2,1,0:T(8,128)S(1)}, u32[]{:S(2)}, u32[]{:S(2)}) %collective-permute-start.6) | collective-permute-done | bytes 262176 | tf_op jit(solution)/shard_map/ppermute | solution.py:300
  69.5 1.9 collective-permute-start.7
  71.5 3.4 collective-permute-start.8
  76.6 5.2 %collective-permute-done.8.behind = f32[8,64,128]{2,1,0:T(8,128)S(1)} collective-permute-done((f32[8,64,128]{2,1,0:T(8,128)S(1)}, f32[8,64,128]{2,1,0:T(8,128)S(1)}, u32[]{:S(2)}, u32[]{:S(2)}) %collective-permute-start.8) | collective-permute-done | bytes 262176 | tf_op jit(solution)/shard_map/ppermute | solution.py:300
  81.9 1.7 next_slices.6.x.more.own
  83.6 1.9 collective-permute-start.10
  85.5 6.7 %collective-permute-start.9 = (f32[8,64,128]{2,1,0:T(8,128)}, f32[8,64,128]{2,1,0:T(8,128)S(1)}, u32[]{:S(2)}, u32[]{:S(2)}) collective-permute-start(f32[8,64,128]{2,1,0:T(8,128)} %next_slices.6.x.more.own), channel_id=1, source_target_pairs={{0,504},{8,0},{16,8},{24,16},{32,24},{40,32},{48,40},{56,48},{64,5... | collective-permute-start | bytes 786440 | tf_op jit(solution)/shard_map/ppermute | solution.py:300
  92.2 3.1 collective-permute-start.11
  95.3 8.8 %collective-permute-start.12 = (f32[8,64,128]{2,1,0:T(8,128)}, f32[8,64,128]{2,1,0:T(8,128)S(1)}, u32[]{:S(2)}, u32[]{:S(2)}) collective-permute-start(f32[8,64,128]{2,1,0:T(8,128)} %next_slices.6.x.more.own), channel_id=1, source_target_pairs={{3,0},{2,1},{5,2},{4,3},{7,4},{6,5},{1,6},{0,7},{11,8},{10,9},{13,... | collective-permute-start | bytes 786440 | tf_op jit(solution)/shard_map/ppermute | solution.py:392
  104.1 1.9 collective-permute-start.13
  106.1 3.4 collective-permute-start.14
  109.5 1.7 own_slice.9.own
  111.3 1.4 next_slices.7.image
  112.6 5.6 %collective-permute-done.14.fourth = f32[8,64,128]{2,1,0:T(8,128)S(1)} collective-permute-done((f32[8,64,128]{2,1,0:T(8,128)}, f32[8,64,128]{2,1,0:T(8,128)S(1)}, u32[]{:S(2)}, u32[]{:S(2)}) %collective-permute-start.14) | collective-permute-done | bytes 262176 | tf_op jit(solution)/shard_map/ppermute | solution.py:392
  118.2 1.8 products.1
  120.1 24.1 %all_to_all.10.parts = f32[64,8,128]{2,1,0:T(8,128)S(1)} all-to-all(f32[64,8,128]{2,1,0:T(8,128)S(1)} %bitcast.12), channel_id=1, replica_groups=mesh['site'=64,'vec'=8] {'site'}, dimensions={0} | all-to-all | bytes 524288 | tf_op jit(solution)/shard_map/all_to_all | solution.py:407
  144.3 24.5 %all_to_all.11 = f32[64,8,128]{2,1,0:T(8,128)S(1)} all-to-all(f32[64,8,128]{2,1,0:T(8,128)S(1)} %sum_parts.1), channel_id=1, replica_groups=mesh['site'=64,'vec'=8] {'site'}, dimensions={0} | all-to-all | bytes 524288 | tf_op jit(solution)/shard_map/all_to_all | solution.py:411
  169.5 17.2 %all_gather.21.gathered = f32[8,160,128]{2,1,0:T(8,128)S(1)} all-gather(f32[1,160,128]{2,1,0:T(8,128)S(1)} %slice_bitcast_fusion.1), channel_id=1, replica_groups=mesh['site'=64,'vec'=8] {'vec'}, dimensions={0}, use_global_device_ids=true | all-gather | bytes 737280 | tf_op jit(solution)/shard_map/all_gather | solution.py:413
  186.6 247.7 %inverse_factor.1.inverse = f32[512,512]{1,0:T(8,128)S(1)} custom-call(f32[8,160,128]{2,1,0:T(8,128)S(1)} %all_gather.21.gathered), custom_call_target="tpu_custom_call" | custom-call | flops 7247757312 | bytes 2097152 | tf_op jit(solution)/shard_map/inverse_factor/pallas_call | solution.py:415
  434.4 1.6 copy-done.2
  435.9 1.4 basis.1
  438.6 2.2 projected.1
  (39 shorter events, 16.8 us)
Async XLA Ops:
  7.2 427.2 %all-gather.6.cloned.1.call-start = ((), (), s32[]{:S(2)}) async-start(), calls=%async_computation.3 | async-start | bytes 2359296 | tf_op jit(solution)/shard_map/all_gather | solution.py:405
  7.2 1.2 copy-start
  8.4 0.7 copy-start.4
  10.5 25.3 %collective-permute-start.1 = (f32[8,64,128]{2,1,0:T(8,128)S(1)}, f32[8,64,128]{2,1,0:T(8,128)S(1)}, u32[]{:S(2)}, u32[]{:S(2)}) collective-permute-start(f32[8,64,128]{2,1,0:T(8,128)S(1)} %get-tuple-element.8), channel_id=1, source_target_pairs={{0,8},{8,16},{16,24},{24,32},{32,40},{40,48},{48,56},{56,64},{64,7... | collective-permute-start | bytes 786440 | tf_op jit(solution)/shard_map/ppermute | solution.py:300
  14.8 20.9 %collective-permute-start = (f32[8,64,128]{2,1,0:T(8,128)}, f32[8,64,128]{2,1,0:T(8,128)S(1)}, u32[]{:S(2)}, u32[]{:S(2)}) collective-permute-start(f32[8,64,128]{2,1,0:T(8,128)} %bitcast.1.x.more), channel_id=1, source_target_pairs={{0,504},{8,0},{16,8},{24,16},{32,24},{40,32},{48,40},{56,48},{64,5... | collective-permute-start | bytes 786440 | tf_op jit(solution)/shard_map/ppermute | solution.py:300
  26.8 18.5 %collective-permute-start.4 = (f32[8,64,128]{2,1,0:T(8,128)S(1)}, f32[8,64,128]{2,1,0:T(8,128)S(1)}, u32[]{:S(2)}, u32[]{:S(2)}) collective-permute-start(f32[8,64,128]{2,1,0:T(8,128)S(1)} %get-tuple-element.10), channel_id=1, source_target_pairs={{0,8},{8,16},{16,24},{24,32},{32,40},{40,48},{48,56},{56,64},{64,7... | collective-permute-start | bytes 786440 | tf_op jit(solution)/shard_map/ppermute | solution.py:300
  28.7 1.2 copy-start.1
  30.0 0.9 copy-start.5
  36.6 11.0 %collective-permute-start.2 = (f32[8,64,128]{2,1,0:T(8,128)S(1)}, f32[8,64,128]{2,1,0:T(8,128)S(1)}, u32[]{:S(2)}, u32[]{:S(2)}) collective-permute-start(f32[8,64,128]{2,1,0:T(8,128)S(1)} %first_step.1.x.more), channel_id=1, source_target_pairs={{0,504},{8,0},{16,8},{24,16},{32,24},{40,32},{48,40},{56,48},{64,5... | collective-permute-start | bytes 786440 | tf_op jit(solution)/shard_map/ppermute | solution.py:300
  43.3 11.5 %collective-permute-start.3 = (f32[8,64,128]{2,1,0:T(8,128)S(1)}, f32[8,64,128]{2,1,0:T(8,128)S(1)}, u32[]{:S(2)}, u32[]{:S(2)}) collective-permute-start(f32[8,64,128]{2,1,0:T(8,128)S(1)} %first_step.1.x.more), channel_id=1, source_target_pairs={{0,8},{8,16},{16,24},{24,32},{32,40},{40,48},{48,56},{56,64},{64,7... | collective-permute-start | bytes 786440 | tf_op jit(solution)/shard_map/ppermute | solution.py:300
  56.2 7.1 %collective-permute-start.5 = (f32[8,64,128]{2,1,0:T(8,128)S(1)}, f32[8,64,128]{2,1,0:T(8,128)S(1)}, u32[]{:S(2)}, u32[]{:S(2)}) collective-permute-start(f32[8,64,128]{2,1,0:T(8,128)S(1)} %next_slices.4.x.more), channel_id=1, source_target_pairs={{0,504},{8,0},{16,8},{24,16},{32,24},{40,32},{48,40},{56,48},{64,5... | collective-permute-start | bytes 786440 | tf_op jit(solution)/shard_map/ppermute | solution.py:300
  58.1 10.4 %collective-permute-start.6 = (f32[8,64,128]{2,1,0:T(8,128)S(1)}, f32[8,64,128]{2,1,0:T(8,128)S(1)}, u32[]{:S(2)}, u32[]{:S(2)}) collective-permute-start(f32[8,64,128]{2,1,0:T(8,128)S(1)} %next_slices.4.x.more), channel_id=1, source_target_pairs={{0,8},{8,16},{16,24},{24,32},{32,40},{40,48},{48,56},{56,64},{64,7... | collective-permute-start | bytes 786440 | tf_op jit(solution)/shard_map/ppermute | solution.py:300
  69.5 7.1 %collective-permute-start.7 = (f32[8,64,128]{2,1,0:T(8,128)S(1)}, f32[8,64,128]{2,1,0:T(8,128)S(1)}, u32[]{:S(2)}, u32[]{:S(2)}) collective-permute-start(f32[8,64,128]{2,1,0:T(8,128)S(1)} %next_slices.5.x), channel_id=1, source_target_pairs={{0,504},{8,0},{16,8},{24,16},{32,24},{40,32},{48,40},{56,48},{64,5... | collective-permute-start | bytes 786440 | tf_op jit(solution)/shard_map/ppermute | solution.py:300
  71.5 10.4 %collective-permute-start.8 = (f32[8,64,128]{2,1,0:T(8,128)S(1)}, f32[8,64,128]{2,1,0:T(8,128)S(1)}, u32[]{:S(2)}, u32[]{:S(2)}) collective-permute-start(f32[8,64,128]{2,1,0:T(8,128)S(1)} %next_slices.5.x), channel_id=1, source_target_pairs={{0,8},{8,16},{16,24},{24,32},{32,40},{40,48},{48,56},{56,64},{64,7... | collective-permute-start | bytes 786440 | tf_op jit(solution)/shard_map/ppermute | solution.py:300
  83.6 22.5 %collective-permute-start.10 = (f32[8,64,128]{2,1,0:T(8,128)}, f32[8,64,128]{2,1,0:T(8,128)S(1)}, u32[]{:S(2)}, u32[]{:S(2)}) collective-permute-start(f32[8,64,128]{2,1,0:T(8,128)} %next_slices.6.x.more.own), channel_id=1, source_target_pairs={{0,8},{8,16},{16,24},{24,32},{32,40},{40,48},{48,56},{56,64},{64,7... | collective-permute-start | bytes 786440 | tf_op jit(solution)/shard_map/ppermute | solution.py:300
  85.5 25.8 %collective-permute-start.9 = (f32[8,64,128]{2,1,0:T(8,128)}, f32[8,64,128]{2,1,0:T(8,128)S(1)}, u32[]{:S(2)}, u32[]{:S(2)}) collective-permute-start(f32[8,64,128]{2,1,0:T(8,128)} %next_slices.6.x.more.own), channel_id=1, source_target_pairs={{0,504},{8,0},{16,8},{24,16},{32,24},{40,32},{48,40},{56,48},{64,5... | collective-permute-start | bytes 786440 | tf_op jit(solution)/shard_map/ppermute | solution.py:300
  92.2 20.4 %collective-permute-start.11 = (f32[8,64,128]{2,1,0:T(8,128)}, f32[8,64,128]{2,1,0:T(8,128)S(1)}, u32[]{:S(2)}, u32[]{:S(2)}) collective-permute-start(f32[8,64,128]{2,1,0:T(8,128)} %next_slices.6.x.more.own), channel_id=1, source_target_pairs={{6,0},{7,1},{0,2},{1,3},{2,4},{3,5},{4,6},{5,7},{14,8},{15,9},{8,1... | collective-permute-start | bytes 786440 | tf_op jit(solution)/shard_map/ppermute | solution.py:392
  95.3 17.3 %collective-permute-start.12 = (f32[8,64,128]{2,1,0:T(8,128)}, f32[8,64,128]{2,1,0:T(8,128)S(1)}, u32[]{:S(2)}, u32[]{:S(2)}) collective-permute-start(f32[8,64,128]{2,1,0:T(8,128)} %next_slices.6.x.more.own), channel_id=1, source_target_pairs={{3,0},{2,1},{5,2},{4,3},{7,4},{6,5},{1,6},{0,7},{11,8},{10,9},{13,... | collective-permute-start | bytes 786440 | tf_op jit(solution)/shard_map/ppermute | solution.py:392
  104.1 8.5 %collective-permute-start.13 = (f32[8,64,128]{2,1,0:T(8,128)}, f32[8,64,128]{2,1,0:T(8,128)S(1)}, u32[]{:S(2)}, u32[]{:S(2)}) collective-permute-start(f32[8,64,128]{2,1,0:T(8,128)} %next_slices.6.x.more.own), channel_id=1, source_target_pairs={{1,0},{0,1},{3,2},{2,3},{5,4},{4,5},{7,6},{6,7},{9,8},{8,9},{11,10... | collective-permute-start | bytes 786440 | tf_op jit(solution)/shard_map/ppermute | solution.py:392
  106.1 12.1 %collective-permute-start.14 = (f32[8,64,128]{2,1,0:T(8,128)}, f32[8,64,128]{2,1,0:T(8,128)S(1)}, u32[]{:S(2)}, u32[]{:S(2)}) collective-permute-start(f32[8,64,128]{2,1,0:T(8,128)} %next_slices.6.x.more.own), channel_id=1, source_target_pairs={{5,0},{4,1},{7,2},{6,3},{0,4},{1,5},{2,6},{3,7},{13,8},{12,9},{15,... | collective-permute-start | bytes 786440 | tf_op jit(solution)/shard_map/ppermute | solution.py:392
  120.0 317.4 %all-gather.4.cloned.1.call-start = ((), (), s32[]{:S(2)}) async-start(), calls=%async_computation.2 | async-start | bytes 1179648 | tf_op jit(solution)/shard_map/all_gather | solution.py:412
  434.4 1.6 copy-start.2
  437.4 1.2 copy-start.3
Sparse Core Ops, SparseCore 0:
  120.2 20.1 all-gather.5
  169.6 24.3 all-gather.3

commit v5 on v4

--- a/solution.py
+++ b/solution.py
@@ -13,6 +13,7 @@
 NEWTON_LIMIT = 12
 NEWTON_DONE = 1e-6
 VMEM_LIMIT = 44 * 1024 * 1024
+VMEM_WHOLE = 44 * 1024 * 1024
 
 f32 = jnp.float32
 bf16 = jnp.bfloat16
@@ -20,7 +21,16 @@
 SMEM_SPEC = pl.BlockSpec(memory_space=pltpu.SMEM)
 
 
-def call(kernel, out_shape, n_smem, n_vmem, scratch=(), flops=0, moved=0, name=None):
+def call(
+    kernel,
+    out_shape,
+    n_smem,
+    n_vmem,
+    scratch=(),
+    flops=0,
+    moved=0,
+    name=None,
+):
     return pl.pallas_call(
         kernel,
         out_shape=out_shape,
@@ -42,9 +52,14 @@
 NN = (((1,), (0,)), ((), ()))
 
 
-def left_operand(x):
-    high, low = split(x)
-    return jnp.concatenate([high, low, high], axis=1)
+def stacked(x):
+    return jnp.concatenate(split(x), axis=0)
+
+
+def three_products(parts, high, low):
+    m = parts.shape[0] // 2
+    both = jnp.dot(parts, high, preferred_element_type=f32)
+    return both[:m] + (both[m:] + jnp.dot(parts[:m], low, preferred_element_type=f32))
 
 
 def low_lanes(shape):
@@ -68,71 +83,61 @@
 def right_operand(block):
     turned = swapped(block)
     full = jnp.concatenate([block, jnp.where(low_lanes(block.shape), -turned, turned)], axis=0)
-    high, low = split(full * (1.0 / RADIUS))
-    return jnp.concatenate([high, high, low], axis=0)
-
-
-def backward_kernel(near, x, hop, out, hop_out):
+    return split(full * (1.0 / RADIUS))
+
+
+def backward_kernel(x, hop, out, high, low):
     for s in range(x.shape[0]):
-        block = hop[s, 0]
-        hop_out[s] = block
-        out[s] = jnp.dot(
-            left_operand(x[s]), right_operand(conjugated(block)), preferred_element_type=f32
-        )
-
-
-def prepare_kernel(near, diag, hop, own_ref, ahead_ref):
+        high[s], low[s] = right_operand(conjugated(hop[s, 0]))
+        out[s] = three_products(stacked(x[s]), high[s], low[s])
+
+
+def prepare_kernel(near, diag, hop, own_high, own_low, ahead_high, ahead_low):
     sites, half, wide = diag.shape
     rows = lax.broadcasted_iota(jnp.int32, (half, wide), 0)
     cols = lax.broadcasted_iota(jnp.int32, (half, wide), 1)
     unit = jnp.where(rows == cols, CENTER, 0.0)
     for s in range(sites):
-        parts = [right_operand(transposed(diag[s]) - unit)]
+        own_high[s, :wide], own_low[s, :wide] = right_operand(transposed(diag[s]) - unit)
         for d in range(3):
+            place = slice((1 + d) * wide, (2 + d) * wide)
             other = hop[lax.rem(near[s, 4 + d], sites), d]
-            parts.append(right_operand(transposed(hop[s, d]) + conjugated(other)))
-        own_ref[s] = jnp.concatenate(parts, axis=0)
-        ahead_ref[s] = right_operand(transposed(hop[s, 3]))
-
-
-def prepare_back_kernel(near, hop_back, back_ref):
-    sites = hop_back.shape[0]
-    for s in range(sites):
-        back_ref[s] = right_operand(conjugated(hop_back[lax.rem(near[s, 7], sites)]))
-
-
-def own_kernel(near, x, mats, out, spread):
+            own_high[s, place], own_low[s, place] = right_operand(
+                transposed(hop[s, d]) + conjugated(other)
+            )
+        ahead_high[s], ahead_low[s] = right_operand(transposed(hop[s, 3]))
+
+
+def own_kernel(near, x, high, low, out, spread):
     sites = x.shape[0]
     for n in range(sites):
-        spread[n] = left_operand(x[n])
+        spread[n] = stacked(x[n])
     for s in range(sites):
         index = [s] + [lax.rem(near[s, d], sites) for d in range(3)]
-        left = jnp.concatenate([spread[n] for n in index], axis=1)
-        out[s] = jnp.dot(left, mats[s], preferred_element_type=f32)
-
-
-def first_kernel(near, own, ahead, received, ahead_mats, out):
+        parts = jnp.concatenate([spread[n] for n in index], axis=1)
+        out[s] = three_products(parts, high[s], low[s])
+
+
+def step_kernel(mode, near, own, ahead, received, ahead_high, ahead_low, *rest):
     sites = own.shape[0]
+    more = rest[0] if mode != "first" else None
+    if mode == "image":
+        out, back = rest[-1], None
+    else:
+        back_high, back_low, out, back = rest[-4:]
     for s in range(sites):
-        left = left_operand(ahead[lax.rem(near[s, 3], sites)])
-        part = jnp.dot(left, ahead_mats[s], preferred_element_type=f32)
-        out[s] = own[s] + part + received[lax.rem(near[s, 7], sites)]
-
-
-def next_kernel(mode, near, own, ahead, behind, ahead_mats, back_mats, more, out):
-    sites = own.shape[0]
-    for s in range(sites):
-        left = left_operand(ahead[lax.rem(near[s, 3], sites)])
-        right = left_operand(behind[lax.rem(near[s, 7], sites)])
-        applied = own[s] + jnp.dot(
-            jnp.concatenate([left, right], axis=1),
-            jnp.concatenate([ahead_mats[s], back_mats[s]], axis=0),
-            preferred_element_type=f32,
-        )
-        if mode == "next":
+        parts = stacked(ahead[lax.rem(near[s, 3], sites)])
+        part = three_products(parts, ahead_high[s], ahead_low[s])
+        applied = own[s] + (part + received[lax.rem(near[s, 7], sites)])
+        if mode == "first":
+            out[s] = applied
+        elif mode == "next":
             out[s] = 2.0 * applied - more[s]
         else:
             out[s] = RADIUS * applied + CENTER * more[s]
+    if back is not None:
+        for s in range(sites):
+            back[s] = three_products(stacked(out[s]), back_high[s], back_low[s])
 
 
 def senders(devices):
@@ -213,7 +218,7 @@
     return dot(ah, bh) + (dot(al, bh) + dot(ah, bl))
 
 
-def inverse_kernel(count, gathered, out, scaled, factor, product):
+def inverse_kernel(count, gathered, out, scaled, factor):
     n = out.shape[0]
     half = gathered.shape[2] // 2
     for v, line in enumerate(lines_of(gathered)):
@@ -231,20 +236,59 @@
     scaled[...] = matrix
     factor[...] = unit - weight * (matrix - unit)
 
+    mid = n // 2
+    dot = functools.partial(lax.dot_general, preferred_element_type=f32)
+    square = (mid, mid)
+    r, c = (lax.broadcasted_iota(jnp.int32, square, i) for i in range(2))
+    small_weight = jnp.where(r > c, 1.0, jnp.where(r == c, 0.5, 0.0))
+    small_unit = jnp.where(r == c, 1.0, 0.0)
+
+    def improve(product, cut):
+        s1 = cut(scaled[:, :mid])
+        s2 = cut(scaled[:, mid:])
+        top = cut(factor[:mid, :mid])
+        side = cut(factor[mid:, :mid])
+        low = cut(factor[mid:, mid:])
+        lower = cut(factor[mid:, :])
+
+        def part(x, piece):
+            return tuple(y[piece] for y in x)
+
+        t11 = cut(product(top, part(s1, slice(0, mid)), NN))
+        t21 = cut(product(lower, s1, NN))
+        t22 = cut(product(lower, s2, NN))
+        e11 = product(t11, top, NT) - small_unit
+        e21 = product(t21, top, NT)
+        e22 = product(t21, side, NT) + product(t22, low, NT) - small_unit
+        p11, p22 = small_weight * e11, small_weight * e22
+        size = jnp.sum(p11 * p11 + p22 * p22 + e21 * e21)
+        p11, p21, p22 = cut(p11), cut(e21), cut(p22)
+        factor[:mid, :mid] = factor[:mid, :mid] - product(p11, top, NN)
+        factor[mid:, :mid] = factor[mid:, :mid] - (
+            product(p21, top, NN) + product(p22, side, NN)
+        )
+        factor[mid:, mid:] = factor[mid:, mid:] - product(p22, low, NN)
+        return size
+
+    def once(a, b, dims):
+        return dot(a[0], b[0], dimension_numbers=dims)
+
+    def thrice(a, b, dims):
+        (ah, al), (bh, bl) = a, b
+        return dot(ah, bh, dimension_numbers=dims) + (
+            dot(al, bh, dimension_numbers=dims) + dot(ah, bl, dimension_numbers=dims)
+        )
+
+    improve(once, lambda x: (x.astype(bf16),))
+
     def go_on(state):
         step, size = state
         return jnp.logical_and(step < NEWTON_LIMIT, jnp.logical_not(size < NEWTON_DONE))
 
-    def improve(state):
-        step, _ = state
-        current = factor[...]
-        product[...] = multiply(current, scaled[...], NN)
-        error = multiply(product[...], current, NT) - unit
-        size = jnp.sum(error * error)
-        factor[...] = current - multiply(weight * error, current, NN)
-        return step + 1, size
-
-    _, size = lax.while_loop(go_on, improve, (jnp.int32(0), jnp.float32(1.0)))
+    def body(state):
+        return state[0] + 1, improve(thrice, split)
+
+    _, size = lax.while_loop(go_on, body, (jnp.int32(0), jnp.float32(1.0)))
 
     @pl.when(jnp.logical_not(size < NEWTON_DONE))
     def _():
@@ -269,22 +313,15 @@
     out[...] = factor[...] * scale_row
 
 
-def basis_kernel(place, everything, inverse, out):
-    devices = everything.shape[0]
-    sites, cols, wide = out.shape
-    mine = inverse[pl.ds(pl.multiple_of(place[0] * cols, cols), cols), :]
-    right = jnp.concatenate(
-        [
-            jnp.concatenate(
-                [everything[u, s * cols : (s + 1) * cols] for s in range(sites)], axis=1
-            )
-            for u in range(devices)
-        ],
-        axis=0,
-    )
-    result = multiply(mine, right, NN)
+def basis_kernel(place, vectors, inverse, out):
+    sites, columns, _ = out.shape
+    mine = inverse[pl.ds(pl.multiple_of(place[0] * columns, columns), columns), :]
     for s in range(sites):
-        out[s] = result[:, s * wide : (s + 1) * wide]
+        block = jnp.concatenate(
+            [vectors[u, s * columns : (s + 1) * columns] for u in range(vectors.shape[0])],
+            axis=0,
+        )
+        out[s] = multiply(mine, block, NN)
 
 
 def projected_kernel(count, place, moments, inverse, out):
@@ -313,80 +350,73 @@
     size = sites * cols * both * 4
 
     def matrices(blocks):
-        return shape((sites, 3 * blocks * both, both), bf16)
+        return (shape((sites, blocks * both, both), bf16),) * 2
 
     def work(blocks):
         return sites * cols * blocks * 3 * both * both * 2
 
     current = jnp.swapaxes(start_basis, 1, 2)
-    ahead = passed_along(current, -1)
-    back, links = pl.pallas_call(
+    back, *back_mats = pl.pallas_call(
         backward_kernel,
-        out_shape=(block, shape((sites, half, both), f32)),
+        out_shape=(block, *matrices(1)),
         grid=(1,),
         in_specs=[
-            SMEM_SPEC,
             pl.BlockSpec((sites, cols, both), lambda i: (0, 0, 0)),
             pl.BlockSpec((sites, 1, half, both), lambda i: (0, 3, 0, 0)),
         ],
         out_specs=(
             pl.BlockSpec((sites, cols, both), lambda i: (0, 0, 0)),
-            pl.BlockSpec((sites, half, both), lambda i: (0, 0, 0)),
+            *[pl.BlockSpec((sites, both, both), lambda i: (0, 0, 0))] * 2,
         ),
-        compiler_params=pltpu.CompilerParams(vmem_limit_bytes=VMEM_LIMIT),
+        compiler_params=pltpu.CompilerParams(vmem_limit_bytes=VMEM_WHOLE),
         cost_estimate=pl.CostEstimate(
             flops=work(1), bytes_accessed=4 * size, transcendentals=0
         ),
         name="backward",
-    )(neighbors, current, hop_blocks)
-    received = passed_along(back, 1)
-    links_back = passed_along(links, 1)
-    own_mats, ahead_mats = call(
+    )(current, hop_blocks)
+    mats = call(
         prepare_kernel,
-        (matrices(4), matrices(1)),
+        (*matrices(4), *matrices(1)),
         1,
         2,
         flops=1 << 24,
         moved=1 << 23,
         name="prepare",
     )(neighbors, diag_blocks, hop_blocks)
-    back_mats = call(
-        prepare_back_kernel, matrices(1), 1, 1, flops=1 << 22, moved=1 << 21, name="prepare_back"
-    )(neighbors, links_back)
-
-    def own_part(vectors):
-        return call(
+    own_mats, ahead_mats = mats[:2], mats[2:]
+
+    def apply(vectors, back, mode, *more):
+        ahead = passed_along(vectors, -1)
+        received = passed_along(back, 1)
+        own = call(
             own_kernel,
             block,
             1,
-            2,
-            scratch=[pltpu.VMEM((sites, cols, 3 * both), bf16)],
+            3,
+            scratch=[pltpu.VMEM((sites, 2 * cols, both), bf16)],
             flops=work(4),
             moved=8 * size,
             name="own_slice",
-        )(neighbors, vectors, own_mats)
-
-    def apply(vectors, mode, more):
-        ahead = passed_along(vectors, -1)
-        behind = passed_along(vectors, 1)
+        )(neighbors, vectors, *own_mats)
+        if mode != "image":
+            more = (*more, *back_mats)
         return call(
-            functools.partial(next_kernel, mode),
-            block,
+            functools.partial(step_kernel, mode),
+            block if mode == "image" else (block, block),
             1,
-            6,
-            flops=work(2),
+            5 + len(more),
+            flops=work(1),
             moved=8 * size,
             name="next_slices",
-        )(neighbors, own_part(vectors), ahead, behind, ahead_mats, back_mats, more)
+        )(neighbors, own, ahead, received, *ahead_mats, *more)
 
     previous = current
-    current = call(first_kernel, block, 1, 4, flops=work(1), moved=6 * size, name="first_step")(
-        neighbors, own_part(current), ahead, received, ahead_mats
-    )
+    current, back = apply(current, back, "first")
     for _ in range(DEGREE - 1):
-        previous, current = current, apply(current, "next", previous)
-
-    image = apply(current, "image", current)
+        following, back = apply(current, back, "next", previous)
+        previous, current = current, following
+
+    image = apply(current, back, "image", current)
     table = senders(devices)
     others = [
         lax.ppermute(current, "vec", [(table[v][i], v) for v in range(devices)]) for i in range(4)
@@ -409,6 +439,7 @@
         sum_kernel, shape((slices, 8, both), f32), 0, 1, moved=1 << 19, name="sum_parts"
     )(parts)
     whole = lax.all_to_all(summed, "site", 0, 0, tiled=True).reshape(slices * 8, both)
+    whole, everything = lax.optimization_barrier((whole, everything))
     moments = lax.all_gather(whole[kept : kept + all_cols // 2], "vec", axis=0)
     gram = lax.all_gather(whole[:kept], "vec", axis=0)
 
@@ -417,7 +448,7 @@
         shape((all_cols, all_cols), f32),
         0,
         1,
-        scratch=[pltpu.VMEM((all_cols, all_cols), f32)] * 3,
+        scratch=[pltpu.VMEM((all_cols, all_cols), f32)] * 2,
         flops=9 * 6 * all_cols**3,
         moved=1 << 21,
         name="inverse_factor",

time: 449 us -> 430 us (0.958)
  Pallas kernels: 272 us -> 259 us
  starting transfers between devices: 63.4 us -> 56.8 us
    pallas_call x1, Pallas kernels: 248 us -> 236 us  [local(): call(functools.partial(inverse_kernel, count), shape((all_cols, all_cols)...]
    ppermute x11 -> x10, starting transfers between devices: 46 us -> 39.1 us  [passed_along(): return lax.ppermute(x, 'site', [(i, (i + by) % size) for i in range(size)])]
    pallas_call x13 -> x12, Pallas kernels: 18.9 us -> 17.5 us  [the longest x5 6.68 us: apply(): call(own_kernel, block, 1, 3, scratch=[pltpu.VMEM((sites, 2 * cols, both)...]
    ppermute x11 -> x10, waiting for transfers between devices: 18.9 us -> 19.8 us  [passed_along(): return lax.ppermute(x, 'site', [(i, (i + by) % size) for i in range(size)])]
  transfers between devices with their start and end apart: 17 -> 16, of which waited for: 7 -> 7; matrix products, arithmetic and copies ran while one was open for 0% -> 0% of each run, Pallas kernels for 59% -> 58%
where the time goes in v5:
time: 430 us; the launch traced here: 429 us
  Pallas kernels  259 us (60%)
  blocking collectives  67 us (16%)
  starting transfers between devices  56.8 us (13%)
  waiting for transfers between devices  25.7 us (6%)
  between operations  14.3 us (3%)
  local copies, waits for them, and re-layouts  5.98 us (1%)
    pallas_call x1, Pallas kernels, local(): call(functools.partial(inverse_kernel, count), shape((all_cols, all_cols)...  236 us
    ppermute x10, starting transfers between devices, passed_along(): return lax.ppermute(x, 'site', [(i, (i + by) % size) for i in range(size)])  39.1 us
    all_to_all x1, blocking collectives, local(): lax.all_to_all(summed, 'site', 0, 0, tiled=True).reshape(slices * 8, both)  25 us
    all_to_all x1, blocking collectives, local(): lax.all_to_all(products.reshape(slices, 8, both), 'site', 0, 0, tiled=True)  25 us
    ppermute x10, waiting for transfers between devices, passed_along(): return lax.ppermute(x, 'site', [(i, (i + by) % size) for i in range(size)])  19.8 us
    ppermute x4, starting transfers between devices, local(): lax.ppermute(current, 'vec', [(table[v][i], v) for v in range(devices)])  17.6 us
    all_gather x1, blocking collectives, local(): gram = lax.all_gather(whole[:kept], 'vec', axis=0)  17.1 us
  transfers between devices with their start and end apart: 16, of which 7 were waited for; matrix products, arithmetic and copies ran while one was open for 0% of the time, Pallas kernels for 58%

profile of v5, /device:TPU:1, one launch (start us, length us, event | category | flops | bytes accessed | tf_op | source)
XLA Modules:
  0.0 429.1 jit_solution(7057416624102887412)
XLA Ops:
  8.4 1.3 backward.1
  9.8 4.4 %collective-permute-start.1 = (f32[8,64,128]{2,1,0:T(8,128)S(1)}, f32[8,64,128]{2,1,0:T(8,128)S(1)}, u32[]{:S(2)}, u32[]{:S(2)}) collective-permute-start(f32[8,64,128]{2,1,0:T(8,128)S(1)} %get-tuple-element.22), channel_id=1, source_target_pairs={{0,8},{8,16},{16,24},{24,32},{32,40},{40,48},{48,56},{56,64},{64,7... | collective-permute-start | bytes 786440 | tf_op jit(solution)/shard_map/ppermute | solution.py:337
  14.1 11.9 %collective-permute-start = (f32[8,64,128]{2,1,0:T(8,128)}, f32[8,64,128]{2,1,0:T(8,128)S(1)}, u32[]{:S(2)}, u32[]{:S(2)}) collective-permute-start(f32[8,64,128]{2,1,0:T(8,128)} %bitcast.1.x.rest_0_), channel_id=1, source_target_pairs={{0,504},{8,0},{16,8},{24,16},{32,24},{40,32},{48,40},{56,48},{64,5... | collective-permute-start | bytes 786440 | tf_op jit(solution)/shard_map/ppermute | solution.py:337
  29.0 3.1 prepare.1
  32.1 1.6 own_slice.5.own
  34.7 5.0 %collective-permute-start.2 = (f32[8,64,128]{2,1,0:T(8,128)S(1)}, f32[8,64,128]{2,1,0:T(8,128)S(1)}, u32[]{:S(2)}, u32[]{:S(2)}) collective-permute-start(f32[8,64,128]{2,1,0:T(8,128)S(1)} %get-tuple-element.27.x.rest_0_), channel_id=1, source_target_pairs={{0,504},{8,0},{16,8},{24,16},{32,24},{40,32},{48,40},{56,48},{64,5... | collective-permute-start | bytes 786440 | tf_op jit(solution)/shard_map/ppermute | solution.py:337
  39.7 1.9 collective-permute-start.3
  43.8 7.2 %collective-permute-done.3.received = f32[8,64,128]{2,1,0:T(8,128)S(1)} collective-permute-done((f32[8,64,128]{2,1,0:T(8,128)S(1)}, f32[8,64,128]{2,1,0:T(8,128)S(1)}, u32[]{:S(2)}, u32[]{:S(2)}) %collective-permute-start.3) | collective-permute-done | bytes 262176 | tf_op jit(solution)/shard_map/ppermute | solution.py:337
  50.9 1.4 next_slices.6
  52.3 1.9 collective-permute-start.4
  54.3 3.4 collective-permute-start.5
  59.5 5.2 %collective-permute-done.5.received = f32[8,64,128]{2,1,0:T(8,128)S(1)} collective-permute-done((f32[8,64,128]{2,1,0:T(8,128)S(1)}, f32[8,64,128]{2,1,0:T(8,128)S(1)}, u32[]{:S(2)}, u32[]{:S(2)}) %collective-permute-start.5) | collective-permute-done | bytes 262176 | tf_op jit(solution)/shard_map/ppermute | solution.py:337
  65.8 1.9 collective-permute-start.6
  67.7 3.4 collective-permute-start.7
  72.9 5.2 %collective-permute-done.7.received = f32[8,64,128]{2,1,0:T(8,128)S(1)} collective-permute-done((f32[8,64,128]{2,1,0:T(8,128)S(1)}, f32[8,64,128]{2,1,0:T(8,128)S(1)}, u32[]{:S(2)}, u32[]{:S(2)}) %collective-permute-start.7) | collective-permute-done | bytes 262176 | tf_op jit(solution)/shard_map/ppermute | solution.py:337
  78.1 1.6 next_slices.8
  79.8 1.9 collective-permute-start.8
  81.7 3.4 collective-permute-start.9
  85.0 3.1 collective-permute-start.10
  88.2 9.1 %collective-permute-start.11 = (f32[8,64,128]{2,1,0:T(8,128)}, f32[8,64,128]{2,1,0:T(8,128)S(1)}, u32[]{:S(2)}, u32[]{:S(2)}) collective-permute-start(f32[8,64,128]{2,1,0:T(8,128)} %get-tuple-element.33.x.rest_0_.own), channel_id=1, source_target_pairs={{3,0},{2,1},{5,2},{4,3},{7,4},{6,5},{1,6},{0,7},{11,8},{10,9},{13,... | collective-permute-start | bytes 786440 | tf_op jit(solution)/shard_map/ppermute | solution.py:422
  97.3 1.9 collective-permute-start.12
  99.3 3.4 collective-permute-start.13
  102.7 1.6 own_slice.9.own
  104.3 1.3 next_slices.9.image
  105.6 5.8 %collective-permute-done.13.fourth = f32[8,64,128]{2,1,0:T(8,128)S(1)} collective-permute-done((f32[8,64,128]{2,1,0:T(8,128)}, f32[8,64,128]{2,1,0:T(8,128)S(1)}, u32[]{:S(2)}, u32[]{:S(2)}) %collective-permute-start.13) | collective-permute-done | bytes 262176 | tf_op jit(solution)/shard_map/ppermute | solution.py:422
  111.4 1.8 products.1
  113.3 25.0 %all_to_all.10.parts = f32[64,8,128]{2,1,0:T(8,128)S(1)} all-to-all(f32[64,8,128]{2,1,0:T(8,128)S(1)} %bitcast.12), channel_id=1, replica_groups=mesh['site'=64,'vec'=8] {'site'}, dimensions={0} | all-to-all | bytes 524288 | tf_op jit(solution)/shard_map/all_to_all | solution.py:437
  138.3 25.0 %all_to_all.11 = f32[64,8,128]{2,1,0:T(8,128)S(1)} all-to-all(f32[64,8,128]{2,1,0:T(8,128)S(1)} %sum_parts.1), channel_id=1, replica_groups=mesh['site'=64,'vec'=8] {'site'}, dimensions={0} | all-to-all | bytes 524288 | tf_op jit(solution)/shard_map/all_to_all | solution.py:441
  164.0 17.1 %all-gather.1 = f32[1280,128]{1,0:T(8,128)S(1)} all-gather(f32[160,128]{1,0:T(8,128)S(1)} %slice.6), channel_id=3, replica_groups=mesh['site'=64,'vec'=8] {'vec'}, dimensions={0}, use_global_device_ids=true | all-gather | bytes 737280 | tf_op jit(solution)/shard_map/all_gather | solution.py:444
  181.1 236.5 %inverse_factor.1.inverse = f32[512,512]{1,0:T(8,128)S(1)} custom-call(f32[8,160,128]{2,1,0:T(8,128)S(1)} %bitcast.13), custom_call_target="tpu_custom_call" | custom-call | flops 7247757312 | bytes 2097152 | tf_op jit(solution)/shard_map/inverse_factor/pallas_call | solution.py:446
  417.6 1.3 basis.1
  420.1 2.2 projected.1
  (36 shorter events, 14.0 us)
Async XLA Ops:
  7.2 156.1 %all-gather.6.cloned.1.call-start = ((), (), s32[]{:S(2)}) async-start(), calls=%async_computation.2 | async-start | bytes 2359296 | tf_op jit(solution)/shard_map/all_gather | solution.py:435
  7.2 1.2 copy-start
  9.8 23.9 %collective-permute-start.1 = (f32[8,64,128]{2,1,0:T(8,128)S(1)}, f32[8,64,128]{2,1,0:T(8,128)S(1)}, u32[]{:S(2)}, u32[]{:S(2)}) collective-permute-start(f32[8,64,128]{2,1,0:T(8,128)S(1)} %get-tuple-element.22), channel_id=1, source_target_pairs={{0,8},{8,16},{16,24},{24,32},{32,40},{40,48},{48,56},{56,64},{64,7... | collective-permute-start | bytes 786440 | tf_op jit(solution)/shard_map/ppermute | solution.py:337
  14.1 19.5 %collective-permute-start = (f32[8,64,128]{2,1,0:T(8,128)}, f32[8,64,128]{2,1,0:T(8,128)S(1)}, u32[]{:S(2)}, u32[]{:S(2)}) collective-permute-start(f32[8,64,128]{2,1,0:T(8,128)} %bitcast.1.x.rest_0_), channel_id=1, source_target_pairs={{0,504},{8,0},{16,8},{24,16},{32,24},{40,32},{48,40},{56,48},{64,5... | collective-permute-start | bytes 786440 | tf_op jit(solution)/shard_map/ppermute | solution.py:337
  26.1 1.2 copy-start.1
  27.3 0.7 copy-start.4
  28.0 0.9 copy-start.5
  34.7 9.1 %collective-permute-start.2 = (f32[8,64,128]{2,1,0:T(8,128)S(1)}, f32[8,64,128]{2,1,0:T(8,128)S(1)}, u32[]{:S(2)}, u32[]{:S(2)}) collective-permute-start(f32[8,64,128]{2,1,0:T(8,128)S(1)} %get-tuple-element.27.x.rest_0_), channel_id=1, source_target_pairs={{0,504},{8,0},{16,8},{24,16},{32,24},{40,32},{48,40},{56,48},{64,5... | collective-permute-start | bytes 786440 | tf_op jit(solution)/shard_map/ppermute | solution.py:337
  39.7 11.2 %collective-permute-start.3 = (f32[8,64,128]{2,1,0:T(8,128)S(1)}, f32[8,64,128]{2,1,0:T(8,128)S(1)}, u32[]{:S(2)}, u32[]{:S(2)}) collective-permute-start(f32[8,64,128]{2,1,0:T(8,128)S(1)} %get-tuple-element.28), channel_id=1, source_target_pairs={{0,8},{8,16},{16,24},{24,32},{32,40},{40,48},{48,56},{56,64},{64,7... | collective-permute-start | bytes 786440 | tf_op jit(solution)/shard_map/ppermute | solution.py:337
  52.3 7.1 %collective-permute-start.4 = (f32[8,64,128]{2,1,0:T(8,128)S(1)}, f32[8,64,128]{2,1,0:T(8,128)S(1)}, u32[]{:S(2)}, u32[]{:S(2)}) collective-permute-start(f32[8,64,128]{2,1,0:T(8,128)S(1)} %get-tuple-element.29.x.rest_0_), channel_id=1, source_target_pairs={{0,504},{8,0},{16,8},{24,16},{32,24},{40,32},{48,40},{56,48},{64,5... | collective-permute-start | bytes 786440 | tf_op jit(solution)/shard_map/ppermute | solution.py:337
  54.3 10.4 %collective-permute-start.5 = (f32[8,64,128]{2,1,0:T(8,128)S(1)}, f32[8,64,128]{2,1,0:T(8,128)S(1)}, u32[]{:S(2)}, u32[]{:S(2)}) collective-permute-start(f32[8,64,128]{2,1,0:T(8,128)S(1)} %get-tuple-element.30), channel_id=1, source_target_pairs={{0,8},{8,16},{16,24},{24,32},{32,40},{40,48},{48,56},{56,64},{64,7... | collective-permute-start | bytes 786440 | tf_op jit(solution)/shard_map/ppermute | solution.py:337
  65.8 7.1 %collective-permute-start.6 = (f32[8,64,128]{2,1,0:T(8,128)S(1)}, f32[8,64,128]{2,1,0:T(8,128)S(1)}, u32[]{:S(2)}, u32[]{:S(2)}) collective-permute-start(f32[8,64,128]{2,1,0:T(8,128)S(1)} %get-tuple-element.31.x), channel_id=1, source_target_pairs={{0,504},{8,0},{16,8},{24,16},{32,24},{40,32},{48,40},{56,48},{64,5... | collective-permute-start | bytes 786440 | tf_op jit(solution)/shard_map/ppermute | solution.py:337
  67.7 10.4 %collective-permute-start.7 = (f32[8,64,128]{2,1,0:T(8,128)S(1)}, f32[8,64,128]{2,1,0:T(8,128)S(1)}, u32[]{:S(2)}, u32[]{:S(2)}) collective-permute-start(f32[8,64,128]{2,1,0:T(8,128)S(1)} %get-tuple-element.32), channel_id=1, source_target_pairs={{0,8},{8,16},{16,24},{24,32},{32,40},{40,48},{48,56},{56,64},{64,7... | collective-permute-start | bytes 786440 | tf_op jit(solution)/shard_map/ppermute | solution.py:337
  79.8 19.5 %collective-permute-start.8 = (f32[8,64,128]{2,1,0:T(8,128)}, f32[8,64,128]{2,1,0:T(8,128)S(1)}, u32[]{:S(2)}, u32[]{:S(2)}) collective-permute-start(f32[8,64,128]{2,1,0:T(8,128)} %get-tuple-element.33.x.rest_0_.own), channel_id=1, source_target_pairs={{0,504},{8,0},{16,8},{24,16},{32,24},{40,32},{48,40},{56,48},{64,5... | collective-permute-start | bytes 786440 | tf_op jit(solution)/shard_map/ppermute | solution.py:337
  81.7 22.6 %collective-permute-start.9 = (f32[8,64,128]{2,1,0:T(8,128)S(1)}, f32[8,64,128]{2,1,0:T(8,128)S(1)}, u32[]{:S(2)}, u32[]{:S(2)}) collective-permute-start(f32[8,64,128]{2,1,0:T(8,128)S(1)} %get-tuple-element.34), channel_id=1, source_target_pairs={{0,8},{8,16},{16,24},{24,32},{32,40},{40,48},{48,56},{56,64},{64,7... | collective-permute-start | bytes 786440 | tf_op jit(solution)/shard_map/ppermute | solution.py:337
  85.0 20.5 %collective-permute-start.10 = (f32[8,64,128]{2,1,0:T(8,128)}, f32[8,64,128]{2,1,0:T(8,128)S(1)}, u32[]{:S(2)}, u32[]{:S(2)}) collective-permute-start(f32[8,64,128]{2,1,0:T(8,128)} %get-tuple-element.33.x.rest_0_.own), channel_id=1, source_target_pairs={{6,0},{7,1},{0,2},{1,3},{2,4},{3,5},{4,6},{5,7},{14,8},{15,9},{8,1... | collective-permute-start | bytes 786440 | tf_op jit(solution)/shard_map/ppermute | solution.py:422
  88.2 17.4 %collective-permute-start.11 = (f32[8,64,128]{2,1,0:T(8,128)}, f32[8,64,128]{2,1,0:T(8,128)S(1)}, u32[]{:S(2)}, u32[]{:S(2)}) collective-permute-start(f32[8,64,128]{2,1,0:T(8,128)} %get-tuple-element.33.x.rest_0_.own), channel_id=1, source_target_pairs={{3,0},{2,1},{5,2},{4,3},{7,4},{6,5},{1,6},{0,7},{11,8},{10,9},{13,... | collective-permute-start | bytes 786440 | tf_op jit(solution)/shard_map/ppermute | solution.py:422
  97.3 8.2 %collective-permute-start.12 = (f32[8,64,128]{2,1,0:T(8,128)}, f32[8,64,128]{2,1,0:T(8,128)S(1)}, u32[]{:S(2)}, u32[]{:S(2)}) collective-permute-start(f32[8,64,128]{2,1,0:T(8,128)} %get-tuple-element.33.x.rest_0_.own), channel_id=1, source_target_pairs={{1,0},{0,1},{3,2},{2,3},{5,4},{4,5},{7,6},{6,7},{9,8},{8,9},{11,10... | collective-permute-start | bytes 786440 | tf_op jit(solution)/shard_map/ppermute | solution.py:422
  99.3 12.1 %collective-permute-start.13 = (f32[8,64,128]{2,1,0:T(8,128)}, f32[8,64,128]{2,1,0:T(8,128)S(1)}, u32[]{:S(2)}, u32[]{:S(2)}) collective-permute-start(f32[8,64,128]{2,1,0:T(8,128)} %get-tuple-element.33.x.rest_0_.own), channel_id=1, source_target_pairs={{5,0},{4,1},{7,2},{6,3},{0,4},{1,5},{2,6},{3,7},{13,8},{12,9},{15,... | collective-permute-start | bytes 786440 | tf_op jit(solution)/shard_map/ppermute | solution.py:422
  113.2 305.7 %all-gather.8.cloned.1.call-start = ((), (), s32[]{:S(2)}) async-start(), calls=%async_computation.3 | async-start | bytes 1179648 | tf_op jit(solution)/shard_map/all_gather | solution.py:443
  181.1 236.5 %copy-start.2 = (f32[4096,128]{1,0:T(8,128)S(1)}, f32[4096,128]{1,0:T(8,128)}, u32[]{:S(2)}) copy-start(f32[4096,128]{1,0:T(8,128)} %all-gather.6.cloned.1.call-done) | copy-start | bytes 6291460
  418.9 1.2 copy-start.3
Sparse Core Ops, SparseCore 0:
  113.3 22.8 all-gather.5
  164.1 24.2 all-gather.7

commit v6 on v5

--- a/solution.py
+++ b/solution.py
@@ -48,6 +48,11 @@
     return high, (x - high.astype(f32)).astype(bf16)
 
 
+def repeat_kernel(x, out):
+    for i in range(out.shape[0]):
+        out[i] = x[: out.shape[1]]
+
+
 NT = (((1,), (1,)), ((), ()))
 NN = (((1,), (0,)), ((), ()))
 
@@ -181,17 +186,19 @@
     out[10 * half :] = jnp.zeros((out.shape[0] - 10 * half, wide), f32)
 
 
-def lines_of(gathered):
+def lines_of(gathered, which):
     devices, _, wide = gathered.shape
     half = wide // 2
+    at = which * 5 * half // 2
     blocks = {}
     for v, others in enumerate(senders(devices)):
         for j, u in enumerate([v, *others]):
             if j < 4:
-                rows = gathered[v, (j // 2) * half : (j // 2 + 1) * half]
+                start = at + (j // 2) * half
+                rows = gathered[v, start : start + half]
                 block = rows[:, (j % 2) * half : (j % 2 + 1) * half]
             else:
-                rows = gathered[v, wide : wide + half // 2]
+                rows = gathered[v, at + wide : at + wide + half // 2]
                 block = jnp.concatenate([rows[:, :half], rows[:, half:]], axis=0)
             blocks[v, u] = block
     for v in range(devices):
@@ -221,7 +228,7 @@
 def inverse_kernel(count, gathered, out, scaled, factor):
     n = out.shape[0]
     half = gathered.shape[2] // 2
-    for v, line in enumerate(lines_of(gathered)):
+    for v, line in enumerate(lines_of(gathered, 0)):
         scaled[v * half : (v + 1) * half, :] = line * (1.0 / count)
     rows = lax.broadcasted_iota(jnp.int32, (n, n), 0)
     cols = lax.broadcasted_iota(jnp.int32, (n, n), 1)
@@ -324,9 +331,9 @@
         out[s] = multiply(mine, block, NN)
 
 
-def projected_kernel(count, place, moments, inverse, out):
-    half = moments.shape[2] // 2
-    moment = jnp.concatenate(lines_of(moments), axis=0)
+def projected_kernel(count, place, gathered, inverse, out):
+    half = gathered.shape[2] // 2
+    moment = jnp.concatenate(lines_of(gathered, 1), axis=0)
     mine = inverse[pl.ds(pl.multiple_of(place[0] * half, half), half), :]
     half_way = multiply(mine, moment, NN)
     out[...] = multiply(half_way, inverse[...], NT) * (1.0 / count)
@@ -439,9 +446,16 @@
         sum_kernel, shape((slices, 8, both), f32), 0, 1, moved=1 << 19, name="sum_parts"
     )(parts)
     whole = lax.all_to_all(summed, "site", 0, 0, tiled=True).reshape(slices * 8, both)
-    whole, everything = lax.optimization_barrier((whole, everything))
-    moments = lax.all_gather(whole[kept : kept + all_cols // 2], "vec", axis=0)
-    gram = lax.all_gather(whole[:kept], "vec", axis=0)
+    copies = call(
+        repeat_kernel,
+        shape((devices, 2 * kept, both), f32),
+        0,
+        1,
+        moved=1 << 21,
+        name="repeat",
+    )(whole)
+    copies, everything = lax.optimization_barrier((copies, everything))
+    gathered = lax.all_to_all(copies, "vec", 0, 0, tiled=True)
 
     inverse = call(
         functools.partial(inverse_kernel, count),
@@ -452,7 +466,7 @@
         flops=9 * 6 * all_cols**3,
         moved=1 << 21,
         name="inverse_factor",
-    )(gram)
+    )(gathered)
     basis = call(
         basis_kernel,
         block,
@@ -470,7 +484,7 @@
         flops=12 * all_cols * all_cols * cols,
         moved=1 << 22,
         name="projected",
-    )(place, moments, inverse)
+    )(place, gathered, inverse)
     return jnp.swapaxes(basis, 1, 2), projected.T
 
 

time: 430 us -> 437 us (1.016)
  waiting for transfers between devices: 25.7 us -> 43.6 us
  blocking collectives: 67 us -> 49.9 us
  starting transfers between devices: 56.8 us -> 66.1 us
    all_to_all x0 -> x1, waiting for transfers between devices: none -> 17.9 us  [local(): gathered = lax.all_to_all(copies, 'vec', 0, 0, tiled=True)]
    all_gather x1 -> x0, blocking collectives: 17.1 us -> none  [local(): gram = lax.all_gather(whole[:kept], 'vec', axis=0)]
    all_to_all x0 -> x1, starting transfers between devices: none -> 7.26 us  [local(): gathered = lax.all_to_all(copies, 'vec', 0, 0, tiled=True)]
  transfers between devices with their start and end apart: 16 -> 16, of which waited for: 7 -> 8; matrix products, arithmetic and copies ran while one was open for 0% -> 0% of each run, Pallas kernels for 58% -> 3%
where the time goes in v6:
time: 437 us; the launch traced here: 436 us
  Pallas kernels  259 us (59%)
  starting transfers between devices  66.1 us (15%)
  blocking collectives  49.9 us (11%)
  waiting for transfers between devices  43.6 us (10%)
  between operations  14.3 us (3%)
    pallas_call x1, Pallas kernels, local(): call(functools.partial(inverse_kernel, count), shape((all_cols, all_cols)...  236 us
    ppermute x10, starting transfers between devices, passed_along(): return lax.ppermute(x, 'site', [(i, (i + by) % size) for i in range(size)])  41.1 us
    all_to_all x1, blocking collectives, local(): lax.all_to_all(summed, 'site', 0, 0, tiled=True).reshape(slices * 8, both)  25 us
    all_to_all x1, blocking collectives, local(): lax.all_to_all(products.reshape(slices, 8, both), 'site', 0, 0, tiled=True)  25 us
    ppermute x10, waiting for transfers between devices, passed_along(): return lax.ppermute(x, 'site', [(i, (i + by) % size) for i in range(size)])  19.8 us
    all_to_all x1, waiting for transfers between devices, local(): gathered = lax.all_to_all(copies, 'vec', 0, 0, tiled=True)  17.9 us
    ppermute x4, starting transfers between devices, local(): lax.ppermute(current, 'vec', [(table[v][i], v) for v in range(devices)])  17.6 us
  transfers between devices with their start and end apart: 16, of which 8 were waited for; matrix products, arithmetic and copies ran while one was open for 0% of the time, Pallas kernels for 3%

profile of v6, /device:TPU:1, one launch (start us, length us, event | category | flops | bytes accessed | tf_op | source)
XLA Modules:
  0.0 435.9 jit_solution(2938758272022145538)
XLA Ops:
  7.2 1.2 copy-done
  9.8 4.4 %collective-permute-start.1 = (f32[8,64,128]{2,1,0:T(8,128)S(1)}, f32[8,64,128]{2,1,0:T(8,128)S(1)}, u32[]{:S(2)}, u32[]{:S(2)}) collective-permute-start(f32[8,64,128]{2,1,0:T(8,128)S(1)} %get-tuple-element.22), channel_id=1, source_target_pairs={{0,8},{8,16},{16,24},{24,32},{32,40},{40,48},{48,56},{56,64},{64,7... | collective-permute-start | bytes 786440 | tf_op jit(solution)/shard_map/ppermute | solution.py:344
  14.1 11.9 %collective-permute-start = (f32[8,64,128]{2,1,0:T(8,128)S(1)}, f32[8,64,128]{2,1,0:T(8,128)S(1)}, u32[]{:S(2)}, u32[]{:S(2)}) collective-permute-start(f32[8,64,128]{2,1,0:T(8,128)S(1)} %bitcast.9), channel_id=1, source_target_pairs={{0,504},{8,0},{16,8},{24,16},{32,24},{40,32},{48,40},{56,48},{64,5... | collective-permute-start | bytes 786440 | tf_op jit(solution)/shard_map/ppermute | solution.py:344
  27.1 3.1 prepare.1
  30.2 1.2 own_slice.5.own
  32.5 7.1 %collective-permute-start.2 = (f32[8,64,128]{2,1,0:T(8,128)S(1)}, f32[8,64,128]{2,1,0:T(8,128)S(1)}, u32[]{:S(2)}, u32[]{:S(2)}) collective-permute-start(f32[8,64,128]{2,1,0:T(8,128)S(1)} %get-tuple-element.27.x.rest_0_), channel_id=1, source_target_pairs={{0,504},{8,0},{16,8},{24,16},{32,24},{40,32},{48,40},{56,48},{64,5... | collective-permute-start | bytes 786440 | tf_op jit(solution)/shard_map/ppermute | solution.py:344
  39.5 1.9 collective-permute-start.3
  43.5 7.2 %collective-permute-done.3.received = f32[8,64,128]{2,1,0:T(8,128)S(1)} collective-permute-done((f32[8,64,128]{2,1,0:T(8,128)S(1)}, f32[8,64,128]{2,1,0:T(8,128)S(1)}, u32[]{:S(2)}, u32[]{:S(2)}) %collective-permute-start.3) | collective-permute-done | bytes 262176 | tf_op jit(solution)/shard_map/ppermute | solution.py:344
  51.8 1.9 collective-permute-start.4
  53.7 3.4 collective-permute-start.5
  58.9 5.2 %collective-permute-done.5.received = f32[8,64,128]{2,1,0:T(8,128)S(1)} collective-permute-done((f32[8,64,128]{2,1,0:T(8,128)S(1)}, f32[8,64,128]{2,1,0:T(8,128)S(1)}, u32[]{:S(2)}, u32[]{:S(2)}) %collective-permute-start.5) | collective-permute-done | bytes 262176 | tf_op jit(solution)/shard_map/ppermute | solution.py:344
  65.2 1.9 collective-permute-start.6
  67.1 3.4 collective-permute-start.7
  72.3 5.2 %collective-permute-done.7.received = f32[8,64,128]{2,1,0:T(8,128)S(1)} collective-permute-done((f32[8,64,128]{2,1,0:T(8,128)S(1)}, f32[8,64,128]{2,1,0:T(8,128)S(1)}, u32[]{:S(2)}, u32[]{:S(2)}) %collective-permute-start.7) | collective-permute-done | bytes 262176 | tf_op jit(solution)/shard_map/ppermute | solution.py:344
  77.6 1.6 next_slices.8
  79.2 1.9 collective-permute-start.8
  81.1 3.4 collective-permute-start.9
  84.5 3.1 collective-permute-start.10
  87.6 9.1 %collective-permute-start.11 = (f32[8,64,128]{2,1,0:T(8,128)}, f32[8,64,128]{2,1,0:T(8,128)S(1)}, u32[]{:S(2)}, u32[]{:S(2)}) collective-permute-start(f32[8,64,128]{2,1,0:T(8,128)} %get-tuple-element.33.x.rest_0_.own), channel_id=1, source_target_pairs={{3,0},{2,1},{5,2},{4,3},{7,4},{6,5},{1,6},{0,7},{11,8},{10,9},{13,... | collective-permute-start | bytes 786440 | tf_op jit(solution)/shard_map/ppermute | solution.py:429
  96.7 1.9 collective-permute-start.12
  98.7 3.5 collective-permute-start.13
  102.1 1.6 own_slice.9.own
  103.7 1.3 next_slices.9.image
  105.0 5.8 %collective-permute-done.13.fourth = f32[8,64,128]{2,1,0:T(8,128)S(1)} collective-permute-done((f32[8,64,128]{2,1,0:T(8,128)}, f32[8,64,128]{2,1,0:T(8,128)S(1)}, u32[]{:S(2)}, u32[]{:S(2)}) %collective-permute-start.13) | collective-permute-done | bytes 262176 | tf_op jit(solution)/shard_map/ppermute | solution.py:429
  110.8 1.8 products.1
  112.6 25.0 %all_to_all.15.parts = f32[64,8,128]{2,1,0:T(8,128)S(1)} all-to-all(f32[64,8,128]{2,1,0:T(8,128)S(1)} %bitcast.13), channel_id=1, replica_groups=mesh['site'=64,'vec'=8] {'site'}, dimensions={0} | all-to-all | bytes 524288 | tf_op jit(solution)/shard_map/all_to_all | solution.py:444
  137.7 25.0 %all_to_all.16 = f32[64,8,128]{2,1,0:T(8,128)S(1)} all-to-all(f32[64,8,128]{2,1,0:T(8,128)S(1)} %sum_parts.1), channel_id=1, replica_groups=mesh['site'=64,'vec'=8] {'site'}, dimensions={0} | all-to-all | bytes 524288 | tf_op jit(solution)/shard_map/all_to_all | solution.py:448
  163.8 7.3 %all-to-all-start.2 = ((f32[8,320,128]{2,1,0:T(8,128)}), f32[8,320,128]{2,1,0:T(8,128)S(1)}, u32[]{:S(2)}, u32[]{:S(2)}) async-start(f32[8,320,128]{2,1,0:T(8,128)} %repeat.1), calls=%async_computation.2 | async-start | bytes 2621440 | tf_op jit(solution)/shard_map/all_to_all | solution.py:458
  171.1 17.9 %all-to-all-done.2.gathered = f32[8,320,128]{2,1,0:T(8,128)S(1)} async-done(((f32[8,320,128]{2,1,0:T(8,128)}), f32[8,320,128]{2,1,0:T(8,128)S(1)}, u32[]{:S(2)}, u32[]{:S(2)}) %all-to-all-start.2) | async-done | bytes 1310752 | tf_op jit(solution)/shard_map/all_to_all | solution.py:458
  189.0 236.5 %inverse_factor.1.inverse = f32[512,512]{1,0:T(8,128)S(1)} custom-call(f32[8,320,128]{2,1,0:T(8,128)S(1)} %all-to-all-done.2.gathered), custom_call_target="tpu_custom_call" | custom-call | flops 7247757312 | bytes 2097152 | tf_op jit(solution)/shard_map/inverse_factor/pallas_call | solution.py:460
  425.5 1.3 basis.1
  426.8 2.2 projected.1
  (33 shorter events, 12.5 us)
Async XLA Ops:
  7.2 156.7 %all-gather.3.cloned.1.call-start = ((), (), s32[]{:S(2)}) async-start(), calls=%async_computation.3 | async-start | bytes 2359296 | tf_op jit(solution)/shard_map/all_gather | solution.py:442
  7.2 1.2 copy-start
  8.4 0.9 copy-start.2
  9.4 16.7 %copy-start.1 = (f32[8,4,64,128]{3,2,1,0:T(8,128)S(1)}, f32[8,4,64,128]{3,2,1,0:T(8,128)}, u32[]{:S(2)}) copy-start(f32[8,4,64,128]{3,2,1,0:T(8,128)} %hop.3) | copy-start | bytes 3145732
  9.4 16.7 %copy-start.4 = (s32[8,8]{1,0:T(8,128)S(1)}, s32[8,8]{1,0:T(8,128)}, u32[]{:S(2)}) copy-start(s32[8,8]{1,0:T(8,128)} %near.21) | copy-start | bytes 772
  9.8 21.6 %collective-permute-start.1 = (f32[8,64,128]{2,1,0:T(8,128)S(1)}, f32[8,64,128]{2,1,0:T(8,128)S(1)}, u32[]{:S(2)}, u32[]{:S(2)}) collective-permute-start(f32[8,64,128]{2,1,0:T(8,128)S(1)} %get-tuple-element.22), channel_id=1, source_target_pairs={{0,8},{8,16},{16,24},{24,32},{32,40},{40,48},{48,56},{56,64},{64,7... | collective-permute-start | bytes 786440 | tf_op jit(solution)/shard_map/ppermute | solution.py:344
  14.1 17.3 %collective-permute-start = (f32[8,64,128]{2,1,0:T(8,128)S(1)}, f32[8,64,128]{2,1,0:T(8,128)S(1)}, u32[]{:S(2)}, u32[]{:S(2)}) collective-permute-start(f32[8,64,128]{2,1,0:T(8,128)S(1)} %bitcast.9), channel_id=1, source_target_pairs={{0,504},{8,0},{16,8},{24,16},{32,24},{40,32},{48,40},{56,48},{64,5... | collective-permute-start | bytes 786440 | tf_op jit(solution)/shard_map/ppermute | solution.py:344
  26.1 1.0 copy-start.5
  32.5 11.1 %collective-permute-start.2 = (f32[8,64,128]{2,1,0:T(8,128)S(1)}, f32[8,64,128]{2,1,0:T(8,128)S(1)}, u32[]{:S(2)}, u32[]{:S(2)}) collective-permute-start(f32[8,64,128]{2,1,0:T(8,128)S(1)} %get-tuple-element.27.x.rest_0_), channel_id=1, source_target_pairs={{0,504},{8,0},{16,8},{24,16},{32,24},{40,32},{48,40},{56,48},{64,5... | collective-permute-start | bytes 786440 | tf_op jit(solution)/shard_map/ppermute | solution.py:344
  39.5 11.2 %collective-permute-start.3 = (f32[8,64,128]{2,1,0:T(8,128)S(1)}, f32[8,64,128]{2,1,0:T(8,128)S(1)}, u32[]{:S(2)}, u32[]{:S(2)}) collective-permute-start(f32[8,64,128]{2,1,0:T(8,128)S(1)} %get-tuple-element.28), channel_id=1, source_target_pairs={{0,8},{8,16},{16,24},{24,32},{32,40},{40,48},{48,56},{56,64},{64,7... | collective-permute-start | bytes 786440 | tf_op jit(solution)/shard_map/ppermute | solution.py:344
  51.8 7.1 %collective-permute-start.4 = (f32[8,64,128]{2,1,0:T(8,128)S(1)}, f32[8,64,128]{2,1,0:T(8,128)S(1)}, u32[]{:S(2)}, u32[]{:S(2)}) collective-permute-start(f32[8,64,128]{2,1,0:T(8,128)S(1)} %get-tuple-element.29.x.rest_0_), channel_id=1, source_target_pairs={{0,504},{8,0},{16,8},{24,16},{32,24},{40,32},{48,40},{56,48},{64,5... | collective-permute-start | bytes 786440 | tf_op jit(solution)/shard_map/ppermute | solution.py:344
  53.7 10.4 %collective-permute-start.5 = (f32[8,64,128]{2,1,0:T(8,128)S(1)}, f32[8,64,128]{2,1,0:T(8,128)S(1)}, u32[]{:S(2)}, u32[]{:S(2)}) collective-permute-start(f32[8,64,128]{2,1,0:T(8,128)S(1)} %get-tuple-element.30), channel_id=1, source_target_pairs={{0,8},{8,16},{16,24},{24,32},{32,40},{40,48},{48,56},{56,64},{64,7... | collective-permute-start | bytes 786440 | tf_op jit(solution)/shard_map/ppermute | solution.py:344
  65.2 7.1 %collective-permute-start.6 = (f32[8,64,128]{2,1,0:T(8,128)S(1)}, f32[8,64,128]{2,1,0:T(8,128)S(1)}, u32[]{:S(2)}, u32[]{:S(2)}) collective-permute-start(f32[8,64,128]{2,1,0:T(8,128)S(1)} %get-tuple-element.31.x), channel_id=1, source_target_pairs={{0,504},{8,0},{16,8},{24,16},{32,24},{40,32},{48,40},{56,48},{64,5... | collective-permute-start | bytes 786440 | tf_op jit(solution)/shard_map/ppermute | solution.py:344
  67.1 10.4 %collective-permute-start.7 = (f32[8,64,128]{2,1,0:T(8,128)S(1)}, f32[8,64,128]{2,1,0:T(8,128)S(1)}, u32[]{:S(2)}, u32[]{:S(2)}) collective-permute-start(f32[8,64,128]{2,1,0:T(8,128)S(1)} %get-tuple-element.32), channel_id=1, source_target_pairs={{0,8},{8,16},{16,24},{24,32},{32,40},{40,48},{48,56},{56,64},{64,7... | collective-permute-start | bytes 786440 | tf_op jit(solution)/shard_map/ppermute | solution.py:344
  79.2 19.5 %collective-permute-start.8 = (f32[8,64,128]{2,1,0:T(8,128)}, f32[8,64,128]{2,1,0:T(8,128)S(1)}, u32[]{:S(2)}, u32[]{:S(2)}) collective-permute-start(f32[8,64,128]{2,1,0:T(8,128)} %get-tuple-element.33.x.rest_0_.own), channel_id=1, source_target_pairs={{0,504},{8,0},{16,8},{24,16},{32,24},{40,32},{48,40},{56,48},{64,5... | collective-permute-start | bytes 786440 | tf_op jit(solution)/shard_map/ppermute | solution.py:344
  81.1 22.6 %collective-permute-start.9 = (f32[8,64,128]{2,1,0:T(8,128)S(1)}, f32[8,64,128]{2,1,0:T(8,128)S(1)}, u32[]{:S(2)}, u32[]{:S(2)}) collective-permute-start(f32[8,64,128]{2,1,0:T(8,128)S(1)} %get-tuple-element.34), channel_id=1, source_target_pairs={{0,8},{8,16},{16,24},{24,32},{32,40},{40,48},{48,56},{56,64},{64,7... | collective-permute-start | bytes 786440 | tf_op jit(solution)/shard_map/ppermute | solution.py:344
  84.5 20.5 %collective-permute-start.10 = (f32[8,64,128]{2,1,0:T(8,128)}, f32[8,64,128]{2,1,0:T(8,128)S(1)}, u32[]{:S(2)}, u32[]{:S(2)}) collective-permute-start(f32[8,64,128]{2,1,0:T(8,128)} %get-tuple-element.33.x.rest_0_.own), channel_id=1, source_target_pairs={{6,0},{7,1},{0,2},{1,3},{2,4},{3,5},{4,6},{5,7},{14,8},{15,9},{8,1... | collective-permute-start | bytes 786440 | tf_op jit(solution)/shard_map/ppermute | solution.py:429
  87.6 17.4 %collective-permute-start.11 = (f32[8,64,128]{2,1,0:T(8,128)}, f32[8,64,128]{2,1,0:T(8,128)S(1)}, u32[]{:S(2)}, u32[]{:S(2)}) collective-permute-start(f32[8,64,128]{2,1,0:T(8,128)} %get-tuple-element.33.x.rest_0_.own), channel_id=1, source_target_pairs={{3,0},{2,1},{5,2},{4,3},{7,4},{6,5},{1,6},{0,7},{11,8},{10,9},{13,... | collective-permute-start | bytes 786440 | tf_op jit(solution)/shard_map/ppermute | solution.py:429
  96.7 8.3 %collective-permute-start.12 = (f32[8,64,128]{2,1,0:T(8,128)}, f32[8,64,128]{2,1,0:T(8,128)S(1)}, u32[]{:S(2)}, u32[]{:S(2)}) collective-permute-start(f32[8,64,128]{2,1,0:T(8,128)} %get-tuple-element.33.x.rest_0_.own), channel_id=1, source_target_pairs={{1,0},{0,1},{3,2},{2,3},{5,4},{4,5},{7,6},{6,7},{9,8},{8,9},{11,10... | collective-permute-start | bytes 786440 | tf_op jit(solution)/shard_map/ppermute | solution.py:429
  98.7 12.1 %collective-permute-start.13 = (f32[8,64,128]{2,1,0:T(8,128)}, f32[8,64,128]{2,1,0:T(8,128)S(1)}, u32[]{:S(2)}, u32[]{:S(2)}) collective-permute-start(f32[8,64,128]{2,1,0:T(8,128)} %get-tuple-element.33.x.rest_0_.own), channel_id=1, source_target_pairs={{5,0},{4,1},{7,2},{6,3},{0,4},{1,5},{2,6},{3,7},{13,8},{12,9},{15,... | collective-permute-start | bytes 786440 | tf_op jit(solution)/shard_map/ppermute | solution.py:429
  163.8 25.2 %all-to-all-start.2 = ((f32[8,320,128]{2,1,0:T(8,128)}), f32[8,320,128]{2,1,0:T(8,128)S(1)}, u32[]{:S(2)}, u32[]{:S(2)}) async-start(f32[8,320,128]{2,1,0:T(8,128)} %repeat.1), calls=%async_computation.2 | async-start | bytes 2621440 | tf_op jit(solution)/shard_map/all_to_all | solution.py:458
  189.0 236.5 %copy-start.3 = (f32[4096,128]{1,0:T(8,128)S(1)}, f32[4096,128]{1,0:T(8,128)}, u32[]{:S(2)}) copy-start(f32[4096,128]{1,0:T(8,128)} %all-gather.3.cloned.1.call-done) | copy-start | bytes 6291460
Sparse Core Ops, SparseCore 0:
  112.8 22.9 all-gather.2

commit v7 on v5

--- a/solution.py
+++ b/solution.py
@@ -86,10 +86,18 @@
     return split(full * (1.0 / RADIUS))
 
 
-def backward_kernel(x, hop, out, high, low):
+def in_turn(place, forward, backward):
+    even = place[0] % 2 == 0
+    return jnp.where(even, forward, backward), jnp.where(even, backward, forward)
+
+
+def backward_kernel(place, x, hop, first, second, high, low, hop_out):
     for s in range(x.shape[0]):
-        high[s], low[s] = right_operand(conjugated(hop[s, 0]))
-        out[s] = three_products(stacked(x[s]), high[s], low[s])
+        high[s], low[s] = right_operand(conjugated(hop[s, 3]))
+        vectors = x[s]
+        back = three_products(stacked(vectors), high[s], low[s])
+        first[s], second[s] = in_turn(place, vectors, back)
+        hop_out[s] = hop[s]
 
 
 def prepare_kernel(near, diag, hop, own_high, own_low, ahead_high, ahead_low):
@@ -118,26 +126,30 @@
         out[s] = three_products(parts, high[s], low[s])
 
 
-def step_kernel(mode, near, own, ahead, received, ahead_high, ahead_low, *rest):
+def step_kernel(mode, near, place, own, came_first, came_second, ahead_high, ahead_low, *rest):
     sites = own.shape[0]
     more = rest[0] if mode != "first" else None
     if mode == "image":
-        out, back = rest[-1], None
+        out = rest[-1]
     else:
-        back_high, back_low, out, back = rest[-4:]
+        back_high, back_low, out, first, second = rest[-5:]
     for s in range(sites):
-        parts = stacked(ahead[lax.rem(near[s, 3], sites)])
-        part = three_products(parts, ahead_high[s], ahead_low[s])
-        applied = own[s] + (part + received[lax.rem(near[s, 7], sites)])
+        n, m = lax.rem(near[s, 3], sites), lax.rem(near[s, 7], sites)
+        ahead, _ = in_turn(place, came_first[n], came_second[n])
+        _, received = in_turn(place, came_first[m], came_second[m])
+        part = three_products(stacked(ahead), ahead_high[s], ahead_low[s])
+        applied = own[s] + (part + received)
         if mode == "first":
             out[s] = applied
         elif mode == "next":
             out[s] = 2.0 * applied - more[s]
         else:
             out[s] = RADIUS * applied + CENTER * more[s]
-    if back is not None:
+    if mode != "image":
         for s in range(sites):
-            back[s] = three_products(stacked(out[s]), back_high[s], back_low[s])
+            vectors = out[s]
+            back = three_products(stacked(vectors), back_high[s], back_low[s])
+            first[s], second[s] = in_turn(place, vectors, back)
 
 
 def senders(devices):
@@ -148,7 +160,7 @@
         opposite = (x + chips // 2) % chips
         table.append(
             [
-                2 * ((x - 1) % chips) + c,
+                2 * ((x - 1 + 2 * c) % chips) + c,
                 2 * ((x + 1) % chips) + 1 - c,
                 2 * x + 1 - c,
                 2 * opposite + (1 - c if x < chips // 2 else c),
@@ -332,9 +344,18 @@
     out[...] = multiply(half_way, inverse[...], NT) * (1.0 / count)
 
 
-def passed_along(x, by):
-    size = lax.axis_size("site")
-    return lax.ppermute(x, "site", [(i, (i + by) % size) for i in range(size)])
+def exchanged(first, second):
+    slices, devices = lax.axis_size("site"), lax.axis_size("vec")
+
+    def pairs(way):
+        return [
+            (s * devices + v, ((s + (way if v % 2 == 0 else -way)) % slices) * devices + v)
+            for s in range(slices)
+            for v in range(devices)
+        ]
+
+    axes = ("site", "vec")
+    return lax.ppermute(first, axes, pairs(-1)), lax.ppermute(second, axes, pairs(1))
 
 
 def local(diag_blocks, hop_blocks, neighbors, start_basis):
@@ -356,24 +377,15 @@
         return sites * cols * blocks * 3 * both * both * 2
 
     current = jnp.swapaxes(start_basis, 1, 2)
-    back, *back_mats = pl.pallas_call(
+    first, second, *back_mats, links = call(
         backward_kernel,
-        out_shape=(block, *matrices(1)),
-        grid=(1,),
-        in_specs=[
-            pl.BlockSpec((sites, cols, both), lambda i: (0, 0, 0)),
-            pl.BlockSpec((sites, 1, half, both), lambda i: (0, 3, 0, 0)),
-        ],
-        out_specs=(
-            pl.BlockSpec((sites, cols, both), lambda i: (0, 0, 0)),
-            *[pl.BlockSpec((sites, both, both), lambda i: (0, 0, 0))] * 2,
-        ),
-        compiler_params=pltpu.CompilerParams(vmem_limit_bytes=VMEM_WHOLE),
-        cost_estimate=pl.CostEstimate(
-            flops=work(1), bytes_accessed=4 * size, transcendentals=0
-        ),
+        (block, block, *matrices(1), shape(hop_blocks.shape, f32)),
+        1,
+        2,
+        flops=work(1),
+        moved=8 * size,
         name="backward",
-    )(current, hop_blocks)
+    )(place, current, hop_blocks)
     mats = call(
         prepare_kernel,
         (*matrices(4), *matrices(1)),
@@ -382,12 +394,11 @@
         flops=1 << 24,
         moved=1 << 23,
         name="prepare",
-    )(neighbors, diag_blocks, hop_blocks)
+    )(neighbors, diag_blocks, links)
     own_mats, ahead_mats = mats[:2], mats[2:]
 
-    def apply(vectors, back, mode, *more):
-        ahead = passed_along(vectors, -1)
-        received = passed_along(back, 1)
+    def apply(vectors, sent, mode, *more):
+        came = exchanged(*sent)
         own = call(
             own_kernel,
             block,
@@ -402,21 +413,21 @@
             more = (*more, *back_mats)
         return call(
             functools.partial(step_kernel, mode),
-            block if mode == "image" else (block, block),
-            1,
+            block if mode == "image" else (block, block, block),
+            2,
             5 + len(more),
             flops=work(1),
             moved=8 * size,
             name="next_slices",
-        )(neighbors, own, ahead, received, *ahead_mats, *more)
+        )(neighbors, place, own, *came, *ahead_mats, *more)
 
     previous = current
-    current, back = apply(current, back, "first")
+    current, *sent = apply(current, (first, second), "first")
     for _ in range(DEGREE - 1):
-        following, back = apply(current, back, "next", previous)
+        following, *sent = apply(current, sent, "next", previous)
         previous, current = current, following
 
-    image = apply(current, back, "image", current)
+    image = apply(current, sent, "image", current)
     table = senders(devices)
     others = [
         lax.ppermute(current, "vec", [(table[v][i], v) for v in range(devices)]) for i in range(4)

time: 430 us -> 429 us (level)
  starting transfers between devices: 56.8 us -> 65.8 us
  waiting for transfers between devices: 25.7 us -> 17.1 us
    ppermute x10, starting transfers between devices: 39.1 us -> 52.1 us  [the longest x5 40.1 us: exchanged(): lax.ppermute(second, axes, pairs(1))]
    ppermute x10, waiting for transfers between devices: 19.8 us -> 11.8 us  [the longest x5 9.89 us: exchanged(): lax.ppermute(second, axes, pairs(1))]
  transfers between devices with their start and end apart: 16 -> 16, of which waited for: 7 -> 8; matrix products, arithmetic and copies ran while one was open for 0% -> 0% of each run, Pallas kernels for 58% -> 58%
where the time goes in v7:
time: 429 us; the launch traced here: 428 us
  Pallas kernels  258 us (60%)
  blocking collectives  67.8 us (16%)
  starting transfers between devices  65.8 us (15%)
  waiting for transfers between devices  17.1 us (4%)
  between operations  14.3 us (3%)
  local copies, waits for them, and re-layouts  5.71 us (1%)
    pallas_call x1, Pallas kernels, local(): call(functools.partial(inverse_kernel, count), shape((all_cols, all_cols)...  236 us
    ppermute x5, starting transfers between devices, exchanged(): lax.ppermute(second, axes, pairs(1))  40.1 us
    all_to_all x1, blocking collectives, local(): lax.all_to_all(products.reshape(slices, 8, both), 'site', 0, 0, tiled=True)  25.4 us
    all_to_all x1, blocking collectives, local(): lax.all_to_all(summed, 'site', 0, 0, tiled=True).reshape(slices * 8, both)  25.3 us
    all_gather x1, blocking collectives, local(): gram = lax.all_gather(whole[:kept], 'vec', axis=0)  17 us
    ppermute x4, starting transfers between devices, local(): lax.ppermute(current, 'vec', [(table[v][i], v) for v in range(devices)])  13.6 us
    ppermute x5, starting transfers between devices, exchanged(): lax.ppermute(first, axes, pairs(-1))  12 us
    ppermute x5, waiting for transfers between devices, exchanged(): lax.ppermute(second, axes, pairs(1))  9.89 us
  transfers between devices with their start and end apart: 16, of which 8 were waited for; matrix products, arithmetic and copies ran while one was open for 0% of the time, Pallas kernels for 58%

profile of v7, /device:TPU:1, one launch (start us, length us, event | category | flops | bytes accessed | tf_op | source)
XLA Modules:
  0.0 428.3 jit_solution(12964361380129987739)
XLA Ops:
  8.2 1.2 copy-done.4
  9.8 4.4 %collective-permute-start = (f32[8,64,128]{2,1,0:T(8,128)S(1)}, f32[8,64,128]{2,1,0:T(8,128)S(1)}, u32[]{:S(2)}, u32[]{:S(2)}) collective-permute-start(f32[8,64,128]{2,1,0:T(8,128)S(1)} %get-tuple-element.29), channel_id=1, source_target_pairs={{0,504},{1,9},{2,506},{3,11},{4,508},{5,13},{6,510},{7,15},{8,0},{... | collective-permute-start | bytes 786440 | tf_op jit(solution)/shard_map/ppermute | solution.py:358
  14.1 11.9 %collective-permute-start.1 = (f32[8,64,128]{2,1,0:T(8,128)S(1)}, f32[8,64,128]{2,1,0:T(8,128)S(1)}, u32[]{:S(2)}, u32[]{:S(2)}) collective-permute-start(f32[8,64,128]{2,1,0:T(8,128)S(1)} %get-tuple-element.30), channel_id=1, source_target_pairs={{0,8},{1,505},{2,10},{3,507},{4,12},{5,509},{6,14},{7,511},{8,16},... | collective-permute-start | bytes 786440 | tf_op jit(solution)/shard_map/ppermute | solution.py:358
  27.7 3.1 prepare.1
  33.2 1.9 collective-permute-start.2
  35.1 6.7 %collective-permute-start.3 = (f32[8,64,128]{2,1,0:T(8,128)S(1)}, f32[8,64,128]{2,1,0:T(8,128)S(1)}, u32[]{:S(2)}, u32[]{:S(2)}) collective-permute-start(f32[8,64,128]{2,1,0:T(8,128)S(1)} %get-tuple-element.37), channel_id=1, source_target_pairs={{0,8},{1,505},{2,10},{3,507},{4,12},{5,509},{6,14},{7,511},{8,16},... | collective-permute-start | bytes 786440 | tf_op jit(solution)/shard_map/ppermute | solution.py:358
  43.6 4.0 collective-permute-done.3.came_second
  48.7 1.9 collective-permute-start.4
  50.7 7.2 %collective-permute-start.5 = (f32[8,64,128]{2,1,0:T(8,128)S(1)}, f32[8,64,128]{2,1,0:T(8,128)S(1)}, u32[]{:S(2)}, u32[]{:S(2)}) collective-permute-start(f32[8,64,128]{2,1,0:T(8,128)S(1)} %get-tuple-element.40), channel_id=1, source_target_pairs={{0,8},{1,505},{2,10},{3,507},{4,12},{5,509},{6,14},{7,511},{8,16},... | collective-permute-start | bytes 786440 | tf_op jit(solution)/shard_map/ppermute | solution.py:358
  59.7 3.2 collective-permute-done.5.came_second
  64.0 1.9 collective-permute-start.6
  65.9 7.1 %collective-permute-start.7 = (f32[8,64,128]{2,1,0:T(8,128)S(1)}, f32[8,64,128]{2,1,0:T(8,128)S(1)}, u32[]{:S(2)}, u32[]{:S(2)}) collective-permute-start(f32[8,64,128]{2,1,0:T(8,128)S(1)} %get-tuple-element.43), channel_id=1, source_target_pairs={{0,8},{1,505},{2,10},{3,507},{4,12},{5,509},{6,14},{7,511},{8,16},... | collective-permute-start | bytes 786440 | tf_op jit(solution)/shard_map/ppermute | solution.py:358
  74.9 2.6 collective-permute-done.7.came_second
  77.5 1.6 next_slices.8
  79.1 1.9 collective-permute-start.8
  81.0 7.1 %collective-permute-start.9 = (f32[8,64,128]{2,1,0:T(8,128)S(1)}, f32[8,64,128]{2,1,0:T(8,128)S(1)}, u32[]{:S(2)}, u32[]{:S(2)}) collective-permute-start(f32[8,64,128]{2,1,0:T(8,128)S(1)} %get-tuple-element.46), channel_id=1, source_target_pairs={{0,8},{1,505},{2,10},{3,507},{4,12},{5,509},{6,14},{7,511},{8,16},... | collective-permute-start | bytes 786440 | tf_op jit(solution)/shard_map/ppermute | solution.py:358
  88.2 4.6 %collective-permute-start.13 = (f32[8,64,128]{2,1,0:T(8,128)}, f32[8,64,128]{2,1,0:T(8,128)S(1)}, u32[]{:S(2)}, u32[]{:S(2)}) collective-permute-start(f32[8,64,128]{2,1,0:T(8,128)} %get-tuple-element.44.x.rest_0_.own), channel_id=1, source_target_pairs={{5,0},{4,1},{7,2},{6,3},{0,4},{1,5},{2,6},{3,7},{13,8},{12,9},{15,... | collective-permute-start | bytes 786440 | tf_op jit(solution)/shard_map/ppermute | solution.py:433
  92.8 4.3 collective-permute-start.12
  97.1 2.8 collective-permute-start.11
  99.9 1.9 collective-permute-start.10
  101.9 1.6 own_slice.9.own
  103.4 1.3 next_slices.9.image
  104.7 3.4 collective-permute-done.11.second
  108.1 1.9 collective-permute-done.10.first
  110.0 1.8 products.1
  111.9 25.4 %all_to_all.10.parts = f32[64,8,128]{2,1,0:T(8,128)S(1)} all-to-all(f32[64,8,128]{2,1,0:T(8,128)S(1)} %bitcast.15), channel_id=1, replica_groups=mesh['site'=64,'vec'=8] {'site'}, dimensions={0} | all-to-all | bytes 524288 | tf_op jit(solution)/shard_map/all_to_all | solution.py:448
  137.3 25.3 %all_to_all.11 = f32[64,8,128]{2,1,0:T(8,128)S(1)} all-to-all(f32[64,8,128]{2,1,0:T(8,128)S(1)} %sum_parts.1), channel_id=1, replica_groups=mesh['site'=64,'vec'=8] {'site'}, dimensions={0} | all-to-all | bytes 524288 | tf_op jit(solution)/shard_map/all_to_all | solution.py:452
  163.4 17.0 %all-gather.1 = f32[1280,128]{1,0:T(8,128)S(1)} all-gather(f32[160,128]{1,0:T(8,128)S(1)} %slice.6), channel_id=3, replica_groups=mesh['site'=64,'vec'=8] {'vec'}, dimensions={0}, use_global_device_ids=true | all-gather | bytes 737280 | tf_op jit(solution)/shard_map/all_gather | solution.py:455
  180.4 236.3 %inverse_factor.1.inverse = f32[512,512]{1,0:T(8,128)S(1)} custom-call(f32[8,160,128]{2,1,0:T(8,128)S(1)} %bitcast.16), custom_call_target="tpu_custom_call" | custom-call | flops 7247757312 | bytes 2097152 | tf_op jit(solution)/shard_map/inverse_factor/pallas_call | solution.py:457
  416.8 1.3 basis.1
  418.1 1.2 copy-done.3
  419.3 2.2 projected.1
  (40 shorter events, 13.7 us)
Async XLA Ops:
  7.2 155.5 %all-gather.6.cloned.1.call-start = ((), (), s32[]{:S(2)}) async-start(), calls=%async_computation.2 | async-start | bytes 2359296 | tf_op jit(solution)/shard_map/all_gather | solution.py:446
  7.2 1.0 copy-start
  8.2 1.2 copy-start.4
  9.4 21.5 %copy-start.1 = (f32[8,128,64]{1,2,0:T(8,128)S(1)}, f32[8,128,64]{1,2,0:T(8,128)}, u32[]{:S(2)}) copy-start(f32[8,128,64]{1,2,0:T(8,128)} %param.7) | copy-start | bytes 786436
  9.8 22.3 %collective-permute-start = (f32[8,64,128]{2,1,0:T(8,128)S(1)}, f32[8,64,128]{2,1,0:T(8,128)S(1)}, u32[]{:S(2)}, u32[]{:S(2)}) collective-permute-start(f32[8,64,128]{2,1,0:T(8,128)S(1)} %get-tuple-element.29), channel_id=1, source_target_pairs={{0,504},{1,9},{2,506},{3,11},{4,508},{5,13},{6,510},{7,15},{8,0},{... | collective-permute-start | bytes 786440 | tf_op jit(solution)/shard_map/ppermute | solution.py:358
  14.1 17.9 %collective-permute-start.1 = (f32[8,64,128]{2,1,0:T(8,128)S(1)}, f32[8,64,128]{2,1,0:T(8,128)S(1)}, u32[]{:S(2)}, u32[]{:S(2)}) collective-permute-start(f32[8,64,128]{2,1,0:T(8,128)S(1)} %get-tuple-element.30), channel_id=1, source_target_pairs={{0,8},{1,505},{2,10},{3,507},{4,12},{5,509},{6,14},{7,511},{8,16},... | collective-permute-start | bytes 786440 | tf_op jit(solution)/shard_map/ppermute | solution.py:358
  26.1 0.7 copy-start.5
  26.8 0.9 copy-start.7
  32.1 15.6 %copy-start.6 = (s32[8,8]{1,0:T(8,128)S(1)}, s32[8,8]{1,0:T(8,128)}, u32[]{:S(2)}) copy-start(s32[8,8]{1,0:T(8,128)} %near.21) | copy-start | bytes 772
  33.2 10.4 %collective-permute-start.2 = (f32[8,64,128]{2,1,0:T(8,128)S(1)}, f32[8,64,128]{2,1,0:T(8,128)S(1)}, u32[]{:S(2)}, u32[]{:S(2)}) collective-permute-start(f32[8,64,128]{2,1,0:T(8,128)S(1)} %get-tuple-element.36), channel_id=1, source_target_pairs={{0,504},{1,9},{2,506},{3,11},{4,508},{5,13},{6,510},{7,15},{8,0},{... | collective-permute-start | bytes 786440 | tf_op jit(solution)/shard_map/ppermute | solution.py:358
  35.1 12.6 %collective-permute-start.3 = (f32[8,64,128]{2,1,0:T(8,128)S(1)}, f32[8,64,128]{2,1,0:T(8,128)S(1)}, u32[]{:S(2)}, u32[]{:S(2)}) collective-permute-start(f32[8,64,128]{2,1,0:T(8,128)S(1)} %get-tuple-element.37), channel_id=1, source_target_pairs={{0,8},{1,505},{2,10},{3,507},{4,12},{5,509},{6,14},{7,511},{8,16},... | collective-permute-start | bytes 786440 | tf_op jit(solution)/shard_map/ppermute | solution.py:358
  48.7 10.9 %collective-permute-start.4 = (f32[8,64,128]{2,1,0:T(8,128)S(1)}, f32[8,64,128]{2,1,0:T(8,128)S(1)}, u32[]{:S(2)}, u32[]{:S(2)}) collective-permute-start(f32[8,64,128]{2,1,0:T(8,128)S(1)} %get-tuple-element.39), channel_id=1, source_target_pairs={{0,504},{1,9},{2,506},{3,11},{4,508},{5,13},{6,510},{7,15},{8,0},{... | collective-permute-start | bytes 786440 | tf_op jit(solution)/shard_map/ppermute | solution.py:358
  50.7 12.2 %collective-permute-start.5 = (f32[8,64,128]{2,1,0:T(8,128)S(1)}, f32[8,64,128]{2,1,0:T(8,128)S(1)}, u32[]{:S(2)}, u32[]{:S(2)}) collective-permute-start(f32[8,64,128]{2,1,0:T(8,128)S(1)} %get-tuple-element.40), channel_id=1, source_target_pairs={{0,8},{1,505},{2,10},{3,507},{4,12},{5,509},{6,14},{7,511},{8,16},... | collective-permute-start | bytes 786440 | tf_op jit(solution)/shard_map/ppermute | solution.py:358
  64.0 10.9 %collective-permute-start.6 = (f32[8,64,128]{2,1,0:T(8,128)S(1)}, f32[8,64,128]{2,1,0:T(8,128)S(1)}, u32[]{:S(2)}, u32[]{:S(2)}) collective-permute-start(f32[8,64,128]{2,1,0:T(8,128)S(1)} %get-tuple-element.42), channel_id=1, source_target_pairs={{0,504},{1,9},{2,506},{3,11},{4,508},{5,13},{6,510},{7,15},{8,0},{... | collective-permute-start | bytes 786440 | tf_op jit(solution)/shard_map/ppermute | solution.py:358
  65.9 11.6 %collective-permute-start.7 = (f32[8,64,128]{2,1,0:T(8,128)S(1)}, f32[8,64,128]{2,1,0:T(8,128)S(1)}, u32[]{:S(2)}, u32[]{:S(2)}) collective-permute-start(f32[8,64,128]{2,1,0:T(8,128)S(1)} %get-tuple-element.43), channel_id=1, source_target_pairs={{0,8},{1,505},{2,10},{3,507},{4,12},{5,509},{6,14},{7,511},{8,16},... | collective-permute-start | bytes 786440 | tf_op jit(solution)/shard_map/ppermute | solution.py:358
  79.1 20.8 %collective-permute-start.8 = (f32[8,64,128]{2,1,0:T(8,128)S(1)}, f32[8,64,128]{2,1,0:T(8,128)S(1)}, u32[]{:S(2)}, u32[]{:S(2)}) collective-permute-start(f32[8,64,128]{2,1,0:T(8,128)S(1)} %get-tuple-element.45), channel_id=1, source_target_pairs={{0,504},{1,9},{2,506},{3,11},{4,508},{5,13},{6,510},{7,15},{8,0},{... | collective-permute-start | bytes 786440 | tf_op jit(solution)/shard_map/ppermute | solution.py:358
  81.0 22.4 %collective-permute-start.9 = (f32[8,64,128]{2,1,0:T(8,128)S(1)}, f32[8,64,128]{2,1,0:T(8,128)S(1)}, u32[]{:S(2)}, u32[]{:S(2)}) collective-permute-start(f32[8,64,128]{2,1,0:T(8,128)S(1)} %get-tuple-element.46), channel_id=1, source_target_pairs={{0,8},{1,505},{2,10},{3,507},{4,12},{5,509},{6,14},{7,511},{8,16},... | collective-permute-start | bytes 786440 | tf_op jit(solution)/shard_map/ppermute | solution.py:358
  88.2 16.5 %collective-permute-start.13 = (f32[8,64,128]{2,1,0:T(8,128)}, f32[8,64,128]{2,1,0:T(8,128)S(1)}, u32[]{:S(2)}, u32[]{:S(2)}) collective-permute-start(f32[8,64,128]{2,1,0:T(8,128)} %get-tuple-element.44.x.rest_0_.own), channel_id=1, source_target_pairs={{5,0},{4,1},{7,2},{6,3},{0,4},{1,5},{2,6},{3,7},{13,8},{12,9},{15,... | collective-permute-start | bytes 786440 | tf_op jit(solution)/shard_map/ppermute | solution.py:433
  92.8 11.9 %collective-permute-start.12 = (f32[8,64,128]{2,1,0:T(8,128)}, f32[8,64,128]{2,1,0:T(8,128)S(1)}, u32[]{:S(2)}, u32[]{:S(2)}) collective-permute-start(f32[8,64,128]{2,1,0:T(8,128)} %get-tuple-element.44.x.rest_0_.own), channel_id=1, source_target_pairs={{1,0},{0,1},{3,2},{2,3},{5,4},{4,5},{7,6},{6,7},{9,8},{8,9},{11,10... | collective-permute-start | bytes 786440 | tf_op jit(solution)/shard_map/ppermute | solution.py:433
  97.1 11.0 %collective-permute-start.11 = (f32[8,64,128]{2,1,0:T(8,128)}, f32[8,64,128]{2,1,0:T(8,128)S(1)}, u32[]{:S(2)}, u32[]{:S(2)}) collective-permute-start(f32[8,64,128]{2,1,0:T(8,128)} %get-tuple-element.44.x.rest_0_.own), channel_id=1, source_target_pairs={{3,0},{2,1},{5,2},{4,3},{7,4},{6,5},{1,6},{0,7},{11,8},{10,9},{13,... | collective-permute-start | bytes 786440 | tf_op jit(solution)/shard_map/ppermute | solution.py:433
  99.9 10.1 %collective-permute-start.10 = (f32[8,64,128]{2,1,0:T(8,128)}, f32[8,64,128]{2,1,0:T(8,128)S(1)}, u32[]{:S(2)}, u32[]{:S(2)}) collective-permute-start(f32[8,64,128]{2,1,0:T(8,128)} %get-tuple-element.44.x.rest_0_.own), channel_id=1, source_target_pairs={{6,0},{3,1},{0,2},{5,3},{2,4},{7,5},{4,6},{1,7},{14,8},{11,9},{8,1... | collective-permute-start | bytes 786440 | tf_op jit(solution)/shard_map/ppermute | solution.py:433
  111.8 306.2 %all-gather.8.cloned.1.call-start = ((), (), s32[]{:S(2)}) async-start(), calls=%async_computation.3 | async-start | bytes 1179648 | tf_op jit(solution)/shard_map/all_gather | solution.py:454
  180.4 236.3 %copy-start.2 = (f32[4096,128]{1,0:T(8,128)S(1)}, f32[4096,128]{1,0:T(8,128)}, u32[]{:S(2)}) copy-start(f32[4096,128]{1,0:T(8,128)} %all-gather.6.cloned.1.call-done) | copy-start | bytes 6291460
  418.1 1.2 copy-start.3
Sparse Core Ops, SparseCore 0:
  111.9 23.4 all-gather.5
  163.5 24.9 all-gather.7

commit v8 on v5

--- a/solution.py
+++ b/solution.py
@@ -86,10 +86,11 @@
     return split(full * (1.0 / RADIUS))
 
 
-def backward_kernel(x, hop, out, high, low):
+def backward_kernel(x, hop, out, high, low, hop_out):
     for s in range(x.shape[0]):
-        high[s], low[s] = right_operand(conjugated(hop[s, 0]))
+        high[s], low[s] = right_operand(conjugated(hop[s, 3]))
         out[s] = three_products(stacked(x[s]), high[s], low[s])
+        hop_out[s] = hop[s]
 
 
 def prepare_kernel(near, diag, hop, own_high, own_low, ahead_high, ahead_low):
@@ -148,7 +149,7 @@
         opposite = (x + chips // 2) % chips
         table.append(
             [
-                2 * ((x - 1) % chips) + c,
+                2 * ((x - 1 + 2 * c) % chips) + c,
                 2 * ((x + 1) % chips) + 1 - c,
                 2 * x + 1 - c,
                 2 * opposite + (1 - c if x < chips // 2 else c),
@@ -356,22 +357,13 @@
         return sites * cols * blocks * 3 * both * both * 2
 
     current = jnp.swapaxes(start_basis, 1, 2)
-    back, *back_mats = pl.pallas_call(
+    back, *back_mats, links = call(
         backward_kernel,
-        out_shape=(block, *matrices(1)),
-        grid=(1,),
-        in_specs=[
-            pl.BlockSpec((sites, cols, both), lambda i: (0, 0, 0)),
-            pl.BlockSpec((sites, 1, half, both), lambda i: (0, 3, 0, 0)),
-        ],
-        out_specs=(
-            pl.BlockSpec((sites, cols, both), lambda i: (0, 0, 0)),
-            *[pl.BlockSpec((sites, both, both), lambda i: (0, 0, 0))] * 2,
-        ),
-        compiler_params=pltpu.CompilerParams(vmem_limit_bytes=VMEM_WHOLE),
-        cost_estimate=pl.CostEstimate(
-            flops=work(1), bytes_accessed=4 * size, transcendentals=0
-        ),
+        (block, *matrices(1), shape(hop_blocks.shape, f32)),
+        0,
+        2,
+        flops=work(1),
+        moved=8 * size,
         name="backward",
     )(current, hop_blocks)
     mats = call(
@@ -382,7 +374,7 @@
         flops=1 << 24,
         moved=1 << 23,
         name="prepare",
-    )(neighbors, diag_blocks, hop_blocks)
+    )(neighbors, diag_blocks, links)
     own_mats, ahead_mats = mats[:2], mats[2:]
 
     def apply(vectors, back, mode, *more):

time: 430 us -> 430 us (level)
  no operation moved by 1% of the time
where the time goes in v8:
time: 430 us; the launch traced here: 429 us
  Pallas kernels  259 us (60%)
  blocking collectives  67 us (16%)
  starting transfers between devices  58 us (13%)
  waiting for transfers between devices  25.7 us (6%)
  between operations  14.3 us (3%)
  local copies, waits for them, and re-layouts  4.75 us (1%)
    pallas_call x1, Pallas kernels, local(): call(functools.partial(inverse_kernel, count), shape((all_cols, all_cols)...  236 us
    ppermute x10, starting transfers between devices, passed_along(): return lax.ppermute(x, 'site', [(i, (i + by) % size) for i in range(size)])  40.3 us
    all_to_all x1, blocking collectives, local(): lax.all_to_all(summed, 'site', 0, 0, tiled=True).reshape(slices * 8, both)  25 us
    all_to_all x1, blocking collectives, local(): lax.all_to_all(products.reshape(slices, 8, both), 'site', 0, 0, tiled=True)  25 us
    ppermute x10, waiting for transfers between devices, passed_along(): return lax.ppermute(x, 'site', [(i, (i + by) % size) for i in range(size)])  19.8 us
    ppermute x4, starting transfers between devices, local(): lax.ppermute(current, 'vec', [(table[v][i], v) for v in range(devices)])  17.6 us
    all_gather x1, blocking collectives, local(): gram = lax.all_gather(whole[:kept], 'vec', axis=0)  17.1 us
  transfers between devices with their start and end apart: 16, of which 7 were waited for; matrix products, arithmetic and copies ran while one was open for 0% of the time, Pallas kernels for 58%

profile of v8, /device:TPU:1, one launch (start us, length us, event | category | flops | bytes accessed | tf_op | source)
XLA Modules:
  0.0 429.1 jit_solution(12239739958093854169)
XLA Ops:
  8.4 1.4 backward.1
  9.8 4.4 %collective-permute-start.1 = (f32[8,64,128]{2,1,0:T(8,128)S(1)}, f32[8,64,128]{2,1,0:T(8,128)S(1)}, u32[]{:S(2)}, u32[]{:S(2)}) collective-permute-start(f32[8,64,128]{2,1,0:T(8,128)S(1)} %get-tuple-element.24), channel_id=1, source_target_pairs={{0,8},{8,16},{16,24},{24,32},{32,40},{40,48},{48,56},{56,64},{64,7... | collective-permute-start | bytes 786440 | tf_op jit(solution)/shard_map/ppermute | solution.py:338
  14.2 12.0 %collective-permute-start = (f32[8,64,128]{2,1,0:T(8,128)}, f32[8,64,128]{2,1,0:T(8,128)S(1)}, u32[]{:S(2)}, u32[]{:S(2)}) collective-permute-start(f32[8,64,128]{2,1,0:T(8,128)} %bitcast.1.x.rest_0_), channel_id=1, source_target_pairs={{0,504},{8,0},{16,8},{24,16},{32,24},{40,32},{48,40},{56,48},{64,5... | collective-permute-start | bytes 786440 | tf_op jit(solution)/shard_map/ppermute | solution.py:338
  27.8 3.1 prepare.1
  30.9 1.6 own_slice.5.own
  33.6 6.2 %collective-permute-start.2 = (f32[8,64,128]{2,1,0:T(8,128)S(1)}, f32[8,64,128]{2,1,0:T(8,128)S(1)}, u32[]{:S(2)}, u32[]{:S(2)}) collective-permute-start(f32[8,64,128]{2,1,0:T(8,128)S(1)} %get-tuple-element.29.x.rest_0_), channel_id=1, source_target_pairs={{0,504},{8,0},{16,8},{24,16},{32,24},{40,32},{48,40},{56,48},{64,5... | collective-permute-start | bytes 786440 | tf_op jit(solution)/shard_map/ppermute | solution.py:338
  39.8 1.9 collective-permute-start.3
  43.8 7.2 %collective-permute-done.3.received = f32[8,64,128]{2,1,0:T(8,128)S(1)} collective-permute-done((f32[8,64,128]{2,1,0:T(8,128)S(1)}, f32[8,64,128]{2,1,0:T(8,128)S(1)}, u32[]{:S(2)}, u32[]{:S(2)}) %collective-permute-start.3) | collective-permute-done | bytes 262176 | tf_op jit(solution)/shard_map/ppermute | solution.py:338
  51.0 1.4 next_slices.6
  52.4 1.9 collective-permute-start.4
  54.4 3.4 collective-permute-start.5
  59.5 5.2 %collective-permute-done.5.received = f32[8,64,128]{2,1,0:T(8,128)S(1)} collective-permute-done((f32[8,64,128]{2,1,0:T(8,128)S(1)}, f32[8,64,128]{2,1,0:T(8,128)S(1)}, u32[]{:S(2)}, u32[]{:S(2)}) %collective-permute-start.5) | collective-permute-done | bytes 262176 | tf_op jit(solution)/shard_map/ppermute | solution.py:338
  65.8 1.9 collective-permute-start.6
  67.8 3.4 collective-permute-start.7
  73.0 5.2 %collective-permute-done.7.received = f32[8,64,128]{2,1,0:T(8,128)S(1)} collective-permute-done((f32[8,64,128]{2,1,0:T(8,128)S(1)}, f32[8,64,128]{2,1,0:T(8,128)S(1)}, u32[]{:S(2)}, u32[]{:S(2)}) %collective-permute-start.7) | collective-permute-done | bytes 262176 | tf_op jit(solution)/shard_map/ppermute | solution.py:338
  78.2 1.6 next_slices.8
  79.9 1.9 collective-permute-start.8
  81.8 3.4 collective-permute-start.9
  85.1 4.4 %collective-permute-start.10 = (f32[8,64,128]{2,1,0:T(8,128)}, f32[8,64,128]{2,1,0:T(8,128)S(1)}, u32[]{:S(2)}, u32[]{:S(2)}) collective-permute-start(f32[8,64,128]{2,1,0:T(8,128)} %get-tuple-element.35.x.rest_0_.own), channel_id=1, source_target_pairs={{6,0},{3,1},{0,2},{5,3},{2,4},{7,5},{4,6},{1,7},{14,8},{11,9},{8,1... | collective-permute-start | bytes 786440 | tf_op jit(solution)/shard_map/ppermute | solution.py:414
  89.5 7.9 %collective-permute-start.11 = (f32[8,64,128]{2,1,0:T(8,128)}, f32[8,64,128]{2,1,0:T(8,128)S(1)}, u32[]{:S(2)}, u32[]{:S(2)}) collective-permute-start(f32[8,64,128]{2,1,0:T(8,128)} %get-tuple-element.35.x.rest_0_.own), channel_id=1, source_target_pairs={{3,0},{2,1},{5,2},{4,3},{7,4},{6,5},{1,6},{0,7},{11,8},{10,9},{13,... | collective-permute-start | bytes 786440 | tf_op jit(solution)/shard_map/ppermute | solution.py:414
  97.4 1.9 collective-permute-start.12
  99.4 3.4 collective-permute-start.13
  102.8 1.6 own_slice.9.own
  104.4 1.3 next_slices.9.image
  105.7 5.8 %collective-permute-done.13.fourth = f32[8,64,128]{2,1,0:T(8,128)S(1)} collective-permute-done((f32[8,64,128]{2,1,0:T(8,128)}, f32[8,64,128]{2,1,0:T(8,128)S(1)}, u32[]{:S(2)}, u32[]{:S(2)}) %collective-permute-start.13) | collective-permute-done | bytes 262176 | tf_op jit(solution)/shard_map/ppermute | solution.py:414
  111.5 1.8 products.1
  113.4 25.0 %all_to_all.10.parts = f32[64,8,128]{2,1,0:T(8,128)S(1)} all-to-all(f32[64,8,128]{2,1,0:T(8,128)S(1)} %bitcast.12), channel_id=1, replica_groups=mesh['site'=64,'vec'=8] {'site'}, dimensions={0} | all-to-all | bytes 524288 | tf_op jit(solution)/shard_map/all_to_all | solution.py:429
  138.4 25.0 %all_to_all.11 = f32[64,8,128]{2,1,0:T(8,128)S(1)} all-to-all(f32[64,8,128]{2,1,0:T(8,128)S(1)} %sum_parts.1), channel_id=1, replica_groups=mesh['site'=64,'vec'=8] {'site'}, dimensions={0} | all-to-all | bytes 524288 | tf_op jit(solution)/shard_map/all_to_all | solution.py:433
  164.1 17.1 %all-gather.1 = f32[1280,128]{1,0:T(8,128)S(1)} all-gather(f32[160,128]{1,0:T(8,128)S(1)} %slice.6), channel_id=3, replica_groups=mesh['site'=64,'vec'=8] {'vec'}, dimensions={0}, use_global_device_ids=true | all-gather | bytes 737280 | tf_op jit(solution)/shard_map/all_gather | solution.py:436
  181.2 236.3 %inverse_factor.1.inverse = f32[512,512]{1,0:T(8,128)S(1)} custom-call(f32[8,160,128]{2,1,0:T(8,128)S(1)} %bitcast.13), custom_call_target="tpu_custom_call" | custom-call | flops 7247757312 | bytes 2097152 | tf_op jit(solution)/shard_map/inverse_factor/pallas_call | solution.py:438
  417.5 1.3 basis.1
  420.1 2.2 projected.1
  (36 shorter events, 12.8 us)
Async XLA Ops:
  7.2 156.2 %all-gather.6.cloned.1.call-start = ((), (), s32[]{:S(2)}) async-start(), calls=%async_computation.2 | async-start | bytes 2359296 | tf_op jit(solution)/shard_map/all_gather | solution.py:427
  7.2 1.2 copy-start.1
  8.4 22.5 %copy-start.4 = (s32[8,8]{1,0:T(8,128)S(1)}, s32[8,8]{1,0:T(8,128)}, u32[]{:S(2)}) copy-start(s32[8,8]{1,0:T(8,128)} %near.21) | copy-start | bytes 772
  9.8 22.7 %collective-permute-start.1 = (f32[8,64,128]{2,1,0:T(8,128)S(1)}, f32[8,64,128]{2,1,0:T(8,128)S(1)}, u32[]{:S(2)}, u32[]{:S(2)}) collective-permute-start(f32[8,64,128]{2,1,0:T(8,128)S(1)} %get-tuple-element.24), channel_id=1, source_target_pairs={{0,8},{8,16},{16,24},{24,32},{32,40},{40,48},{48,56},{56,64},{64,7... | collective-permute-start | bytes 786440 | tf_op jit(solution)/shard_map/ppermute | solution.py:338
  14.2 18.3 %collective-permute-start = (f32[8,64,128]{2,1,0:T(8,128)}, f32[8,64,128]{2,1,0:T(8,128)S(1)}, u32[]{:S(2)}, u32[]{:S(2)}) collective-permute-start(f32[8,64,128]{2,1,0:T(8,128)} %bitcast.1.x.rest_0_), channel_id=1, source_target_pairs={{0,504},{8,0},{16,8},{24,16},{32,24},{40,32},{48,40},{56,48},{64,5... | collective-permute-start | bytes 786440 | tf_op jit(solution)/shard_map/ppermute | solution.py:338
  26.2 0.7 copy-start.3
  26.9 0.9 copy-start.5
  33.6 10.3 %collective-permute-start.2 = (f32[8,64,128]{2,1,0:T(8,128)S(1)}, f32[8,64,128]{2,1,0:T(8,128)S(1)}, u32[]{:S(2)}, u32[]{:S(2)}) collective-permute-start(f32[8,64,128]{2,1,0:T(8,128)S(1)} %get-tuple-element.29.x.rest_0_), channel_id=1, source_target_pairs={{0,504},{8,0},{16,8},{24,16},{32,24},{40,32},{48,40},{56,48},{64,5... | collective-permute-start | bytes 786440 | tf_op jit(solution)/shard_map/ppermute | solution.py:338
  39.8 11.2 %collective-permute-start.3 = (f32[8,64,128]{2,1,0:T(8,128)S(1)}, f32[8,64,128]{2,1,0:T(8,128)S(1)}, u32[]{:S(2)}, u32[]{:S(2)}) collective-permute-start(f32[8,64,128]{2,1,0:T(8,128)S(1)} %get-tuple-element.30), channel_id=1, source_target_pairs={{0,8},{8,16},{16,24},{24,32},{32,40},{40,48},{48,56},{56,64},{64,7... | collective-permute-start | bytes 786440 | tf_op jit(solution)/shard_map/ppermute | solution.py:338
  52.4 7.1 %collective-permute-start.4 = (f32[8,64,128]{2,1,0:T(8,128)S(1)}, f32[8,64,128]{2,1,0:T(8,128)S(1)}, u32[]{:S(2)}, u32[]{:S(2)}) collective-permute-start(f32[8,64,128]{2,1,0:T(8,128)S(1)} %get-tuple-element.31.x.rest_0_), channel_id=1, source_target_pairs={{0,504},{8,0},{16,8},{24,16},{32,24},{40,32},{48,40},{56,48},{64,5... | collective-permute-start | bytes 786440 | tf_op jit(solution)/shard_map/ppermute | solution.py:338
  54.4 10.4 %collective-permute-start.5 = (f32[8,64,128]{2,1,0:T(8,128)S(1)}, f32[8,64,128]{2,1,0:T(8,128)S(1)}, u32[]{:S(2)}, u32[]{:S(2)}) collective-permute-start(f32[8,64,128]{2,1,0:T(8,128)S(1)} %get-tuple-element.32), channel_id=1, source_target_pairs={{0,8},{8,16},{16,24},{24,32},{32,40},{40,48},{48,56},{56,64},{64,7... | collective-permute-start | bytes 786440 | tf_op jit(solution)/shard_map/ppermute | solution.py:338
  65.8 7.1 %collective-permute-start.6 = (f32[8,64,128]{2,1,0:T(8,128)S(1)}, f32[8,64,128]{2,1,0:T(8,128)S(1)}, u32[]{:S(2)}, u32[]{:S(2)}) collective-permute-start(f32[8,64,128]{2,1,0:T(8,128)S(1)} %get-tuple-element.33.x), channel_id=1, source_target_pairs={{0,504},{8,0},{16,8},{24,16},{32,24},{40,32},{48,40},{56,48},{64,5... | collective-permute-start | bytes 786440 | tf_op jit(solution)/shard_map/ppermute | solution.py:338
  67.8 10.4 %collective-permute-start.7 = (f32[8,64,128]{2,1,0:T(8,128)S(1)}, f32[8,64,128]{2,1,0:T(8,128)S(1)}, u32[]{:S(2)}, u32[]{:S(2)}) collective-permute-start(f32[8,64,128]{2,1,0:T(8,128)S(1)} %get-tuple-element.34), channel_id=1, source_target_pairs={{0,8},{8,16},{16,24},{24,32},{32,40},{40,48},{48,56},{56,64},{64,7... | collective-permute-start | bytes 786440 | tf_op jit(solution)/shard_map/ppermute | solution.py:338
  79.9 19.5 %collective-permute-start.8 = (f32[8,64,128]{2,1,0:T(8,128)}, f32[8,64,128]{2,1,0:T(8,128)S(1)}, u32[]{:S(2)}, u32[]{:S(2)}) collective-permute-start(f32[8,64,128]{2,1,0:T(8,128)} %get-tuple-element.35.x.rest_0_.own), channel_id=1, source_target_pairs={{0,504},{8,0},{16,8},{24,16},{32,24},{40,32},{48,40},{56,48},{64,5... | collective-permute-start | bytes 786440 | tf_op jit(solution)/shard_map/ppermute | solution.py:338
  81.8 22.6 %collective-permute-start.9 = (f32[8,64,128]{2,1,0:T(8,128)S(1)}, f32[8,64,128]{2,1,0:T(8,128)S(1)}, u32[]{:S(2)}, u32[]{:S(2)}) collective-permute-start(f32[8,64,128]{2,1,0:T(8,128)S(1)} %get-tuple-element.36), channel_id=1, source_target_pairs={{0,8},{8,16},{16,24},{24,32},{32,40},{40,48},{48,56},{56,64},{64,7... | collective-permute-start | bytes 786440 | tf_op jit(solution)/shard_map/ppermute | solution.py:338
  85.1 20.5 %collective-permute-start.10 = (f32[8,64,128]{2,1,0:T(8,128)}, f32[8,64,128]{2,1,0:T(8,128)S(1)}, u32[]{:S(2)}, u32[]{:S(2)}) collective-permute-start(f32[8,64,128]{2,1,0:T(8,128)} %get-tuple-element.35.x.rest_0_.own), channel_id=1, source_target_pairs={{6,0},{3,1},{0,2},{5,3},{2,4},{7,5},{4,6},{1,7},{14,8},{11,9},{8,1... | collective-permute-start | bytes 786440 | tf_op jit(solution)/shard_map/ppermute | solution.py:414
  89.5 16.1 %collective-permute-start.11 = (f32[8,64,128]{2,1,0:T(8,128)}, f32[8,64,128]{2,1,0:T(8,128)S(1)}, u32[]{:S(2)}, u32[]{:S(2)}) collective-permute-start(f32[8,64,128]{2,1,0:T(8,128)} %get-tuple-element.35.x.rest_0_.own), channel_id=1, source_target_pairs={{3,0},{2,1},{5,2},{4,3},{7,4},{6,5},{1,6},{0,7},{11,8},{10,9},{13,... | collective-permute-start | bytes 786440 | tf_op jit(solution)/shard_map/ppermute | solution.py:414
  97.4 8.2 %collective-permute-start.12 = (f32[8,64,128]{2,1,0:T(8,128)}, f32[8,64,128]{2,1,0:T(8,128)S(1)}, u32[]{:S(2)}, u32[]{:S(2)}) collective-permute-start(f32[8,64,128]{2,1,0:T(8,128)} %get-tuple-element.35.x.rest_0_.own), channel_id=1, source_target_pairs={{1,0},{0,1},{3,2},{2,3},{5,4},{4,5},{7,6},{6,7},{9,8},{8,9},{11,10... | collective-permute-start | bytes 786440 | tf_op jit(solution)/shard_map/ppermute | solution.py:414
  99.4 12.1 %collective-permute-start.13 = (f32[8,64,128]{2,1,0:T(8,128)}, f32[8,64,128]{2,1,0:T(8,128)S(1)}, u32[]{:S(2)}, u32[]{:S(2)}) collective-permute-start(f32[8,64,128]{2,1,0:T(8,128)} %get-tuple-element.35.x.rest_0_.own), channel_id=1, source_target_pairs={{5,0},{4,1},{7,2},{6,3},{0,4},{1,5},{2,6},{3,7},{13,8},{12,9},{15,... | collective-permute-start | bytes 786440 | tf_op jit(solution)/shard_map/ppermute | solution.py:414
  113.3 305.5 %all-gather.8.cloned.1.call-start = ((), (), s32[]{:S(2)}) async-start(), calls=%async_computation.3 | async-start | bytes 1179648 | tf_op jit(solution)/shard_map/all_gather | solution.py:435
  181.2 236.3 %copy-start = (f32[4096,128]{1,0:T(8,128)S(1)}, f32[4096,128]{1,0:T(8,128)}, u32[]{:S(2)}) copy-start(f32[4096,128]{1,0:T(8,128)} %all-gather.6.cloned.1.call-done) | copy-start | bytes 6291460
  418.8 1.2 copy-start.2
Sparse Core Ops, SparseCore 0:
  113.4 22.8 all-gather.5
  164.2 24.4 all-gather.7

commit v9 on v8

--- a/solution.py
+++ b/solution.py
@@ -149,10 +149,10 @@
         opposite = (x + chips // 2) % chips
         table.append(
             [
+                2 * opposite + (1 - c if x < chips // 2 else c),
+                2 * ((x + 1) % chips) + 1 - c,
                 2 * ((x - 1 + 2 * c) % chips) + c,
-                2 * ((x + 1) % chips) + 1 - c,
                 2 * x + 1 - c,
-                2 * opposite + (1 - c if x < chips // 2 else c),
             ]
         )
     return table

time: 430 us -> 428 us (level)
  transfers between devices with their start and end apart: 16 -> 16, of which waited for: 7 -> 8; matrix products, arithmetic and copies ran while one was open for 0% -> 0% of each run, Pallas kernels for 58% -> 58%
where the time goes in v9:
time: 428 us; the launch traced here: 427 us
  Pallas kernels  259 us (61%)
  blocking collectives  67.9 us (16%)
  starting transfers between devices  57.5 us (13%)
  waiting for transfers between devices  23.3 us (5%)
  between operations  14.3 us (3%)
  local copies, waits for them, and re-layouts  4.75 us (1%)
    pallas_call x1, Pallas kernels, local(): call(functools.partial(inverse_kernel, count), shape((all_cols, all_cols)...  237 us
    ppermute x10, starting transfers between devices, passed_along(): return lax.ppermute(x, 'site', [(i, (i + by) % size) for i in range(size)])  40.3 us
    all_to_all x1, blocking collectives, local(): lax.all_to_all(summed, 'site', 0, 0, tiled=True).reshape(slices * 8, both)  25.9 us
    all_to_all x1, blocking collectives, local(): lax.all_to_all(products.reshape(slices, 8, both), 'site', 0, 0, tiled=True)  25.4 us
    ppermute x10, waiting for transfers between devices, passed_along(): return lax.ppermute(x, 'site', [(i, (i + by) % size) for i in range(size)])  19.8 us
    ppermute x4, starting transfers between devices, local(): lax.ppermute(current, 'vec', [(table[v][i], v) for v in range(devices)])  17.1 us
    all_gather x1, blocking collectives, local(): gram = lax.all_gather(whole[:kept], 'vec', axis=0)  16.6 us
  transfers between devices with their start and end apart: 16, of which 8 were waited for; matrix products, arithmetic and copies ran while one was open for 0% of the time, Pallas kernels for 58%

profile of v9, /device:TPU:1, one launch (start us, length us, event | category | flops | bytes accessed | tf_op | source)
XLA Modules:
  0.0 427.2 jit_solution(9779195935462717761)
XLA Ops:
  8.4 1.4 backward.1
  9.8 4.4 %collective-permute-start.1 = (f32[8,64,128]{2,1,0:T(8,128)S(1)}, f32[8,64,128]{2,1,0:T(8,128)S(1)}, u32[]{:S(2)}, u32[]{:S(2)}) collective-permute-start(f32[8,64,128]{2,1,0:T(8,128)S(1)} %get-tuple-element.24), channel_id=1, source_target_pairs={{0,8},{8,16},{16,24},{24,32},{32,40},{40,48},{48,56},{56,64},{64,7... | collective-permute-start | bytes 786440 | tf_op jit(solution)/shard_map/ppermute | solution.py:338
  14.2 12.0 %collective-permute-start = (f32[8,64,128]{2,1,0:T(8,128)}, f32[8,64,128]{2,1,0:T(8,128)S(1)}, u32[]{:S(2)}, u32[]{:S(2)}) collective-permute-start(f32[8,64,128]{2,1,0:T(8,128)} %bitcast.1.x.rest_0_), channel_id=1, source_target_pairs={{0,504},{8,0},{16,8},{24,16},{32,24},{40,32},{48,40},{56,48},{64,5... | collective-permute-start | bytes 786440 | tf_op jit(solution)/shard_map/ppermute | solution.py:338
  27.8 3.1 prepare.1
  30.9 1.6 own_slice.5.own
  33.6 6.2 %collective-permute-start.2 = (f32[8,64,128]{2,1,0:T(8,128)S(1)}, f32[8,64,128]{2,1,0:T(8,128)S(1)}, u32[]{:S(2)}, u32[]{:S(2)}) collective-permute-start(f32[8,64,128]{2,1,0:T(8,128)S(1)} %get-tuple-element.29.x.rest_0_), channel_id=1, source_target_pairs={{0,504},{8,0},{16,8},{24,16},{32,24},{40,32},{48,40},{56,48},{64,5... | collective-permute-start | bytes 786440 | tf_op jit(solution)/shard_map/ppermute | solution.py:338
  39.8 1.9 collective-permute-start.3
  43.8 7.2 %collective-permute-done.3.received = f32[8,64,128]{2,1,0:T(8,128)S(1)} collective-permute-done((f32[8,64,128]{2,1,0:T(8,128)S(1)}, f32[8,64,128]{2,1,0:T(8,128)S(1)}, u32[]{:S(2)}, u32[]{:S(2)}) %collective-permute-start.3) | collective-permute-done | bytes 262176 | tf_op jit(solution)/shard_map/ppermute | solution.py:338
  51.0 1.4 next_slices.6
  52.4 1.9 collective-permute-start.4
  54.4 3.4 collective-permute-start.5
  59.5 5.2 %collective-permute-done.5.received = f32[8,64,128]{2,1,0:T(8,128)S(1)} collective-permute-done((f32[8,64,128]{2,1,0:T(8,128)S(1)}, f32[8,64,128]{2,1,0:T(8,128)S(1)}, u32[]{:S(2)}, u32[]{:S(2)}) %collective-permute-start.5) | collective-permute-done | bytes 262176 | tf_op jit(solution)/shard_map/ppermute | solution.py:338
  65.8 1.9 collective-permute-start.6
  67.8 3.4 collective-permute-start.7
  73.0 5.2 %collective-permute-done.7.received = f32[8,64,128]{2,1,0:T(8,128)S(1)} collective-permute-done((f32[8,64,128]{2,1,0:T(8,128)S(1)}, f32[8,64,128]{2,1,0:T(8,128)S(1)}, u32[]{:S(2)}, u32[]{:S(2)}) %collective-permute-start.7) | collective-permute-done | bytes 262176 | tf_op jit(solution)/shard_map/ppermute | solution.py:338
  78.2 1.6 next_slices.8
  79.9 1.9 collective-permute-start.8
  81.8 3.4 collective-permute-start.9
  85.1 4.7 %collective-permute-start.10 = (f32[8,64,128]{2,1,0:T(8,128)}, f32[8,64,128]{2,1,0:T(8,128)S(1)}, u32[]{:S(2)}, u32[]{:S(2)}) collective-permute-start(f32[8,64,128]{2,1,0:T(8,128)} %get-tuple-element.35.x.rest_0_.own), channel_id=1, source_target_pairs={{5,0},{4,1},{7,2},{6,3},{0,4},{1,5},{2,6},{3,7},{13,8},{12,9},{15,... | collective-permute-start | bytes 786440 | tf_op jit(solution)/shard_map/ppermute | solution.py:414
  89.8 7.1 %collective-permute-start.11 = (f32[8,64,128]{2,1,0:T(8,128)}, f32[8,64,128]{2,1,0:T(8,128)S(1)}, u32[]{:S(2)}, u32[]{:S(2)}) collective-permute-start(f32[8,64,128]{2,1,0:T(8,128)} %get-tuple-element.35.x.rest_0_.own), channel_id=1, source_target_pairs={{3,0},{2,1},{5,2},{4,3},{7,4},{6,5},{1,6},{0,7},{11,8},{10,9},{13,... | collective-permute-start | bytes 786440 | tf_op jit(solution)/shard_map/ppermute | solution.py:414
  97.0 3.0 collective-permute-start.12
  100.0 2.3 collective-permute-start.13
  102.3 1.6 own_slice.9.own
  103.9 1.3 next_slices.9.image
  106.1 2.5 collective-permute-done.12.third
  108.6 1.8 products.1
  110.5 25.4 %all_to_all.10.parts = f32[64,8,128]{2,1,0:T(8,128)S(1)} all-to-all(f32[64,8,128]{2,1,0:T(8,128)S(1)} %bitcast.12), channel_id=1, replica_groups=mesh['site'=64,'vec'=8] {'site'}, dimensions={0} | all-to-all | bytes 524288 | tf_op jit(solution)/shard_map/all_to_all | solution.py:429
  135.9 25.9 %all_to_all.11 = f32[64,8,128]{2,1,0:T(8,128)S(1)} all-to-all(f32[64,8,128]{2,1,0:T(8,128)S(1)} %sum_parts.1), channel_id=1, replica_groups=mesh['site'=64,'vec'=8] {'site'}, dimensions={0} | all-to-all | bytes 524288 | tf_op jit(solution)/shard_map/all_to_all | solution.py:433
  162.5 16.6 %all-gather.1 = f32[1280,128]{1,0:T(8,128)S(1)} all-gather(f32[160,128]{1,0:T(8,128)S(1)} %slice.6), channel_id=3, replica_groups=mesh['site'=64,'vec'=8] {'vec'}, dimensions={0}, use_global_device_ids=true | all-gather | bytes 737280 | tf_op jit(solution)/shard_map/all_gather | solution.py:436
  179.1 236.5 %inverse_factor.1.inverse = f32[512,512]{1,0:T(8,128)S(1)} custom-call(f32[8,160,128]{2,1,0:T(8,128)S(1)} %bitcast.13), custom_call_target="tpu_custom_call" | custom-call | flops 7247757312 | bytes 2097152 | tf_op jit(solution)/shard_map/inverse_factor/pallas_call | solution.py:438
  415.7 1.3 basis.1
  418.2 2.1 projected.1
  (36 shorter events, 13.7 us)
Async XLA Ops:
  7.2 154.7 %all-gather.6.cloned.1.call-start = ((), (), s32[]{:S(2)}) async-start(), calls=%async_computation.2 | async-start | bytes 2359296 | tf_op jit(solution)/shard_map/all_gather | solution.py:427
  7.2 1.2 copy-start.1
  8.4 22.5 %copy-start.4 = (s32[8,8]{1,0:T(8,128)S(1)}, s32[8,8]{1,0:T(8,128)}, u32[]{:S(2)}) copy-start(s32[8,8]{1,0:T(8,128)} %near.21) | copy-start | bytes 772
  9.8 22.7 %collective-permute-start.1 = (f32[8,64,128]{2,1,0:T(8,128)S(1)}, f32[8,64,128]{2,1,0:T(8,128)S(1)}, u32[]{:S(2)}, u32[]{:S(2)}) collective-permute-start(f32[8,64,128]{2,1,0:T(8,128)S(1)} %get-tuple-element.24), channel_id=1, source_target_pairs={{0,8},{8,16},{16,24},{24,32},{32,40},{40,48},{48,56},{56,64},{64,7... | collective-permute-start | bytes 786440 | tf_op jit(solution)/shard_map/ppermute | solution.py:338
  14.2 18.3 %collective-permute-start = (f32[8,64,128]{2,1,0:T(8,128)}, f32[8,64,128]{2,1,0:T(8,128)S(1)}, u32[]{:S(2)}, u32[]{:S(2)}) collective-permute-start(f32[8,64,128]{2,1,0:T(8,128)} %bitcast.1.x.rest_0_), channel_id=1, source_target_pairs={{0,504},{8,0},{16,8},{24,16},{32,24},{40,32},{48,40},{56,48},{64,5... | collective-permute-start | bytes 786440 | tf_op jit(solution)/shard_map/ppermute | solution.py:338
  26.2 0.7 copy-start.3
  26.9 0.9 copy-start.5
  33.6 10.3 %collective-permute-start.2 = (f32[8,64,128]{2,1,0:T(8,128)S(1)}, f32[8,64,128]{2,1,0:T(8,128)S(1)}, u32[]{:S(2)}, u32[]{:S(2)}) collective-permute-start(f32[8,64,128]{2,1,0:T(8,128)S(1)} %get-tuple-element.29.x.rest_0_), channel_id=1, source_target_pairs={{0,504},{8,0},{16,8},{24,16},{32,24},{40,32},{48,40},{56,48},{64,5... | collective-permute-start | bytes 786440 | tf_op jit(solution)/shard_map/ppermute | solution.py:338
  39.8 11.2 %collective-permute-start.3 = (f32[8,64,128]{2,1,0:T(8,128)S(1)}, f32[8,64,128]{2,1,0:T(8,128)S(1)}, u32[]{:S(2)}, u32[]{:S(2)}) collective-permute-start(f32[8,64,128]{2,1,0:T(8,128)S(1)} %get-tuple-element.30), channel_id=1, source_target_pairs={{0,8},{8,16},{16,24},{24,32},{32,40},{40,48},{48,56},{56,64},{64,7... | collective-permute-start | bytes 786440 | tf_op jit(solution)/shard_map/ppermute | solution.py:338
  52.4 7.1 %collective-permute-start.4 = (f32[8,64,128]{2,1,0:T(8,128)S(1)}, f32[8,64,128]{2,1,0:T(8,128)S(1)}, u32[]{:S(2)}, u32[]{:S(2)}) collective-permute-start(f32[8,64,128]{2,1,0:T(8,128)S(1)} %get-tuple-element.31.x.rest_0_), channel_id=1, source_target_pairs={{0,504},{8,0},{16,8},{24,16},{32,24},{40,32},{48,40},{56,48},{64,5... | collective-permute-start | bytes 786440 | tf_op jit(solution)/shard_map/ppermute | solution.py:338
  54.4 10.4 %collective-permute-start.5 = (f32[8,64,128]{2,1,0:T(8,128)S(1)}, f32[8,64,128]{2,1,0:T(8,128)S(1)}, u32[]{:S(2)}, u32[]{:S(2)}) collective-permute-start(f32[8,64,128]{2,1,0:T(8,128)S(1)} %get-tuple-element.32), channel_id=1, source_target_pairs={{0,8},{8,16},{16,24},{24,32},{32,40},{40,48},{48,56},{56,64},{64,7... | collective-permute-start | bytes 786440 | tf_op jit(solution)/shard_map/ppermute | solution.py:338
  65.8 7.1 %collective-permute-start.6 = (f32[8,64,128]{2,1,0:T(8,128)S(1)}, f32[8,64,128]{2,1,0:T(8,128)S(1)}, u32[]{:S(2)}, u32[]{:S(2)}) collective-permute-start(f32[8,64,128]{2,1,0:T(8,128)S(1)} %get-tuple-element.33.x), channel_id=1, source_target_pairs={{0,504},{8,0},{16,8},{24,16},{32,24},{40,32},{48,40},{56,48},{64,5... | collective-permute-start | bytes 786440 | tf_op jit(solution)/shard_map/ppermute | solution.py:338
  67.8 10.4 %collective-permute-start.7 = (f32[8,64,128]{2,1,0:T(8,128)S(1)}, f32[8,64,128]{2,1,0:T(8,128)S(1)}, u32[]{:S(2)}, u32[]{:S(2)}) collective-permute-start(f32[8,64,128]{2,1,0:T(8,128)S(1)} %get-tuple-element.34), channel_id=1, source_target_pairs={{0,8},{8,16},{16,24},{24,32},{32,40},{40,48},{48,56},{56,64},{64,7... | collective-permute-start | bytes 786440 | tf_op jit(solution)/shard_map/ppermute | solution.py:338
  79.9 20.1 %collective-permute-start.8 = (f32[8,64,128]{2,1,0:T(8,128)}, f32[8,64,128]{2,1,0:T(8,128)S(1)}, u32[]{:S(2)}, u32[]{:S(2)}) collective-permute-start(f32[8,64,128]{2,1,0:T(8,128)} %get-tuple-element.35.x.rest_0_.own), channel_id=1, source_target_pairs={{0,504},{8,0},{16,8},{24,16},{32,24},{40,32},{48,40},{56,48},{64,5... | collective-permute-start | bytes 786440 | tf_op jit(solution)/shard_map/ppermute | solution.py:338
  81.8 22.1 %collective-permute-start.9 = (f32[8,64,128]{2,1,0:T(8,128)S(1)}, f32[8,64,128]{2,1,0:T(8,128)S(1)}, u32[]{:S(2)}, u32[]{:S(2)}) collective-permute-start(f32[8,64,128]{2,1,0:T(8,128)S(1)} %get-tuple-element.36), channel_id=1, source_target_pairs={{0,8},{8,16},{16,24},{24,32},{32,40},{40,48},{48,56},{56,64},{64,7... | collective-permute-start | bytes 786440 | tf_op jit(solution)/shard_map/ppermute | solution.py:338
  85.1 20.0 %collective-permute-start.10 = (f32[8,64,128]{2,1,0:T(8,128)}, f32[8,64,128]{2,1,0:T(8,128)S(1)}, u32[]{:S(2)}, u32[]{:S(2)}) collective-permute-start(f32[8,64,128]{2,1,0:T(8,128)} %get-tuple-element.35.x.rest_0_.own), channel_id=1, source_target_pairs={{5,0},{4,1},{7,2},{6,3},{0,4},{1,5},{2,6},{3,7},{13,8},{12,9},{15,... | collective-permute-start | bytes 786440 | tf_op jit(solution)/shard_map/ppermute | solution.py:414
  89.8 16.3 %collective-permute-start.11 = (f32[8,64,128]{2,1,0:T(8,128)}, f32[8,64,128]{2,1,0:T(8,128)S(1)}, u32[]{:S(2)}, u32[]{:S(2)}) collective-permute-start(f32[8,64,128]{2,1,0:T(8,128)} %get-tuple-element.35.x.rest_0_.own), channel_id=1, source_target_pairs={{3,0},{2,1},{5,2},{4,3},{7,4},{6,5},{1,6},{0,7},{11,8},{10,9},{13,... | collective-permute-start | bytes 786440 | tf_op jit(solution)/shard_map/ppermute | solution.py:414
  97.0 11.6 %collective-permute-start.12 = (f32[8,64,128]{2,1,0:T(8,128)}, f32[8,64,128]{2,1,0:T(8,128)S(1)}, u32[]{:S(2)}, u32[]{:S(2)}) collective-permute-start(f32[8,64,128]{2,1,0:T(8,128)} %get-tuple-element.35.x.rest_0_.own), channel_id=1, source_target_pairs={{6,0},{3,1},{0,2},{5,3},{2,4},{7,5},{4,6},{1,7},{14,8},{11,9},{8,1... | collective-permute-start | bytes 786440 | tf_op jit(solution)/shard_map/ppermute | solution.py:414
  100.0 8.6 %collective-permute-start.13 = (f32[8,64,128]{2,1,0:T(8,128)}, f32[8,64,128]{2,1,0:T(8,128)S(1)}, u32[]{:S(2)}, u32[]{:S(2)}) collective-permute-start(f32[8,64,128]{2,1,0:T(8,128)} %get-tuple-element.35.x.rest_0_.own), channel_id=1, source_target_pairs={{1,0},{0,1},{3,2},{2,3},{5,4},{4,5},{7,6},{6,7},{9,8},{8,9},{11,10... | collective-permute-start | bytes 786440 | tf_op jit(solution)/shard_map/ppermute | solution.py:414
  110.4 306.6 %all-gather.8.cloned.1.call-start = ((), (), s32[]{:S(2)}) async-start(), calls=%async_computation.3 | async-start | bytes 1179648 | tf_op jit(solution)/shard_map/all_gather | solution.py:435
  179.1 236.6 %copy-start = (f32[4096,128]{1,0:T(8,128)S(1)}, f32[4096,128]{1,0:T(8,128)}, u32[]{:S(2)}) copy-start(f32[4096,128]{1,0:T(8,128)} %all-gather.6.cloned.1.call-done) | copy-start | bytes 6291460
  417.0 1.2 copy-start.2
Sparse Core Ops, SparseCore 0:
  110.5 24.4 all-gather.5
  162.6 25.0 all-gather.7

commit v10 on v8

--- a/solution.py
+++ b/solution.py
@@ -46,6 +46,11 @@
 def split(x):
     high = x.astype(bf16)
     return high, (x - high.astype(f32)).astype(bf16)
+
+
+def repeat_kernel(start, x, out):
+    for i in range(out.shape[0]):
+        out[i] = x[start : start + out.shape[1]]
 
 
 NT = (((1,), (1,)), ((), ()))
@@ -410,9 +415,9 @@
 
     image = apply(current, back, "image", current)
     table = senders(devices)
-    others = [
-        lax.ppermute(current, "vec", [(table[v][i], v) for v in range(devices)]) for i in range(4)
-    ]
+    others = [None] * 4
+    for i in (3, 1, 0, 2):
+        others[i] = lax.ppermute(current, "vec", [(table[v][i], v) for v in range(devices)])
     kept = 5 * cols // 2
     products = call(
         product_kernel,
@@ -432,7 +437,15 @@
     )(parts)
     whole = lax.all_to_all(summed, "site", 0, 0, tiled=True).reshape(slices * 8, both)
     whole, everything = lax.optimization_barrier((whole, everything))
-    moments = lax.all_gather(whole[kept : kept + all_cols // 2], "vec", axis=0)
+    copies = call(
+        functools.partial(repeat_kernel, kept),
+        shape((devices, kept + 13 * 8, both), f32),
+        0,
+        1,
+        moved=1 << 21,
+        name="repeat",
+    )(whole)
+    moments = lax.all_to_all(copies, "vec", 0, 0, tiled=True)
     gram = lax.all_gather(whole[:kept], "vec", axis=0)
 
     inverse = call(

time: 430 us -> 444 us (1.033)
  starting transfers between devices: 58 us -> 83.4 us
  blocking collectives: 67 us -> 48.3 us
  waiting for transfers between devices: 25.7 us -> 36 us
    all_to_all x1 -> x0, blocking collectives: 25 us -> none  [local(): lax.all_to_all(summed, 'site', 0, 0, tiled=True).reshape(slices * 8, both)]
    all_to_all x0 -> x2, waiting for transfers between devices: none -> 18.6 us  [the longest x1 18.6 us: local(): lax.all_to_all(summed, 'site', 0, 0, tiled=True).reshape(slices * 8, both)]
    all_to_all x0 -> x2, starting transfers between devices: none -> 13.7 us  [the longest x1 6.92 us: local(): lax.all_to_all(summed, 'site', 0, 0, tiled=True).reshape(slices * 8, both)]
    ppermute x10, starting transfers between devices: 40.3 us -> 52.5 us  [passed_along(): return lax.ppermute(x, 'site', [(i, (i + by) % size) for i in range(size)])]
    ppermute x10, waiting for transfers between devices: 19.8 us -> 12.1 us  [passed_along(): return lax.ppermute(x, 'site', [(i, (i + by) % size) for i in range(size)])]
    all_gather x1, blocking collectives: 17.1 us -> 24.3 us  [local(): gram = lax.all_gather(whole[:kept], 'vec', axis=0)]
  transfers between devices with their start and end apart: 16 -> 17, of which waited for: 7 -> 10; matrix products, arithmetic and copies ran while one was open for 0% -> 0% of each run, Pallas kernels for 58% -> 56%
where the time goes in v10:
time: 444 us
  Pallas kernels  259 us (58%)
  starting transfers between devices  83.4 us (19%)
  blocking collectives  48.3 us (11%)
  waiting for transfers between devices  36 us (8%)
  between operations  14.3 us (3%)
    pallas_call x1, Pallas kernels, local(): call(functools.partial(inverse_kernel, count), shape((all_cols, all_cols)...  236 us
    ppermute x10, starting transfers between devices, passed_along(): return lax.ppermute(x, 'site', [(i, (i + by) % size) for i in range(size)])  52.5 us
    all_gather x1, blocking collectives, local(): gram = lax.all_gather(whole[:kept], 'vec', axis=0)  24.3 us
    all_to_all x1, blocking collectives, local(): lax.all_to_all(products.reshape(slices, 8, both), 'site', 0, 0, tiled=True)  24 us
    all_to_all x1, waiting for transfers between devices, local(): lax.all_to_all(summed, 'site', 0, 0, tiled=True).reshape(slices * 8, both)  18.6 us
    ppermute x4, starting transfers between devices, local(): lax.ppermute(current, 'vec', [(table[v][i], v) for v in range(devices)])  17.2 us
    ppermute x10, waiting for transfers between devices, passed_along(): return lax.ppermute(x, 'site', [(i, (i + by) % size) for i in range(size)])  12.1 us
  transfers between devices with their start and end apart: 17, of which 10 were waited for; matrix products, arithmetic and copies ran while one was open for 0% of the time, Pallas kernels for 56%

profile of v10, /device:TPU:1, one launch (start us, length us, event | category | flops | bytes accessed | tf_op | source)
XLA Modules:
  0.0 443.6 jit_solution(11152312184518877249)
XLA Ops:
  7.2 14.4 %collective-permute-start = (f32[8,64,128]{2,1,0:T(8,128)}, f32[8,64,128]{2,1,0:T(8,128)S(1)}, u32[]{:S(2)}, u32[]{:S(2)}) collective-permute-start(f32[8,64,128]{2,1,0:T(8,128)} %bitcast.9), channel_id=1, source_target_pairs={{0,504},{8,0},{16,8},{24,16},{32,24},{40,32},{48,40},{56,48},{64,5... | collective-permute-start | bytes 786440 | tf_op jit(solution)/shard_map/ppermute | solution.py:343
  24.2 1.9 collective-permute-start.1
  26.1 3.1 prepare.1
  30.5 5.8 %collective-permute-done.1.received = f32[8,64,128]{2,1,0:T(8,128)S(1)} collective-permute-done((f32[8,64,128]{2,1,0:T(8,128)S(1)}, f32[8,64,128]{2,1,0:T(8,128)S(1)}, u32[]{:S(2)}, u32[]{:S(2)}) %collective-permute-start.1) | collective-permute-done | bytes 262176 | tf_op jit(solution)/shard_map/ppermute | solution.py:343
  37.3 1.9 collective-permute-start.3
  39.2 6.7 %collective-permute-start.2 = (f32[8,64,128]{2,1,0:T(8,128)S(1)}, f32[8,64,128]{2,1,0:T(8,128)S(1)}, u32[]{:S(2)}, u32[]{:S(2)}) collective-permute-start(f32[8,64,128]{2,1,0:T(8,128)S(1)} %get-tuple-element.29.x.rest_0_), channel_id=1, source_target_pairs={{0,504},{8,0},{16,8},{24,16},{32,24},{40,32},{48,40},{56,48},{64,5... | collective-permute-start | bytes 786440 | tf_op jit(solution)/shard_map/ppermute | solution.py:343
  47.1 1.3 collective-permute-done.3.received
  50.3 1.9 collective-permute-start.5
  52.2 7.6 %collective-permute-start.4 = (f32[8,64,128]{2,1,0:T(8,128)S(1)}, f32[8,64,128]{2,1,0:T(8,128)S(1)}, u32[]{:S(2)}, u32[]{:S(2)}) collective-permute-start(f32[8,64,128]{2,1,0:T(8,128)S(1)} %get-tuple-element.31.x.rest_0_), channel_id=1, source_target_pairs={{0,504},{8,0},{16,8},{24,16},{32,24},{40,32},{48,40},{56,48},{64,5... | collective-permute-start | bytes 786440 | tf_op jit(solution)/shard_map/ppermute | solution.py:343
  61.6 1.5 collective-permute-done.4.ahead
  64.2 1.9 collective-permute-start.7
  66.1 7.1 %collective-permute-start.6 = (f32[8,64,128]{2,1,0:T(8,128)S(1)}, f32[8,64,128]{2,1,0:T(8,128)S(1)}, u32[]{:S(2)}, u32[]{:S(2)}) collective-permute-start(f32[8,64,128]{2,1,0:T(8,128)S(1)} %get-tuple-element.33.x), channel_id=1, source_target_pairs={{0,504},{8,0},{16,8},{24,16},{32,24},{40,32},{48,40},{56,48},{64,5... | collective-permute-start | bytes 786440 | tf_op jit(solution)/shard_map/ppermute | solution.py:343
  75.0 1.5 collective-permute-done.6.ahead
  76.5 1.6 next_slices.8
  78.1 1.9 collective-permute-start.9
  80.1 7.1 %collective-permute-start.8 = (f32[8,64,128]{2,1,0:T(8,128)}, f32[8,64,128]{2,1,0:T(8,128)S(1)}, u32[]{:S(2)}, u32[]{:S(2)}) collective-permute-start(f32[8,64,128]{2,1,0:T(8,128)} %get-tuple-element.35.x.rest_0_.own), channel_id=1, source_target_pairs={{0,504},{8,0},{16,8},{24,16},{32,24},{40,32},{48,40},{56,48},{64,5... | collective-permute-start | bytes 786440 | tf_op jit(solution)/shard_map/ppermute | solution.py:343
  87.2 4.6 %collective-permute-start.13 = (f32[8,64,128]{2,1,0:T(8,128)}, f32[8,64,128]{2,1,0:T(8,128)S(1)}, u32[]{:S(2)}, u32[]{:S(2)}) collective-permute-start(f32[8,64,128]{2,1,0:T(8,128)} %get-tuple-element.35.x.rest_0_.own), channel_id=1, source_target_pairs={{5,0},{4,1},{7,2},{6,3},{0,4},{1,5},{2,6},{3,7},{13,8},{12,9},{15,... | collective-permute-start | bytes 786440 | tf_op jit(solution)/shard_map/ppermute | solution.py:420
  91.8 7.8 %collective-permute-start.12 = (f32[8,64,128]{2,1,0:T(8,128)}, f32[8,64,128]{2,1,0:T(8,128)S(1)}, u32[]{:S(2)}, u32[]{:S(2)}) collective-permute-start(f32[8,64,128]{2,1,0:T(8,128)} %get-tuple-element.35.x.rest_0_.own), channel_id=1, source_target_pairs={{1,0},{0,1},{3,2},{2,3},{5,4},{4,5},{7,6},{6,7},{9,8},{8,9},{11,10... | collective-permute-start | bytes 786440 | tf_op jit(solution)/shard_map/ppermute | solution.py:420
  99.7 2.8 collective-permute-start.11
  102.5 1.9 collective-permute-start.10
  104.4 1.6 own_slice.9.own
  107.3 3.4 collective-permute-done.11.second
  110.6 1.9 collective-permute-done.10.first
  112.5 1.8 products.1
  114.4 24.0 %all_to_all.15.parts = f32[64,8,128]{2,1,0:T(8,128)S(1)} all-to-all(f32[64,8,128]{2,1,0:T(8,128)S(1)} %bitcast.16), channel_id=1, replica_groups=mesh['site'=64,'vec'=8] {'site'}, dimensions={0} | all-to-all | bytes 524288 | tf_op jit(solution)/shard_map/all_to_all | solution.py:434
  139.2 6.9 %all-to-all-start.1 = ((f32[64,8,128]{2,1,0:T(8,128)}), f32[64,8,128]{2,1,0:T(8,128)S(1)}, u32[]{:S(2)}, u32[]{:S(2)}) async-start(f32[64,8,128]{2,1,0:T(8,128)} %sum_parts.1), calls=%async_computation.1 | async-start | bytes 524288 | tf_op jit(solution)/shard_map/all_to_all | solution.py:438
  146.1 18.6 %all-to-all-done.1 = f32[64,8,128]{2,1,0:T(8,128)S(1)} async-done(((f32[64,8,128]{2,1,0:T(8,128)}), f32[64,8,128]{2,1,0:T(8,128)S(1)}, u32[]{:S(2)}, u32[]{:S(2)}) %all-to-all-start.1) | async-done | bytes 262176 | tf_op jit(solution)/shard_map/all_to_all | solution.py:438
  165.9 6.8 %all-to-all-start.2 = ((f32[8,264,128]{2,1,0:T(8,128)}), f32[8,264,128]{2,1,0:T(8,128)S(1)}, u32[]{:S(2)}, u32[]{:S(2)}) async-start(f32[8,264,128]{2,1,0:T(8,128)} %repeat.1), calls=%async_computation.2 | async-start | bytes 2162688 | tf_op jit(solution)/shard_map/all_to_all | solution.py:448
  172.6 24.3 %all-gather.1 = f32[1280,128]{1,0:T(8,128)S(1)} all-gather(f32[160,128]{1,0:T(8,128)S(1)} %slice.3), channel_id=3, replica_groups=mesh['site'=64,'vec'=8] {'vec'}, dimensions={0}, use_global_device_ids=true | all-gather | bytes 737280 | tf_op jit(solution)/shard_map/all_gather | solution.py:449
  196.9 236.3 %inverse_factor.1.inverse = f32[512,512]{1,0:T(8,128)S(1)} custom-call(f32[8,160,128]{2,1,0:T(8,128)S(1)} %bitcast.17), custom_call_target="tpu_custom_call" | custom-call | flops 7247757312 | bytes 2097152 | tf_op jit(solution)/shard_map/inverse_factor/pallas_call | solution.py:451
  433.3 1.3 basis.1
  434.6 2.2 projected.1
  (36 shorter events, 15.7 us)
Async XLA Ops:
  7.2 157.6 %all-gather.4.cloned.1.call-start = ((), (), s32[]{:S(2)}) async-start(), calls=%async_computation.3 | async-start | bytes 2359296 | tf_op jit(solution)/shard_map/all_gather | solution.py:432
  7.2 23.3 %collective-permute-start = (f32[8,64,128]{2,1,0:T(8,128)}, f32[8,64,128]{2,1,0:T(8,128)S(1)}, u32[]{:S(2)}, u32[]{:S(2)}) collective-permute-start(f32[8,64,128]{2,1,0:T(8,128)} %bitcast.9), channel_id=1, source_target_pairs={{0,504},{8,0},{16,8},{24,16},{32,24},{40,32},{48,40},{56,48},{64,5... | collective-permute-start | bytes 786440 | tf_op jit(solution)/shard_map/ppermute | solution.py:343
  21.6 1.0 copy-start
  22.6 1.2 copy-start.3
  23.8 2.3 copy-start.4
  23.8 2.3 copy-start.5
  23.8 5.5 %copy-start.1 = (f32[8,128,64]{1,2,0:T(8,128)S(1)}, f32[8,128,64]{1,2,0:T(8,128)}, u32[]{:S(2)}) copy-start(f32[8,128,64]{1,2,0:T(8,128)} %param.7) | copy-start | bytes 786436
  24.2 12.1 %collective-permute-start.1 = (f32[8,64,128]{2,1,0:T(8,128)S(1)}, f32[8,64,128]{2,1,0:T(8,128)S(1)}, u32[]{:S(2)}, u32[]{:S(2)}) collective-permute-start(f32[8,64,128]{2,1,0:T(8,128)S(1)} %get-tuple-element.24), channel_id=1, source_target_pairs={{0,8},{8,16},{16,24},{24,32},{32,40},{40,48},{48,56},{56,64},{64,7... | collective-permute-start | bytes 786440 | tf_op jit(solution)/shard_map/ppermute | solution.py:343
  37.3 11.1 %collective-permute-start.3 = (f32[8,64,128]{2,1,0:T(8,128)S(1)}, f32[8,64,128]{2,1,0:T(8,128)S(1)}, u32[]{:S(2)}, u32[]{:S(2)}) collective-permute-start(f32[8,64,128]{2,1,0:T(8,128)S(1)} %get-tuple-element.30), channel_id=1, source_target_pairs={{0,8},{8,16},{16,24},{24,32},{32,40},{40,48},{48,56},{56,64},{64,7... | collective-permute-start | bytes 786440 | tf_op jit(solution)/shard_map/ppermute | solution.py:343
  39.2 10.0 %collective-permute-start.2 = (f32[8,64,128]{2,1,0:T(8,128)S(1)}, f32[8,64,128]{2,1,0:T(8,128)S(1)}, u32[]{:S(2)}, u32[]{:S(2)}) collective-permute-start(f32[8,64,128]{2,1,0:T(8,128)S(1)} %get-tuple-element.29.x.rest_0_), channel_id=1, source_target_pairs={{0,504},{8,0},{16,8},{24,16},{32,24},{40,32},{48,40},{56,48},{64,5... | collective-permute-start | bytes 786440 | tf_op jit(solution)/shard_map/ppermute | solution.py:343
  50.3 11.3 %collective-permute-start.5 = (f32[8,64,128]{2,1,0:T(8,128)S(1)}, f32[8,64,128]{2,1,0:T(8,128)S(1)}, u32[]{:S(2)}, u32[]{:S(2)}) collective-permute-start(f32[8,64,128]{2,1,0:T(8,128)S(1)} %get-tuple-element.32), channel_id=1, source_target_pairs={{0,8},{8,16},{16,24},{24,32},{32,40},{40,48},{48,56},{56,64},{64,7... | collective-permute-start | bytes 786440 | tf_op jit(solution)/shard_map/ppermute | solution.py:343
  52.2 10.9 %collective-permute-start.4 = (f32[8,64,128]{2,1,0:T(8,128)S(1)}, f32[8,64,128]{2,1,0:T(8,128)S(1)}, u32[]{:S(2)}, u32[]{:S(2)}) collective-permute-start(f32[8,64,128]{2,1,0:T(8,128)S(1)} %get-tuple-element.31.x.rest_0_), channel_id=1, source_target_pairs={{0,504},{8,0},{16,8},{24,16},{32,24},{40,32},{48,40},{56,48},{64,5... | collective-permute-start | bytes 786440 | tf_op jit(solution)/shard_map/ppermute | solution.py:343
  64.2 10.9 %collective-permute-start.7 = (f32[8,64,128]{2,1,0:T(8,128)S(1)}, f32[8,64,128]{2,1,0:T(8,128)S(1)}, u32[]{:S(2)}, u32[]{:S(2)}) collective-permute-start(f32[8,64,128]{2,1,0:T(8,128)S(1)} %get-tuple-element.34), channel_id=1, source_target_pairs={{0,8},{8,16},{16,24},{24,32},{32,40},{40,48},{48,56},{56,64},{64,7... | collective-permute-start | bytes 786440 | tf_op jit(solution)/shard_map/ppermute | solution.py:343
  66.1 10.4 %collective-permute-start.6 = (f32[8,64,128]{2,1,0:T(8,128)S(1)}, f32[8,64,128]{2,1,0:T(8,128)S(1)}, u32[]{:S(2)}, u32[]{:S(2)}) collective-permute-start(f32[8,64,128]{2,1,0:T(8,128)S(1)} %get-tuple-element.33.x), channel_id=1, source_target_pairs={{0,504},{8,0},{16,8},{24,16},{32,24},{40,32},{48,40},{56,48},{64,5... | collective-permute-start | bytes 786440 | tf_op jit(solution)/shard_map/ppermute | solution.py:343
  78.1 24.3 %collective-permute-start.9 = (f32[8,64,128]{2,1,0:T(8,128)S(1)}, f32[8,64,128]{2,1,0:T(8,128)S(1)}, u32[]{:S(2)}, u32[]{:S(2)}) collective-permute-start(f32[8,64,128]{2,1,0:T(8,128)S(1)} %get-tuple-element.36), channel_id=1, source_target_pairs={{0,8},{8,16},{16,24},{24,32},{32,40},{40,48},{48,56},{56,64},{64,7... | collective-permute-start | bytes 786440 | tf_op jit(solution)/shard_map/ppermute | solution.py:343
  80.1 25.9 %collective-permute-start.8 = (f32[8,64,128]{2,1,0:T(8,128)}, f32[8,64,128]{2,1,0:T(8,128)S(1)}, u32[]{:S(2)}, u32[]{:S(2)}) collective-permute-start(f32[8,64,128]{2,1,0:T(8,128)} %get-tuple-element.35.x.rest_0_.own), channel_id=1, source_target_pairs={{0,504},{8,0},{16,8},{24,16},{32,24},{40,32},{48,40},{56,48},{64,5... | collective-permute-start | bytes 786440 | tf_op jit(solution)/shard_map/ppermute | solution.py:343
  87.2 20.1 %collective-permute-start.13 = (f32[8,64,128]{2,1,0:T(8,128)}, f32[8,64,128]{2,1,0:T(8,128)S(1)}, u32[]{:S(2)}, u32[]{:S(2)}) collective-permute-start(f32[8,64,128]{2,1,0:T(8,128)} %get-tuple-element.35.x.rest_0_.own), channel_id=1, source_target_pairs={{5,0},{4,1},{7,2},{6,3},{0,4},{1,5},{2,6},{3,7},{13,8},{12,9},{15,... | collective-permute-start | bytes 786440 | tf_op jit(solution)/shard_map/ppermute | solution.py:420
  91.8 15.4 %collective-permute-start.12 = (f32[8,64,128]{2,1,0:T(8,128)}, f32[8,64,128]{2,1,0:T(8,128)S(1)}, u32[]{:S(2)}, u32[]{:S(2)}) collective-permute-start(f32[8,64,128]{2,1,0:T(8,128)} %get-tuple-element.35.x.rest_0_.own), channel_id=1, source_target_pairs={{1,0},{0,1},{3,2},{2,3},{5,4},{4,5},{7,6},{6,7},{9,8},{8,9},{11,10... | collective-permute-start | bytes 786440 | tf_op jit(solution)/shard_map/ppermute | solution.py:420
  99.7 11.0 %collective-permute-start.11 = (f32[8,64,128]{2,1,0:T(8,128)}, f32[8,64,128]{2,1,0:T(8,128)S(1)}, u32[]{:S(2)}, u32[]{:S(2)}) collective-permute-start(f32[8,64,128]{2,1,0:T(8,128)} %get-tuple-element.35.x.rest_0_.own), channel_id=1, source_target_pairs={{3,0},{2,1},{5,2},{4,3},{7,4},{6,5},{1,6},{0,7},{11,8},{10,9},{13,... | collective-permute-start | bytes 786440 | tf_op jit(solution)/shard_map/ppermute | solution.py:420
  102.5 10.0 %collective-permute-start.10 = (f32[8,64,128]{2,1,0:T(8,128)}, f32[8,64,128]{2,1,0:T(8,128)S(1)}, u32[]{:S(2)}, u32[]{:S(2)}) collective-permute-start(f32[8,64,128]{2,1,0:T(8,128)} %get-tuple-element.35.x.rest_0_.own), channel_id=1, source_target_pairs={{6,0},{3,1},{0,2},{5,3},{2,4},{7,5},{4,6},{1,7},{14,8},{11,9},{8,1... | collective-permute-start | bytes 786440 | tf_op jit(solution)/shard_map/ppermute | solution.py:420
  139.2 25.6 %all-to-all-start.1 = ((f32[64,8,128]{2,1,0:T(8,128)}), f32[64,8,128]{2,1,0:T(8,128)S(1)}, u32[]{:S(2)}, u32[]{:S(2)}) async-start(f32[64,8,128]{2,1,0:T(8,128)} %sum_parts.1), calls=%async_computation.1 | async-start | bytes 524288 | tf_op jit(solution)/shard_map/all_to_all | solution.py:438
  165.9 268.7 %all-to-all-start.2 = ((f32[8,264,128]{2,1,0:T(8,128)}), f32[8,264,128]{2,1,0:T(8,128)S(1)}, u32[]{:S(2)}, u32[]{:S(2)}) async-start(f32[8,264,128]{2,1,0:T(8,128)} %repeat.1), calls=%async_computation.2 | async-start | bytes 2162688 | tf_op jit(solution)/shard_map/all_to_all | solution.py:448
  196.9 236.3 %copy-start.2 = (f32[4096,128]{1,0:T(8,128)S(1)}, f32[4096,128]{1,0:T(8,128)}, u32[]{:S(2)}) copy-start(f32[4096,128]{1,0:T(8,128)} %all-gather.4.cloned.1.call-done) | copy-start | bytes 6291460
Sparse Core Ops, SparseCore 0:
  114.5 22.1 all-gather.3

commit v11 on v8

--- a/solution.py
+++ b/solution.py
@@ -213,14 +213,13 @@
 
 
 def multiply(a, b, dims):
-    ah, al = split(a)
-    bh, bl = split(b)
+    (ah, al), (bh, bl) = a, b
     dot = functools.partial(lax.dot_general, dimension_numbers=dims, preferred_element_type=f32)
     return dot(ah, bh) + (dot(al, bh) + dot(ah, bl))
 
 
-def inverse_kernel(count, gathered, out, scaled, factor):
-    n = out.shape[0]
+def inverse_kernel(count, gathered, high, low, scaled, factor):
+    n = high.shape[0]
     half = gathered.shape[2] // 2
     for v, line in enumerate(lines_of(gathered)):
         scaled[v * half : (v + 1) * half, :] = line * (1.0 / count)
@@ -249,7 +248,7 @@
         s2 = cut(scaled[:, mid:])
         top = cut(factor[:mid, :mid])
         side = cut(factor[mid:, :mid])
-        low = cut(factor[mid:, mid:])
+        corner = cut(factor[mid:, mid:])
         lower = cut(factor[mid:, :])
 
         def part(x, piece):
@@ -260,7 +259,7 @@
         t22 = cut(product(lower, s2, NN))
         e11 = product(t11, top, NT) - small_unit
         e21 = product(t21, top, NT)
-        e22 = product(t21, side, NT) + product(t22, low, NT) - small_unit
+        e22 = product(t21, side, NT) + product(t22, corner, NT) - small_unit
         p11, p22 = small_weight * e11, small_weight * e22
         size = jnp.sum(p11 * p11 + p22 * p22 + e21 * e21)
         p11, p21, p22 = cut(p11), cut(e21), cut(p22)
@@ -268,17 +267,11 @@
         factor[mid:, :mid] = factor[mid:, :mid] - (
             product(p21, top, NN) + product(p22, side, NN)
         )
-        factor[mid:, mid:] = factor[mid:, mid:] - product(p22, low, NN)
+        factor[mid:, mid:] = factor[mid:, mid:] - product(p22, corner, NN)
         return size
 
     def once(a, b, dims):
         return dot(a[0], b[0], dimension_numbers=dims)
-
-    def thrice(a, b, dims):
-        (ah, al), (bh, bl) = a, b
-        return dot(ah, bh, dimension_numbers=dims) + (
-            dot(al, bh, dimension_numbers=dims) + dot(ah, bl, dimension_numbers=dims)
-        )
 
     improve(once, lambda x: (x.astype(bf16),))
 
@@ -287,7 +280,7 @@
         return jnp.logical_and(step < NEWTON_LIMIT, jnp.logical_not(size < NEWTON_DONE))
 
     def body(state):
-        return state[0] + 1, improve(thrice, split)
+        return state[0] + 1, improve(multiply, split)
 
     _, size = lax.while_loop(go_on, body, (jnp.int32(0), jnp.float32(1.0)))
 
@@ -311,26 +304,30 @@
 
         lax.fori_loop(0, n, eliminate, 0)
 
-    out[...] = factor[...] * scale_row
-
-
-def basis_kernel(place, vectors, inverse, out):
+    high[...], low[...] = split(factor[...] * scale_row)
+
+
+def own_rows(place, high, low, count):
+    rows = pl.ds(pl.multiple_of(place[0] * count, count), count)
+    return high[rows, :], low[rows, :]
+
+
+def basis_kernel(place, vectors, high, low, out):
     sites, columns, _ = out.shape
-    mine = inverse[pl.ds(pl.multiple_of(place[0] * columns, columns), columns), :]
+    mine = own_rows(place, high, low, columns)
     for s in range(sites):
         block = jnp.concatenate(
             [vectors[u, s * columns : (s + 1) * columns] for u in range(vectors.shape[0])],
             axis=0,
         )
-        out[s] = multiply(mine, block, NN)
-
-
-def projected_kernel(count, place, moments, inverse, out):
-    half = moments.shape[2] // 2
+        out[s] = multiply(mine, split(block), NN)
+
+
+def projected_kernel(count, place, moments, high, low, out):
     moment = jnp.concatenate(lines_of(moments), axis=0)
-    mine = inverse[pl.ds(pl.multiple_of(place[0] * half, half), half), :]
-    half_way = multiply(mine, moment, NN)
-    out[...] = multiply(half_way, inverse[...], NT) * (1.0 / count)
+    mine = own_rows(place, high, low, out.shape[0])
+    half_way = multiply(mine, split(moment), NN)
+    out[...] = multiply(split(half_way), (high[...], low[...]), NT) * (1.0 / count)
 
 
 def passed_along(x, by):
@@ -410,9 +407,9 @@
 
     image = apply(current, back, "image", current)
     table = senders(devices)
-    others = [
-        lax.ppermute(current, "vec", [(table[v][i], v) for v in range(devices)]) for i in range(4)
-    ]
+    others = [None] * 4
+    for i in (3, 1, 0, 2):
+        others[i] = lax.ppermute(current, "vec", [(table[v][i], v) for v in range(devices)])
     kept = 5 * cols // 2
     products = call(
         product_kernel,
@@ -437,7 +434,7 @@
 
     inverse = call(
         functools.partial(inverse_kernel, count),
-        shape((all_cols, all_cols), f32),
+        (shape((all_cols, all_cols), bf16),) * 2,
         0,
         1,
         scratch=[pltpu.VMEM((all_cols, all_cols), f32)] * 2,
@@ -449,20 +446,20 @@
         basis_kernel,
         block,
         1,
-        2,
+        3,
         flops=6 * all_cols * cols * sites * both,
         moved=1 << 22,
         name="basis",
-    )(place, everything, inverse)
+    )(place, everything, *inverse)
     projected = call(
         functools.partial(projected_kernel, count),
         shape((cols, all_cols), f32),
         1,
-        2,
+        3,
         flops=12 * all_cols * all_cols * cols,
         moved=1 << 22,
         name="projected",
-    )(place, moments, inverse)
+    )(place, moments, *inverse)
     return jnp.swapaxes(basis, 1, 2), projected.T
 
 

time: 430 us -> 430 us (level)
  no operation moved by 1% of the time
where the time goes in v11:
time: 430 us; the launch traced here: 429 us
  Pallas kernels  259 us (60%)
  blocking collectives  67 us (16%)
  starting transfers between devices  58 us (13%)
  waiting for transfers between devices  25.7 us (6%)
  between operations  14.3 us (3%)
  local copies, waits for them, and re-layouts  4.75 us (1%)
    pallas_call x1, Pallas kernels, local(): call(functools.partial(inverse_kernel, count), (shape((all_cols, all_cols...  236 us
    ppermute x10, starting transfers between devices, passed_along(): return lax.ppermute(x, 'site', [(i, (i + by) % size) for i in range(size)])  40.3 us
    all_to_all x1, blocking collectives, local(): lax.all_to_all(summed, 'site', 0, 0, tiled=True).reshape(slices * 8, both)  25 us
    all_to_all x1, blocking collectives, local(): lax.all_to_all(products.reshape(slices, 8, both), 'site', 0, 0, tiled=True)  25 us
    ppermute x10, waiting for transfers between devices, passed_along(): return lax.ppermute(x, 'site', [(i, (i + by) % size) for i in range(size)])  19.8 us
    ppermute x4, starting transfers between devices, local(): lax.ppermute(current, 'vec', [(table[v][i], v) for v in range(devices)])  17.6 us
    all_gather x1, blocking collectives, local(): gram = lax.all_gather(whole[:kept], 'vec', axis=0)  17.1 us
  transfers between devices with their start and end apart: 16, of which 7 were waited for; matrix products, arithmetic and copies ran while one was open for 0% of the time, Pallas kernels for 58%

profile of v11, /device:TPU:1, one launch (start us, length us, event | category | flops | bytes accessed | tf_op | source)
XLA Modules:
  0.0 429.2 jit_solution(2767264151663562550)
XLA Ops:
  8.4 1.4 backward.1
  9.8 4.4 %collective-permute-start.1 = (f32[8,64,128]{2,1,0:T(8,128)S(1)}, f32[8,64,128]{2,1,0:T(8,128)S(1)}, u32[]{:S(2)}, u32[]{:S(2)}) collective-permute-start(f32[8,64,128]{2,1,0:T(8,128)S(1)} %get-tuple-element.26), channel_id=1, source_target_pairs={{0,8},{8,16},{16,24},{24,32},{32,40},{40,48},{48,56},{56,64},{64,7... | collective-permute-start | bytes 786440 | tf_op jit(solution)/shard_map/ppermute | solution.py:335
  14.2 12.0 %collective-permute-start = (f32[8,64,128]{2,1,0:T(8,128)}, f32[8,64,128]{2,1,0:T(8,128)S(1)}, u32[]{:S(2)}, u32[]{:S(2)}) collective-permute-start(f32[8,64,128]{2,1,0:T(8,128)} %bitcast.1.x.rest_0_), channel_id=1, source_target_pairs={{0,504},{8,0},{16,8},{24,16},{32,24},{40,32},{48,40},{56,48},{64,5... | collective-permute-start | bytes 786440 | tf_op jit(solution)/shard_map/ppermute | solution.py:335
  27.8 3.1 prepare.1
  30.9 1.6 own_slice.5.own
  33.6 6.2 %collective-permute-start.2 = (f32[8,64,128]{2,1,0:T(8,128)S(1)}, f32[8,64,128]{2,1,0:T(8,128)S(1)}, u32[]{:S(2)}, u32[]{:S(2)}) collective-permute-start(f32[8,64,128]{2,1,0:T(8,128)S(1)} %get-tuple-element.31.x.rest_0_), channel_id=1, source_target_pairs={{0,504},{8,0},{16,8},{24,16},{32,24},{40,32},{48,40},{56,48},{64,5... | collective-permute-start | bytes 786440 | tf_op jit(solution)/shard_map/ppermute | solution.py:335
  39.8 1.9 collective-permute-start.3
  43.8 7.2 %collective-permute-done.3.received = f32[8,64,128]{2,1,0:T(8,128)S(1)} collective-permute-done((f32[8,64,128]{2,1,0:T(8,128)S(1)}, f32[8,64,128]{2,1,0:T(8,128)S(1)}, u32[]{:S(2)}, u32[]{:S(2)}) %collective-permute-start.3) | collective-permute-done | bytes 262176 | tf_op jit(solution)/shard_map/ppermute | solution.py:335
  51.0 1.4 next_slices.6
  52.4 1.9 collective-permute-start.4
  54.4 3.4 collective-permute-start.5
  59.5 5.2 %collective-permute-done.5.received = f32[8,64,128]{2,1,0:T(8,128)S(1)} collective-permute-done((f32[8,64,128]{2,1,0:T(8,128)S(1)}, f32[8,64,128]{2,1,0:T(8,128)S(1)}, u32[]{:S(2)}, u32[]{:S(2)}) %collective-permute-start.5) | collective-permute-done | bytes 262176 | tf_op jit(solution)/shard_map/ppermute | solution.py:335
  65.8 1.9 collective-permute-start.6
  67.8 3.4 collective-permute-start.7
  73.0 5.2 %collective-permute-done.7.received = f32[8,64,128]{2,1,0:T(8,128)S(1)} collective-permute-done((f32[8,64,128]{2,1,0:T(8,128)S(1)}, f32[8,64,128]{2,1,0:T(8,128)S(1)}, u32[]{:S(2)}, u32[]{:S(2)}) %collective-permute-start.7) | collective-permute-done | bytes 262176 | tf_op jit(solution)/shard_map/ppermute | solution.py:335
  78.2 1.6 next_slices.8
  79.9 1.9 collective-permute-start.8
  81.8 3.4 collective-permute-start.9
  85.1 4.4 %collective-permute-start.10 = (f32[8,64,128]{2,1,0:T(8,128)}, f32[8,64,128]{2,1,0:T(8,128)S(1)}, u32[]{:S(2)}, u32[]{:S(2)}) collective-permute-start(f32[8,64,128]{2,1,0:T(8,128)} %get-tuple-element.37.x.rest_0_.own), channel_id=1, source_target_pairs={{6,0},{3,1},{0,2},{5,3},{2,4},{7,5},{4,6},{1,7},{14,8},{11,9},{8,1... | collective-permute-start | bytes 786440 | tf_op jit(solution)/shard_map/ppermute | solution.py:412
  89.5 7.9 %collective-permute-start.11 = (f32[8,64,128]{2,1,0:T(8,128)}, f32[8,64,128]{2,1,0:T(8,128)S(1)}, u32[]{:S(2)}, u32[]{:S(2)}) collective-permute-start(f32[8,64,128]{2,1,0:T(8,128)} %get-tuple-element.37.x.rest_0_.own), channel_id=1, source_target_pairs={{3,0},{2,1},{5,2},{4,3},{7,4},{6,5},{1,6},{0,7},{11,8},{10,9},{13,... | collective-permute-start | bytes 786440 | tf_op jit(solution)/shard_map/ppermute | solution.py:412
  97.4 1.9 collective-permute-start.12
  99.4 3.4 collective-permute-start.13
  102.8 1.6 own_slice.9.own
  104.4 1.3 next_slices.9.image
  105.7 5.8 %collective-permute-done.13.fourth = f32[8,64,128]{2,1,0:T(8,128)S(1)} collective-permute-done((f32[8,64,128]{2,1,0:T(8,128)}, f32[8,64,128]{2,1,0:T(8,128)S(1)}, u32[]{:S(2)}, u32[]{:S(2)}) %collective-permute-start.13) | collective-permute-done | bytes 262176 | tf_op jit(solution)/shard_map/ppermute | solution.py:412
  111.5 1.8 products.1
  113.4 25.0 %all_to_all.10.parts = f32[64,8,128]{2,1,0:T(8,128)S(1)} all-to-all(f32[64,8,128]{2,1,0:T(8,128)S(1)} %bitcast.12), channel_id=1, replica_groups=mesh['site'=64,'vec'=8] {'site'}, dimensions={0} | all-to-all | bytes 524288 | tf_op jit(solution)/shard_map/all_to_all | solution.py:426
  138.4 25.0 %all_to_all.11 = f32[64,8,128]{2,1,0:T(8,128)S(1)} all-to-all(f32[64,8,128]{2,1,0:T(8,128)S(1)} %sum_parts.1), channel_id=1, replica_groups=mesh['site'=64,'vec'=8] {'site'}, dimensions={0} | all-to-all | bytes 524288 | tf_op jit(solution)/shard_map/all_to_all | solution.py:430
  164.1 17.1 %all-gather.1 = f32[1280,128]{1,0:T(8,128)S(1)} all-gather(f32[160,128]{1,0:T(8,128)S(1)} %slice.6), channel_id=3, replica_groups=mesh['site'=64,'vec'=8] {'vec'}, dimensions={0}, use_global_device_ids=true | all-gather | bytes 737280 | tf_op jit(solution)/shard_map/all_gather | solution.py:433
  181.2 236.4 %inverse_factor.1 = (bf16[512,512]{1,0:T(8,128)(2,1)S(1)}, bf16[512,512]{1,0:T(8,128)(2,1)S(1)}) custom-call(f32[8,160,128]{2,1,0:T(8,128)S(1)} %bitcast.13), custom_call_target="tpu_custom_call" | custom-call | flops 7247757312 | bytes 2097152 | tf_op jit(solution)/shard_map/inverse_factor/pallas_call | solution.py:435
  417.6 1.3 basis.1
  420.2 2.2 projected.1
  (36 shorter events, 12.8 us)
Async XLA Ops:
  7.2 156.2 %all-gather.6.cloned.1.call-start = ((), (), s32[]{:S(2)}) async-start(), calls=%async_computation.2 | async-start | bytes 2359296 | tf_op jit(solution)/shard_map/all_gather | solution.py:424
  7.2 1.2 copy-start.1
  8.4 22.5 %copy-start.4 = (s32[8,8]{1,0:T(8,128)S(1)}, s32[8,8]{1,0:T(8,128)}, u32[]{:S(2)}) copy-start(s32[8,8]{1,0:T(8,128)} %near.21) | copy-start | bytes 772
  9.8 22.7 %collective-permute-start.1 = (f32[8,64,128]{2,1,0:T(8,128)S(1)}, f32[8,64,128]{2,1,0:T(8,128)S(1)}, u32[]{:S(2)}, u32[]{:S(2)}) collective-permute-start(f32[8,64,128]{2,1,0:T(8,128)S(1)} %get-tuple-element.26), channel_id=1, source_target_pairs={{0,8},{8,16},{16,24},{24,32},{32,40},{40,48},{48,56},{56,64},{64,7... | collective-permute-start | bytes 786440 | tf_op jit(solution)/shard_map/ppermute | solution.py:335
  14.2 18.3 %collective-permute-start = (f32[8,64,128]{2,1,0:T(8,128)}, f32[8,64,128]{2,1,0:T(8,128)S(1)}, u32[]{:S(2)}, u32[]{:S(2)}) collective-permute-start(f32[8,64,128]{2,1,0:T(8,128)} %bitcast.1.x.rest_0_), channel_id=1, source_target_pairs={{0,504},{8,0},{16,8},{24,16},{32,24},{40,32},{48,40},{56,48},{64,5... | collective-permute-start | bytes 786440 | tf_op jit(solution)/shard_map/ppermute | solution.py:335
  26.2 0.7 copy-start.3
  26.9 0.9 copy-start.5
  33.6 10.3 %collective-permute-start.2 = (f32[8,64,128]{2,1,0:T(8,128)S(1)}, f32[8,64,128]{2,1,0:T(8,128)S(1)}, u32[]{:S(2)}, u32[]{:S(2)}) collective-permute-start(f32[8,64,128]{2,1,0:T(8,128)S(1)} %get-tuple-element.31.x.rest_0_), channel_id=1, source_target_pairs={{0,504},{8,0},{16,8},{24,16},{32,24},{40,32},{48,40},{56,48},{64,5... | collective-permute-start | bytes 786440 | tf_op jit(solution)/shard_map/ppermute | solution.py:335
  39.8 11.2 %collective-permute-start.3 = (f32[8,64,128]{2,1,0:T(8,128)S(1)}, f32[8,64,128]{2,1,0:T(8,128)S(1)}, u32[]{:S(2)}, u32[]{:S(2)}) collective-permute-start(f32[8,64,128]{2,1,0:T(8,128)S(1)} %get-tuple-element.32), channel_id=1, source_target_pairs={{0,8},{8,16},{16,24},{24,32},{32,40},{40,48},{48,56},{56,64},{64,7... | collective-permute-start | bytes 786440 | tf_op jit(solution)/shard_map/ppermute | solution.py:335
  52.4 7.1 %collective-permute-start.4 = (f32[8,64,128]{2,1,0:T(8,128)S(1)}, f32[8,64,128]{2,1,0:T(8,128)S(1)}, u32[]{:S(2)}, u32[]{:S(2)}) collective-permute-start(f32[8,64,128]{2,1,0:T(8,128)S(1)} %get-tuple-element.33.x.rest_0_), channel_id=1, source_target_pairs={{0,504},{8,0},{16,8},{24,16},{32,24},{40,32},{48,40},{56,48},{64,5... | collective-permute-start | bytes 786440 | tf_op jit(solution)/shard_map/ppermute | solution.py:335
  54.4 10.4 %collective-permute-start.5 = (f32[8,64,128]{2,1,0:T(8,128)S(1)}, f32[8,64,128]{2,1,0:T(8,128)S(1)}, u32[]{:S(2)}, u32[]{:S(2)}) collective-permute-start(f32[8,64,128]{2,1,0:T(8,128)S(1)} %get-tuple-element.34), channel_id=1, source_target_pairs={{0,8},{8,16},{16,24},{24,32},{32,40},{40,48},{48,56},{56,64},{64,7... | collective-permute-start | bytes 786440 | tf_op jit(solution)/shard_map/ppermute | solution.py:335
  65.8 7.1 %collective-permute-start.6 = (f32[8,64,128]{2,1,0:T(8,128)S(1)}, f32[8,64,128]{2,1,0:T(8,128)S(1)}, u32[]{:S(2)}, u32[]{:S(2)}) collective-permute-start(f32[8,64,128]{2,1,0:T(8,128)S(1)} %get-tuple-element.35.x), channel_id=1, source_target_pairs={{0,504},{8,0},{16,8},{24,16},{32,24},{40,32},{48,40},{56,48},{64,5... | collective-permute-start | bytes 786440 | tf_op jit(solution)/shard_map/ppermute | solution.py:335
  67.8 10.4 %collective-permute-start.7 = (f32[8,64,128]{2,1,0:T(8,128)S(1)}, f32[8,64,128]{2,1,0:T(8,128)S(1)}, u32[]{:S(2)}, u32[]{:S(2)}) collective-permute-start(f32[8,64,128]{2,1,0:T(8,128)S(1)} %get-tuple-element.36), channel_id=1, source_target_pairs={{0,8},{8,16},{16,24},{24,32},{32,40},{40,48},{48,56},{56,64},{64,7... | collective-permute-start | bytes 786440 | tf_op jit(solution)/shard_map/ppermute | solution.py:335
  79.9 19.5 %collective-permute-start.8 = (f32[8,64,128]{2,1,0:T(8,128)}, f32[8,64,128]{2,1,0:T(8,128)S(1)}, u32[]{:S(2)}, u32[]{:S(2)}) collective-permute-start(f32[8,64,128]{2,1,0:T(8,128)} %get-tuple-element.37.x.rest_0_.own), channel_id=1, source_target_pairs={{0,504},{8,0},{16,8},{24,16},{32,24},{40,32},{48,40},{56,48},{64,5... | collective-permute-start | bytes 786440 | tf_op jit(solution)/shard_map/ppermute | solution.py:335
  81.8 22.6 %collective-permute-start.9 = (f32[8,64,128]{2,1,0:T(8,128)S(1)}, f32[8,64,128]{2,1,0:T(8,128)S(1)}, u32[]{:S(2)}, u32[]{:S(2)}) collective-permute-start(f32[8,64,128]{2,1,0:T(8,128)S(1)} %get-tuple-element.38), channel_id=1, source_target_pairs={{0,8},{8,16},{16,24},{24,32},{32,40},{40,48},{48,56},{56,64},{64,7... | collective-permute-start | bytes 786440 | tf_op jit(solution)/shard_map/ppermute | solution.py:335
  85.1 20.5 %collective-permute-start.10 = (f32[8,64,128]{2,1,0:T(8,128)}, f32[8,64,128]{2,1,0:T(8,128)S(1)}, u32[]{:S(2)}, u32[]{:S(2)}) collective-permute-start(f32[8,64,128]{2,1,0:T(8,128)} %get-tuple-element.37.x.rest_0_.own), channel_id=1, source_target_pairs={{6,0},{3,1},{0,2},{5,3},{2,4},{7,5},{4,6},{1,7},{14,8},{11,9},{8,1... | collective-permute-start | bytes 786440 | tf_op jit(solution)/shard_map/ppermute | solution.py:412
  89.5 16.1 %collective-permute-start.11 = (f32[8,64,128]{2,1,0:T(8,128)}, f32[8,64,128]{2,1,0:T(8,128)S(1)}, u32[]{:S(2)}, u32[]{:S(2)}) collective-permute-start(f32[8,64,128]{2,1,0:T(8,128)} %get-tuple-element.37.x.rest_0_.own), channel_id=1, source_target_pairs={{3,0},{2,1},{5,2},{4,3},{7,4},{6,5},{1,6},{0,7},{11,8},{10,9},{13,... | collective-permute-start | bytes 786440 | tf_op jit(solution)/shard_map/ppermute | solution.py:412
  97.4 8.2 %collective-permute-start.12 = (f32[8,64,128]{2,1,0:T(8,128)}, f32[8,64,128]{2,1,0:T(8,128)S(1)}, u32[]{:S(2)}, u32[]{:S(2)}) collective-permute-start(f32[8,64,128]{2,1,0:T(8,128)} %get-tuple-element.37.x.rest_0_.own), channel_id=1, source_target_pairs={{1,0},{0,1},{3,2},{2,3},{5,4},{4,5},{7,6},{6,7},{9,8},{8,9},{11,10... | collective-permute-start | bytes 786440 | tf_op jit(solution)/shard_map/ppermute | solution.py:412
  99.4 12.1 %collective-permute-start.13 = (f32[8,64,128]{2,1,0:T(8,128)}, f32[8,64,128]{2,1,0:T(8,128)S(1)}, u32[]{:S(2)}, u32[]{:S(2)}) collective-permute-start(f32[8,64,128]{2,1,0:T(8,128)} %get-tuple-element.37.x.rest_0_.own), channel_id=1, source_target_pairs={{5,0},{4,1},{7,2},{6,3},{0,4},{1,5},{2,6},{3,7},{13,8},{12,9},{15,... | collective-permute-start | bytes 786440 | tf_op jit(solution)/shard_map/ppermute | solution.py:412
  113.3 305.6 %all-gather.8.cloned.1.call-start = ((), (), s32[]{:S(2)}) async-start(), calls=%async_computation.3 | async-start | bytes 1179648 | tf_op jit(solution)/shard_map/all_gather | solution.py:432
  181.2 236.5 %copy-start = (f32[4096,128]{1,0:T(8,128)S(1)}, f32[4096,128]{1,0:T(8,128)}, u32[]{:S(2)}) copy-start(f32[4096,128]{1,0:T(8,128)} %all-gather.6.cloned.1.call-done) | copy-start | bytes 6291460
  418.9 1.2 copy-start.2
Sparse Core Ops, SparseCore 0:
  113.4 22.8 all-gather.5
  164.2 24.4 all-gather.7

commit v12 on v11

--- a/solution.py
+++ b/solution.py
@@ -158,7 +158,7 @@
     return table
 
 
-def product_kernel(own, image, first, second, third, fourth, out):
+def product_kernel(own, image, fourth, second, first, third, out):
     sites, cols, wide = own.shape
 
     def flat(ref):
@@ -407,9 +407,10 @@
 
     image = apply(current, back, "image", current)
     table = senders(devices)
-    others = [None] * 4
-    for i in (3, 1, 0, 2):
-        others[i] = lax.ppermute(current, "vec", [(table[v][i], v) for v in range(devices)])
+    others = [
+        lax.ppermute(current, "vec", [(table[v][i], v) for v in range(devices)])
+        for i in (3, 1, 0, 2)
+    ]
     kept = 5 * cols // 2
     products = call(
         product_kernel,

time: 430 us -> 428 us (level)
  transfers between devices with their start and end apart: 16 -> 16, of which waited for: 7 -> 8; matrix products, arithmetic and copies ran while one was open for 0% -> 0% of each run, Pallas kernels for 58% -> 58%
where the time goes in v12:
time: 428 us; the launch traced here: 427 us
  Pallas kernels  259 us (61%)
  blocking collectives  67.9 us (16%)
  starting transfers between devices  57.5 us (13%)
  waiting for transfers between devices  23.3 us (5%)
  between operations  14.3 us (3%)
  local copies, waits for them, and re-layouts  4.75 us (1%)
    pallas_call x1, Pallas kernels, local(): call(functools.partial(inverse_kernel, count), (shape((all_cols, all_cols...  236 us
    ppermute x10, starting transfers between devices, passed_along(): return lax.ppermute(x, 'site', [(i, (i + by) % size) for i in range(size)])  40.3 us
    all_to_all x1, blocking collectives, local(): lax.all_to_all(summed, 'site', 0, 0, tiled=True).reshape(slices * 8, both)  25.9 us
    all_to_all x1, blocking collectives, local(): lax.all_to_all(products.reshape(slices, 8, both), 'site', 0, 0, tiled=True)  25.4 us
    ppermute x10, waiting for transfers between devices, passed_along(): return lax.ppermute(x, 'site', [(i, (i + by) % size) for i in range(size)])  19.8 us
    ppermute x4, starting transfers between devices, local(): lax.ppermute(current, 'vec', [(table[v][i], v) for v in range(devices)])  17.1 us
    all_gather x1, blocking collectives, local(): gram = lax.all_gather(whole[:kept], 'vec', axis=0)  16.6 us
  transfers between devices with their start and end apart: 16, of which 8 were waited for; matrix products, arithmetic and copies ran while one was open for 0% of the time, Pallas kernels for 58%

profile of v12, /device:TPU:1, one launch (start us, length us, event | category | flops | bytes accessed | tf_op | source)
XLA Modules:
  0.0 427.2 jit_solution(2597122471763457446)
XLA Ops:
  8.4 1.4 backward.1
  9.8 4.4 %collective-permute-start.1 = (f32[8,64,128]{2,1,0:T(8,128)S(1)}, f32[8,64,128]{2,1,0:T(8,128)S(1)}, u32[]{:S(2)}, u32[]{:S(2)}) collective-permute-start(f32[8,64,128]{2,1,0:T(8,128)S(1)} %get-tuple-element.26), channel_id=1, source_target_pairs={{0,8},{8,16},{16,24},{24,32},{32,40},{40,48},{48,56},{56,64},{64,7... | collective-permute-start | bytes 786440 | tf_op jit(solution)/shard_map/ppermute | solution.py:335
  14.2 12.0 %collective-permute-start = (f32[8,64,128]{2,1,0:T(8,128)}, f32[8,64,128]{2,1,0:T(8,128)S(1)}, u32[]{:S(2)}, u32[]{:S(2)}) collective-permute-start(f32[8,64,128]{2,1,0:T(8,128)} %bitcast.1.x.rest_0_), channel_id=1, source_target_pairs={{0,504},{8,0},{16,8},{24,16},{32,24},{40,32},{48,40},{56,48},{64,5... | collective-permute-start | bytes 786440 | tf_op jit(solution)/shard_map/ppermute | solution.py:335
  27.8 3.1 prepare.1
  30.9 1.6 own_slice.5.own
  33.6 6.2 %collective-permute-start.2 = (f32[8,64,128]{2,1,0:T(8,128)S(1)}, f32[8,64,128]{2,1,0:T(8,128)S(1)}, u32[]{:S(2)}, u32[]{:S(2)}) collective-permute-start(f32[8,64,128]{2,1,0:T(8,128)S(1)} %get-tuple-element.31.x.rest_0_), channel_id=1, source_target_pairs={{0,504},{8,0},{16,8},{24,16},{32,24},{40,32},{48,40},{56,48},{64,5... | collective-permute-start | bytes 786440 | tf_op jit(solution)/shard_map/ppermute | solution.py:335
  39.8 1.9 collective-permute-start.3
  43.8 7.2 %collective-permute-done.3.received = f32[8,64,128]{2,1,0:T(8,128)S(1)} collective-permute-done((f32[8,64,128]{2,1,0:T(8,128)S(1)}, f32[8,64,128]{2,1,0:T(8,128)S(1)}, u32[]{:S(2)}, u32[]{:S(2)}) %collective-permute-start.3) | collective-permute-done | bytes 262176 | tf_op jit(solution)/shard_map/ppermute | solution.py:335
  51.0 1.4 next_slices.6
  52.4 1.9 collective-permute-start.4
  54.4 3.4 collective-permute-start.5
  59.5 5.2 %collective-permute-done.5.received = f32[8,64,128]{2,1,0:T(8,128)S(1)} collective-permute-done((f32[8,64,128]{2,1,0:T(8,128)S(1)}, f32[8,64,128]{2,1,0:T(8,128)S(1)}, u32[]{:S(2)}, u32[]{:S(2)}) %collective-permute-start.5) | collective-permute-done | bytes 262176 | tf_op jit(solution)/shard_map/ppermute | solution.py:335
  65.8 1.9 collective-permute-start.6
  67.8 3.4 collective-permute-start.7
  73.0 5.2 %collective-permute-done.7.received = f32[8,64,128]{2,1,0:T(8,128)S(1)} collective-permute-done((f32[8,64,128]{2,1,0:T(8,128)S(1)}, f32[8,64,128]{2,1,0:T(8,128)S(1)}, u32[]{:S(2)}, u32[]{:S(2)}) %collective-permute-start.7) | collective-permute-done | bytes 262176 | tf_op jit(solution)/shard_map/ppermute | solution.py:335
  78.2 1.6 next_slices.8
  79.9 1.9 collective-permute-start.8
  81.8 3.4 collective-permute-start.9
  85.1 4.7 %collective-permute-start.10 = (f32[8,64,128]{2,1,0:T(8,128)}, f32[8,64,128]{2,1,0:T(8,128)S(1)}, u32[]{:S(2)}, u32[]{:S(2)}) collective-permute-start(f32[8,64,128]{2,1,0:T(8,128)} %get-tuple-element.37.x.rest_0_.own), channel_id=1, source_target_pairs={{5,0},{4,1},{7,2},{6,3},{0,4},{1,5},{2,6},{3,7},{13,8},{12,9},{15,... | collective-permute-start | bytes 786440 | tf_op jit(solution)/shard_map/ppermute | solution.py:411
  89.8 7.1 %collective-permute-start.11 = (f32[8,64,128]{2,1,0:T(8,128)}, f32[8,64,128]{2,1,0:T(8,128)S(1)}, u32[]{:S(2)}, u32[]{:S(2)}) collective-permute-start(f32[8,64,128]{2,1,0:T(8,128)} %get-tuple-element.37.x.rest_0_.own), channel_id=1, source_target_pairs={{3,0},{2,1},{5,2},{4,3},{7,4},{6,5},{1,6},{0,7},{11,8},{10,9},{13,... | collective-permute-start | bytes 786440 | tf_op jit(solution)/shard_map/ppermute | solution.py:411
  97.0 3.0 collective-permute-start.12
  100.0 2.3 collective-permute-start.13
  102.3 1.6 own_slice.9.own
  103.9 1.3 next_slices.9.image
  106.1 2.5 collective-permute-done.12.first
  108.6 1.8 products.1
  110.5 25.4 %all_to_all.10.parts = f32[64,8,128]{2,1,0:T(8,128)S(1)} all-to-all(f32[64,8,128]{2,1,0:T(8,128)S(1)} %bitcast.12), channel_id=1, replica_groups=mesh['site'=64,'vec'=8] {'site'}, dimensions={0} | all-to-all | bytes 524288 | tf_op jit(solution)/shard_map/all_to_all | solution.py:427
  135.9 25.9 %all_to_all.11 = f32[64,8,128]{2,1,0:T(8,128)S(1)} all-to-all(f32[64,8,128]{2,1,0:T(8,128)S(1)} %sum_parts.1), channel_id=1, replica_groups=mesh['site'=64,'vec'=8] {'site'}, dimensions={0} | all-to-all | bytes 524288 | tf_op jit(solution)/shard_map/all_to_all | solution.py:431
  162.5 16.6 %all-gather.1 = f32[1280,128]{1,0:T(8,128)S(1)} all-gather(f32[160,128]{1,0:T(8,128)S(1)} %slice.6), channel_id=3, replica_groups=mesh['site'=64,'vec'=8] {'vec'}, dimensions={0}, use_global_device_ids=true | all-gather | bytes 737280 | tf_op jit(solution)/shard_map/all_gather | solution.py:434
  179.1 236.4 %inverse_factor.1 = (bf16[512,512]{1,0:T(8,128)(2,1)S(1)}, bf16[512,512]{1,0:T(8,128)(2,1)S(1)}) custom-call(f32[8,160,128]{2,1,0:T(8,128)S(1)} %bitcast.13), custom_call_target="tpu_custom_call" | custom-call | flops 7247757312 | bytes 2097152 | tf_op jit(solution)/shard_map/inverse_factor/pallas_call | solution.py:436
  415.6 1.3 basis.1
  418.1 2.2 projected.1
  (36 shorter events, 13.7 us)
Async XLA Ops:
  7.2 154.7 %all-gather.6.cloned.1.call-start = ((), (), s32[]{:S(2)}) async-start(), calls=%async_computation.2 | async-start | bytes 2359296 | tf_op jit(solution)/shard_map/all_gather | solution.py:425
  7.2 1.2 copy-start.1
  8.4 22.5 %copy-start.4 = (s32[8,8]{1,0:T(8,128)S(1)}, s32[8,8]{1,0:T(8,128)}, u32[]{:S(2)}) copy-start(s32[8,8]{1,0:T(8,128)} %near.21) | copy-start | bytes 772
  9.8 22.7 %collective-permute-start.1 = (f32[8,64,128]{2,1,0:T(8,128)S(1)}, f32[8,64,128]{2,1,0:T(8,128)S(1)}, u32[]{:S(2)}, u32[]{:S(2)}) collective-permute-start(f32[8,64,128]{2,1,0:T(8,128)S(1)} %get-tuple-element.26), channel_id=1, source_target_pairs={{0,8},{8,16},{16,24},{24,32},{32,40},{40,48},{48,56},{56,64},{64,7... | collective-permute-start | bytes 786440 | tf_op jit(solution)/shard_map/ppermute | solution.py:335
  14.2 18.3 %collective-permute-start = (f32[8,64,128]{2,1,0:T(8,128)}, f32[8,64,128]{2,1,0:T(8,128)S(1)}, u32[]{:S(2)}, u32[]{:S(2)}) collective-permute-start(f32[8,64,128]{2,1,0:T(8,128)} %bitcast.1.x.rest_0_), channel_id=1, source_target_pairs={{0,504},{8,0},{16,8},{24,16},{32,24},{40,32},{48,40},{56,48},{64,5... | collective-permute-start | bytes 786440 | tf_op jit(solution)/shard_map/ppermute | solution.py:335
  26.2 0.7 copy-start.3
  26.9 0.9 copy-start.5
  33.6 10.3 %collective-permute-start.2 = (f32[8,64,128]{2,1,0:T(8,128)S(1)}, f32[8,64,128]{2,1,0:T(8,128)S(1)}, u32[]{:S(2)}, u32[]{:S(2)}) collective-permute-start(f32[8,64,128]{2,1,0:T(8,128)S(1)} %get-tuple-element.31.x.rest_0_), channel_id=1, source_target_pairs={{0,504},{8,0},{16,8},{24,16},{32,24},{40,32},{48,40},{56,48},{64,5... | collective-permute-start | bytes 786440 | tf_op jit(solution)/shard_map/ppermute | solution.py:335
  39.8 11.2 %collective-permute-start.3 = (f32[8,64,128]{2,1,0:T(8,128)S(1)}, f32[8,64,128]{2,1,0:T(8,128)S(1)}, u32[]{:S(2)}, u32[]{:S(2)}) collective-permute-start(f32[8,64,128]{2,1,0:T(8,128)S(1)} %get-tuple-element.32), channel_id=1, source_target_pairs={{0,8},{8,16},{16,24},{24,32},{32,40},{40,48},{48,56},{56,64},{64,7... | collective-permute-start | bytes 786440 | tf_op jit(solution)/shard_map/ppermute | solution.py:335
  52.4 7.1 %collective-permute-start.4 = (f32[8,64,128]{2,1,0:T(8,128)S(1)}, f32[8,64,128]{2,1,0:T(8,128)S(1)}, u32[]{:S(2)}, u32[]{:S(2)}) collective-permute-start(f32[8,64,128]{2,1,0:T(8,128)S(1)} %get-tuple-element.33.x.rest_0_), channel_id=1, source_target_pairs={{0,504},{8,0},{16,8},{24,16},{32,24},{40,32},{48,40},{56,48},{64,5... | collective-permute-start | bytes 786440 | tf_op jit(solution)/shard_map/ppermute | solution.py:335
  54.4 10.4 %collective-permute-start.5 = (f32[8,64,128]{2,1,0:T(8,128)S(1)}, f32[8,64,128]{2,1,0:T(8,128)S(1)}, u32[]{:S(2)}, u32[]{:S(2)}) collective-permute-start(f32[8,64,128]{2,1,0:T(8,128)S(1)} %get-tuple-element.34), channel_id=1, source_target_pairs={{0,8},{8,16},{16,24},{24,32},{32,40},{40,48},{48,56},{56,64},{64,7... | collective-permute-start | bytes 786440 | tf_op jit(solution)/shard_map/ppermute | solution.py:335
  65.8 7.1 %collective-permute-start.6 = (f32[8,64,128]{2,1,0:T(8,128)S(1)}, f32[8,64,128]{2,1,0:T(8,128)S(1)}, u32[]{:S(2)}, u32[]{:S(2)}) collective-permute-start(f32[8,64,128]{2,1,0:T(8,128)S(1)} %get-tuple-element.35.x), channel_id=1, source_target_pairs={{0,504},{8,0},{16,8},{24,16},{32,24},{40,32},{48,40},{56,48},{64,5... | collective-permute-start | bytes 786440 | tf_op jit(solution)/shard_map/ppermute | solution.py:335
  67.8 10.4 %collective-permute-start.7 = (f32[8,64,128]{2,1,0:T(8,128)S(1)}, f32[8,64,128]{2,1,0:T(8,128)S(1)}, u32[]{:S(2)}, u32[]{:S(2)}) collective-permute-start(f32[8,64,128]{2,1,0:T(8,128)S(1)} %get-tuple-element.36), channel_id=1, source_target_pairs={{0,8},{8,16},{16,24},{24,32},{32,40},{40,48},{48,56},{56,64},{64,7... | collective-permute-start | bytes 786440 | tf_op jit(solution)/shard_map/ppermute | solution.py:335
  79.9 20.1 %collective-permute-start.8 = (f32[8,64,128]{2,1,0:T(8,128)}, f32[8,64,128]{2,1,0:T(8,128)S(1)}, u32[]{:S(2)}, u32[]{:S(2)}) collective-permute-start(f32[8,64,128]{2,1,0:T(8,128)} %get-tuple-element.37.x.rest_0_.own), channel_id=1, source_target_pairs={{0,504},{8,0},{16,8},{24,16},{32,24},{40,32},{48,40},{56,48},{64,5... | collective-permute-start | bytes 786440 | tf_op jit(solution)/shard_map/ppermute | solution.py:335
  81.8 22.1 %collective-permute-start.9 = (f32[8,64,128]{2,1,0:T(8,128)S(1)}, f32[8,64,128]{2,1,0:T(8,128)S(1)}, u32[]{:S(2)}, u32[]{:S(2)}) collective-permute-start(f32[8,64,128]{2,1,0:T(8,128)S(1)} %get-tuple-element.38), channel_id=1, source_target_pairs={{0,8},{8,16},{16,24},{24,32},{32,40},{40,48},{48,56},{56,64},{64,7... | collective-permute-start | bytes 786440 | tf_op jit(solution)/shard_map/ppermute | solution.py:335
  85.1 20.0 %collective-permute-start.10 = (f32[8,64,128]{2,1,0:T(8,128)}, f32[8,64,128]{2,1,0:T(8,128)S(1)}, u32[]{:S(2)}, u32[]{:S(2)}) collective-permute-start(f32[8,64,128]{2,1,0:T(8,128)} %get-tuple-element.37.x.rest_0_.own), channel_id=1, source_target_pairs={{5,0},{4,1},{7,2},{6,3},{0,4},{1,5},{2,6},{3,7},{13,8},{12,9},{15,... | collective-permute-start | bytes 786440 | tf_op jit(solution)/shard_map/ppermute | solution.py:411
  89.8 16.3 %collective-permute-start.11 = (f32[8,64,128]{2,1,0:T(8,128)}, f32[8,64,128]{2,1,0:T(8,128)S(1)}, u32[]{:S(2)}, u32[]{:S(2)}) collective-permute-start(f32[8,64,128]{2,1,0:T(8,128)} %get-tuple-element.37.x.rest_0_.own), channel_id=1, source_target_pairs={{3,0},{2,1},{5,2},{4,3},{7,4},{6,5},{1,6},{0,7},{11,8},{10,9},{13,... | collective-permute-start | bytes 786440 | tf_op jit(solution)/shard_map/ppermute | solution.py:411
  97.0 11.6 %collective-permute-start.12 = (f32[8,64,128]{2,1,0:T(8,128)}, f32[8,64,128]{2,1,0:T(8,128)S(1)}, u32[]{:S(2)}, u32[]{:S(2)}) collective-permute-start(f32[8,64,128]{2,1,0:T(8,128)} %get-tuple-element.37.x.rest_0_.own), channel_id=1, source_target_pairs={{6,0},{3,1},{0,2},{5,3},{2,4},{7,5},{4,6},{1,7},{14,8},{11,9},{8,1... | collective-permute-start | bytes 786440 | tf_op jit(solution)/shard_map/ppermute | solution.py:411
  100.0 8.6 %collective-permute-start.13 = (f32[8,64,128]{2,1,0:T(8,128)}, f32[8,64,128]{2,1,0:T(8,128)S(1)}, u32[]{:S(2)}, u32[]{:S(2)}) collective-permute-start(f32[8,64,128]{2,1,0:T(8,128)} %get-tuple-element.37.x.rest_0_.own), channel_id=1, source_target_pairs={{1,0},{0,1},{3,2},{2,3},{5,4},{4,5},{7,6},{6,7},{9,8},{8,9},{11,10... | collective-permute-start | bytes 786440 | tf_op jit(solution)/shard_map/ppermute | solution.py:411
  110.4 306.5 %all-gather.8.cloned.1.call-start = ((), (), s32[]{:S(2)}) async-start(), calls=%async_computation.3 | async-start | bytes 1179648 | tf_op jit(solution)/shard_map/all_gather | solution.py:433
  179.1 236.5 %copy-start = (f32[4096,128]{1,0:T(8,128)S(1)}, f32[4096,128]{1,0:T(8,128)}, u32[]{:S(2)}) copy-start(f32[4096,128]{1,0:T(8,128)} %all-gather.6.cloned.1.call-done) | copy-start | bytes 6291460
  416.9 1.2 copy-start.2
Sparse Core Ops, SparseCore 0:
  110.5 24.4 all-gather.5
  162.6 25.0 all-gather.7

commit v13 on v12

--- a/solution.py
+++ b/solution.py
@@ -150,7 +150,7 @@
         table.append(
             [
                 2 * ((x - 1 + 2 * c) % chips) + c,
-                2 * ((x + 1) % chips) + 1 - c,
+                2 * ((x - 1) % chips) + 1 - c,
                 2 * x + 1 - c,
                 2 * opposite + (1 - c if x < chips // 2 else c),
             ]

time: 428 us -> 425 us (level)
  transfers between devices with their start and end apart: 16 -> 16, of which waited for: 8 -> 7; matrix products, arithmetic and copies ran while one was open for 0% -> 0% of each run, Pallas kernels for 58% -> 59%
where the time goes in v13:
time: 425 us; the launch traced here: 424 us
  Pallas kernels  259 us (61%)
  blocking collectives  65.2 us (15%)
  starting transfers between devices  59.2 us (14%)
  waiting for transfers between devices  21.1 us (5%)
  between operations  14.3 us (3%)
  local copies, waits for them, and re-layouts  4.75 us (1%)
    pallas_call x1, Pallas kernels, local(): call(functools.partial(inverse_kernel, count), (shape((all_cols, all_cols...  236 us
    ppermute x10, starting transfers between devices, passed_along(): return lax.ppermute(x, 'site', [(i, (i + by) % size) for i in range(size)])  40.3 us
    all_to_all x1, blocking collectives, local(): lax.all_to_all(summed, 'site', 0, 0, tiled=True).reshape(slices * 8, both)  24.3 us
    all_to_all x1, blocking collectives, local(): lax.all_to_all(products.reshape(slices, 8, both), 'site', 0, 0, tiled=True)  21.7 us
    ppermute x10, waiting for transfers between devices, passed_along(): return lax.ppermute(x, 'site', [(i, (i + by) % size) for i in range(size)])  19.8 us
    all_gather x1, blocking collectives, local(): gram = lax.all_gather(whole[:kept], 'vec', axis=0)  19.2 us
    ppermute x4, starting transfers between devices, local(): lax.ppermute(current, 'vec', [(table[v][i], v) for v in range(devices)])  18.8 us
  transfers between devices with their start and end apart: 16, of which 7 were waited for; matrix products, arithmetic and copies ran while one was open for 0% of the time, Pallas kernels for 59%

profile of v13, /device:TPU:1, one launch (start us, length us, event | category | flops | bytes accessed | tf_op | source)
XLA Modules:
  0.0 423.8 jit_solution(350131588673451992)
XLA Ops:
  8.4 1.4 backward.1
  9.8 4.4 %collective-permute-start.1 = (f32[8,64,128]{2,1,0:T(8,128)S(1)}, f32[8,64,128]{2,1,0:T(8,128)S(1)}, u32[]{:S(2)}, u32[]{:S(2)}) collective-permute-start(f32[8,64,128]{2,1,0:T(8,128)S(1)} %get-tuple-element.26), channel_id=1, source_target_pairs={{0,8},{8,16},{16,24},{24,32},{32,40},{40,48},{48,56},{56,64},{64,7... | collective-permute-start | bytes 786440 | tf_op jit(solution)/shard_map/ppermute | solution.py:335
  14.2 12.0 %collective-permute-start = (f32[8,64,128]{2,1,0:T(8,128)}, f32[8,64,128]{2,1,0:T(8,128)S(1)}, u32[]{:S(2)}, u32[]{:S(2)}) collective-permute-start(f32[8,64,128]{2,1,0:T(8,128)} %bitcast.1.x.rest_0_), channel_id=1, source_target_pairs={{0,504},{8,0},{16,8},{24,16},{32,24},{40,32},{48,40},{56,48},{64,5... | collective-permute-start | bytes 786440 | tf_op jit(solution)/shard_map/ppermute | solution.py:335
  27.8 3.1 prepare.1
  30.9 1.6 own_slice.5.own
  33.6 6.2 %collective-permute-start.2 = (f32[8,64,128]{2,1,0:T(8,128)S(1)}, f32[8,64,128]{2,1,0:T(8,128)S(1)}, u32[]{:S(2)}, u32[]{:S(2)}) collective-permute-start(f32[8,64,128]{2,1,0:T(8,128)S(1)} %get-tuple-element.31.x.rest_0_), channel_id=1, source_target_pairs={{0,504},{8,0},{16,8},{24,16},{32,24},{40,32},{48,40},{56,48},{64,5... | collective-permute-start | bytes 786440 | tf_op jit(solution)/shard_map/ppermute | solution.py:335
  39.8 1.9 collective-permute-start.3
  43.8 7.2 %collective-permute-done.3.received = f32[8,64,128]{2,1,0:T(8,128)S(1)} collective-permute-done((f32[8,64,128]{2,1,0:T(8,128)S(1)}, f32[8,64,128]{2,1,0:T(8,128)S(1)}, u32[]{:S(2)}, u32[]{:S(2)}) %collective-permute-start.3) | collective-permute-done | bytes 262176 | tf_op jit(solution)/shard_map/ppermute | solution.py:335
  51.0 1.4 next_slices.6
  52.4 1.9 collective-permute-start.4
  54.4 3.4 collective-permute-start.5
  59.5 5.2 %collective-permute-done.5.received = f32[8,64,128]{2,1,0:T(8,128)S(1)} collective-permute-done((f32[8,64,128]{2,1,0:T(8,128)S(1)}, f32[8,64,128]{2,1,0:T(8,128)S(1)}, u32[]{:S(2)}, u32[]{:S(2)}) %collective-permute-start.5) | collective-permute-done | bytes 262176 | tf_op jit(solution)/shard_map/ppermute | solution.py:335
  65.8 1.9 collective-permute-start.6
  67.8 3.4 collective-permute-start.7
  73.0 5.2 %collective-permute-done.7.received = f32[8,64,128]{2,1,0:T(8,128)S(1)} collective-permute-done((f32[8,64,128]{2,1,0:T(8,128)S(1)}, f32[8,64,128]{2,1,0:T(8,128)S(1)}, u32[]{:S(2)}, u32[]{:S(2)}) %collective-permute-start.7) | collective-permute-done | bytes 262176 | tf_op jit(solution)/shard_map/ppermute | solution.py:335
  78.2 1.6 next_slices.8
  79.9 1.9 collective-permute-start.8
  81.8 3.4 collective-permute-start.9
  85.1 4.7 %collective-permute-start.10 = (f32[8,64,128]{2,1,0:T(8,128)}, f32[8,64,128]{2,1,0:T(8,128)S(1)}, u32[]{:S(2)}, u32[]{:S(2)}) collective-permute-start(f32[8,64,128]{2,1,0:T(8,128)} %get-tuple-element.37.x.rest_0_.own), channel_id=1, source_target_pairs={{5,0},{4,1},{7,2},{6,3},{0,4},{1,5},{2,6},{3,7},{13,8},{12,9},{15,... | collective-permute-start | bytes 786440 | tf_op jit(solution)/shard_map/ppermute | solution.py:411
  89.8 8.0 %collective-permute-start.11 = (f32[8,64,128]{2,1,0:T(8,128)}, f32[8,64,128]{2,1,0:T(8,128)S(1)}, u32[]{:S(2)}, u32[]{:S(2)}) collective-permute-start(f32[8,64,128]{2,1,0:T(8,128)} %get-tuple-element.37.x.rest_0_.own), channel_id=1, source_target_pairs={{7,0},{6,1},{1,2},{0,3},{3,4},{2,5},{5,6},{4,7},{15,8},{14,9},{9,1... | collective-permute-start | bytes 786440 | tf_op jit(solution)/shard_map/ppermute | solution.py:411
  97.8 4.3 %collective-permute-start.12 = (f32[8,64,128]{2,1,0:T(8,128)}, f32[8,64,128]{2,1,0:T(8,128)S(1)}, u32[]{:S(2)}, u32[]{:S(2)}) collective-permute-start(f32[8,64,128]{2,1,0:T(8,128)} %get-tuple-element.37.x.rest_0_.own), channel_id=1, source_target_pairs={{6,0},{3,1},{0,2},{5,3},{2,4},{7,5},{4,6},{1,7},{14,8},{11,9},{8,1... | collective-permute-start | bytes 786440 | tf_op jit(solution)/shard_map/ppermute | solution.py:411
  102.1 1.9 collective-permute-start.13
  104.0 1.6 own_slice.9.own
  105.6 1.3 next_slices.9.image
  106.9 1.2 collective-permute-done.11.second
  108.1 1.8 products.1
  110.0 21.7 %all_to_all.10.parts = f32[64,8,128]{2,1,0:T(8,128)S(1)} all-to-all(f32[64,8,128]{2,1,0:T(8,128)S(1)} %bitcast.12), channel_id=1, replica_groups=mesh['site'=64,'vec'=8] {'site'}, dimensions={0} | all-to-all | bytes 524288 | tf_op jit(solution)/shard_map/all_to_all | solution.py:427
  131.7 24.3 %all_to_all.11 = f32[64,8,128]{2,1,0:T(8,128)S(1)} all-to-all(f32[64,8,128]{2,1,0:T(8,128)S(1)} %sum_parts.1), channel_id=1, replica_groups=mesh['site'=64,'vec'=8] {'site'}, dimensions={0} | all-to-all | bytes 524288 | tf_op jit(solution)/shard_map/all_to_all | solution.py:431
  156.8 19.2 %all-gather.1 = f32[1280,128]{1,0:T(8,128)S(1)} all-gather(f32[160,128]{1,0:T(8,128)S(1)} %slice.6), channel_id=3, replica_groups=mesh['site'=64,'vec'=8] {'vec'}, dimensions={0}, use_global_device_ids=true | all-gather | bytes 737280 | tf_op jit(solution)/shard_map/all_gather | solution.py:434
  176.0 236.4 %inverse_factor.1 = (bf16[512,512]{1,0:T(8,128)(2,1)S(1)}, bf16[512,512]{1,0:T(8,128)(2,1)S(1)}) custom-call(f32[8,160,128]{2,1,0:T(8,128)S(1)} %bitcast.13), custom_call_target="tpu_custom_call" | custom-call | flops 7247757312 | bytes 2097152 | tf_op jit(solution)/shard_map/inverse_factor/pallas_call | solution.py:436
  412.4 1.3 basis.1
  414.9 2.1 projected.1
  (36 shorter events, 12.8 us)
Async XLA Ops:
  7.2 148.9 %all-gather.6.cloned.1.call-start = ((), (), s32[]{:S(2)}) async-start(), calls=%async_computation.2 | async-start | bytes 2359296 | tf_op jit(solution)/shard_map/all_gather | solution.py:425
  7.2 1.2 copy-start.1
  8.4 22.5 %copy-start.4 = (s32[8,8]{1,0:T(8,128)S(1)}, s32[8,8]{1,0:T(8,128)}, u32[]{:S(2)}) copy-start(s32[8,8]{1,0:T(8,128)} %near.21) | copy-start | bytes 772
  9.8 22.7 %collective-permute-start.1 = (f32[8,64,128]{2,1,0:T(8,128)S(1)}, f32[8,64,128]{2,1,0:T(8,128)S(1)}, u32[]{:S(2)}, u32[]{:S(2)}) collective-permute-start(f32[8,64,128]{2,1,0:T(8,128)S(1)} %get-tuple-element.26), channel_id=1, source_target_pairs={{0,8},{8,16},{16,24},{24,32},{32,40},{40,48},{48,56},{56,64},{64,7... | collective-permute-start | bytes 786440 | tf_op jit(solution)/shard_map/ppermute | solution.py:335
  14.2 18.3 %collective-permute-start = (f32[8,64,128]{2,1,0:T(8,128)}, f32[8,64,128]{2,1,0:T(8,128)S(1)}, u32[]{:S(2)}, u32[]{:S(2)}) collective-permute-start(f32[8,64,128]{2,1,0:T(8,128)} %bitcast.1.x.rest_0_), channel_id=1, source_target_pairs={{0,504},{8,0},{16,8},{24,16},{32,24},{40,32},{48,40},{56,48},{64,5... | collective-permute-start | bytes 786440 | tf_op jit(solution)/shard_map/ppermute | solution.py:335
  26.2 0.7 copy-start.3
  26.9 0.9 copy-start.5
  33.6 10.3 %collective-permute-start.2 = (f32[8,64,128]{2,1,0:T(8,128)S(1)}, f32[8,64,128]{2,1,0:T(8,128)S(1)}, u32[]{:S(2)}, u32[]{:S(2)}) collective-permute-start(f32[8,64,128]{2,1,0:T(8,128)S(1)} %get-tuple-element.31.x.rest_0_), channel_id=1, source_target_pairs={{0,504},{8,0},{16,8},{24,16},{32,24},{40,32},{48,40},{56,48},{64,5... | collective-permute-start | bytes 786440 | tf_op jit(solution)/shard_map/ppermute | solution.py:335
  39.8 11.2 %collective-permute-start.3 = (f32[8,64,128]{2,1,0:T(8,128)S(1)}, f32[8,64,128]{2,1,0:T(8,128)S(1)}, u32[]{:S(2)}, u32[]{:S(2)}) collective-permute-start(f32[8,64,128]{2,1,0:T(8,128)S(1)} %get-tuple-element.32), channel_id=1, source_target_pairs={{0,8},{8,16},{16,24},{24,32},{32,40},{40,48},{48,56},{56,64},{64,7... | collective-permute-start | bytes 786440 | tf_op jit(solution)/shard_map/ppermute | solution.py:335
  52.4 7.1 %collective-permute-start.4 = (f32[8,64,128]{2,1,0:T(8,128)S(1)}, f32[8,64,128]{2,1,0:T(8,128)S(1)}, u32[]{:S(2)}, u32[]{:S(2)}) collective-permute-start(f32[8,64,128]{2,1,0:T(8,128)S(1)} %get-tuple-element.33.x.rest_0_), channel_id=1, source_target_pairs={{0,504},{8,0},{16,8},{24,16},{32,24},{40,32},{48,40},{56,48},{64,5... | collective-permute-start | bytes 786440 | tf_op jit(solution)/shard_map/ppermute | solution.py:335
  54.4 10.4 %collective-permute-start.5 = (f32[8,64,128]{2,1,0:T(8,128)S(1)}, f32[8,64,128]{2,1,0:T(8,128)S(1)}, u32[]{:S(2)}, u32[]{:S(2)}) collective-permute-start(f32[8,64,128]{2,1,0:T(8,128)S(1)} %get-tuple-element.34), channel_id=1, source_target_pairs={{0,8},{8,16},{16,24},{24,32},{32,40},{40,48},{48,56},{56,64},{64,7... | collective-permute-start | bytes 786440 | tf_op jit(solution)/shard_map/ppermute | solution.py:335
  65.8 7.1 %collective-permute-start.6 = (f32[8,64,128]{2,1,0:T(8,128)S(1)}, f32[8,64,128]{2,1,0:T(8,128)S(1)}, u32[]{:S(2)}, u32[]{:S(2)}) collective-permute-start(f32[8,64,128]{2,1,0:T(8,128)S(1)} %get-tuple-element.35.x), channel_id=1, source_target_pairs={{0,504},{8,0},{16,8},{24,16},{32,24},{40,32},{48,40},{56,48},{64,5... | collective-permute-start | bytes 786440 | tf_op jit(solution)/shard_map/ppermute | solution.py:335
  67.8 10.4 %collective-permute-start.7 = (f32[8,64,128]{2,1,0:T(8,128)S(1)}, f32[8,64,128]{2,1,0:T(8,128)S(1)}, u32[]{:S(2)}, u32[]{:S(2)}) collective-permute-start(f32[8,64,128]{2,1,0:T(8,128)S(1)} %get-tuple-element.36), channel_id=1, source_target_pairs={{0,8},{8,16},{16,24},{24,32},{32,40},{40,48},{48,56},{56,64},{64,7... | collective-permute-start | bytes 786440 | tf_op jit(solution)/shard_map/ppermute | solution.py:335
  79.9 22.2 %collective-permute-start.8 = (f32[8,64,128]{2,1,0:T(8,128)}, f32[8,64,128]{2,1,0:T(8,128)S(1)}, u32[]{:S(2)}, u32[]{:S(2)}) collective-permute-start(f32[8,64,128]{2,1,0:T(8,128)} %get-tuple-element.37.x.rest_0_.own), channel_id=1, source_target_pairs={{0,504},{8,0},{16,8},{24,16},{32,24},{40,32},{48,40},{56,48},{64,5... | collective-permute-start | bytes 786440 | tf_op jit(solution)/shard_map/ppermute | solution.py:335
  81.8 23.8 %collective-permute-start.9 = (f32[8,64,128]{2,1,0:T(8,128)S(1)}, f32[8,64,128]{2,1,0:T(8,128)S(1)}, u32[]{:S(2)}, u32[]{:S(2)}) collective-permute-start(f32[8,64,128]{2,1,0:T(8,128)S(1)} %get-tuple-element.38), channel_id=1, source_target_pairs={{0,8},{8,16},{16,24},{24,32},{32,40},{40,48},{48,56},{56,64},{64,7... | collective-permute-start | bytes 786440 | tf_op jit(solution)/shard_map/ppermute | solution.py:335
  85.1 21.7 %collective-permute-start.10 = (f32[8,64,128]{2,1,0:T(8,128)}, f32[8,64,128]{2,1,0:T(8,128)S(1)}, u32[]{:S(2)}, u32[]{:S(2)}) collective-permute-start(f32[8,64,128]{2,1,0:T(8,128)} %get-tuple-element.37.x.rest_0_.own), channel_id=1, source_target_pairs={{5,0},{4,1},{7,2},{6,3},{0,4},{1,5},{2,6},{3,7},{13,8},{12,9},{15,... | collective-permute-start | bytes 786440 | tf_op jit(solution)/shard_map/ppermute | solution.py:411
  89.8 18.3 %collective-permute-start.11 = (f32[8,64,128]{2,1,0:T(8,128)}, f32[8,64,128]{2,1,0:T(8,128)S(1)}, u32[]{:S(2)}, u32[]{:S(2)}) collective-permute-start(f32[8,64,128]{2,1,0:T(8,128)} %get-tuple-element.37.x.rest_0_.own), channel_id=1, source_target_pairs={{7,0},{6,1},{1,2},{0,3},{3,4},{2,5},{5,6},{4,7},{15,8},{14,9},{9,1... | collective-permute-start | bytes 786440 | tf_op jit(solution)/shard_map/ppermute | solution.py:411
  97.8 10.3 %collective-permute-start.12 = (f32[8,64,128]{2,1,0:T(8,128)}, f32[8,64,128]{2,1,0:T(8,128)S(1)}, u32[]{:S(2)}, u32[]{:S(2)}) collective-permute-start(f32[8,64,128]{2,1,0:T(8,128)} %get-tuple-element.37.x.rest_0_.own), channel_id=1, source_target_pairs={{6,0},{3,1},{0,2},{5,3},{2,4},{7,5},{4,6},{1,7},{14,8},{11,9},{8,1... | collective-permute-start | bytes 786440 | tf_op jit(solution)/shard_map/ppermute | solution.py:411
  102.1 6.0 %collective-permute-start.13 = (f32[8,64,128]{2,1,0:T(8,128)}, f32[8,64,128]{2,1,0:T(8,128)S(1)}, u32[]{:S(2)}, u32[]{:S(2)}) collective-permute-start(f32[8,64,128]{2,1,0:T(8,128)} %get-tuple-element.37.x.rest_0_.own), channel_id=1, source_target_pairs={{1,0},{0,1},{3,2},{2,3},{5,4},{4,5},{7,6},{6,7},{9,8},{8,9},{11,10... | collective-permute-start | bytes 786440 | tf_op jit(solution)/shard_map/ppermute | solution.py:411
  109.9 303.8 %all-gather.8.cloned.1.call-start = ((), (), s32[]{:S(2)}) async-start(), calls=%async_computation.3 | async-start | bytes 1179648 | tf_op jit(solution)/shard_map/all_gather | solution.py:433
  176.0 236.4 %copy-start = (f32[4096,128]{1,0:T(8,128)S(1)}, f32[4096,128]{1,0:T(8,128)}, u32[]{:S(2)}) copy-start(f32[4096,128]{1,0:T(8,128)} %all-gather.6.cloned.1.call-done) | copy-start | bytes 6291460
  413.7 1.2 copy-start.2
Sparse Core Ops, SparseCore 0:
  110.0 24.8 all-gather.5
  156.9 27.3 all-gather.7

commit v14 on v13

--- a/solution.py
+++ b/solution.py
@@ -149,7 +149,7 @@
         opposite = (x + chips // 2) % chips
         table.append(
             [
-                2 * ((x - 1 + 2 * c) % chips) + c,
+                2 * ((x - 1) % chips) + c,
                 2 * ((x - 1) % chips) + 1 - c,
                 2 * x + 1 - c,
                 2 * opposite + (1 - c if x < chips // 2 else c),

time: 425 us -> 432 us (1.016)
  waiting for transfers between devices: 21.1 us -> 28.7 us
    ppermute x4, waiting for transfers between devices: 1.24 us -> 8.82 us  [local(): lax.ppermute(current, 'vec', [(table[v][i], v) for v in range(devices)])]
  transfers between devices with their start and end apart: 16 -> 16, of which waited for: 7 -> 8; matrix products, arithmetic and copies ran while one was open for 0% -> 0% of each run, Pallas kernels for 59% -> 58%
where the time goes in v14:
time: 432 us; the launch traced here: 431 us
  Pallas kernels  259 us (60%)
  blocking collectives  67 us (16%)
  starting transfers between devices  57.3 us (13%)
  waiting for transfers between devices  28.7 us (7%)
  between operations  14.3 us (3%)
  local copies, waits for them, and re-layouts  4.75 us (1%)
    pallas_call x1, Pallas kernels, local(): call(functools.partial(inverse_kernel, count), (shape((all_cols, all_cols...  237 us
    ppermute x10, starting transfers between devices, passed_along(): return lax.ppermute(x, 'site', [(i, (i + by) % size) for i in range(size)])  40.3 us
    all_to_all x1, blocking collectives, local(): lax.all_to_all(summed, 'site', 0, 0, tiled=True).reshape(slices * 8, both)  25 us
    all_to_all x1, blocking collectives, local(): lax.all_to_all(products.reshape(slices, 8, both), 'site', 0, 0, tiled=True)  24.9 us
    ppermute x10, waiting for transfers between devices, passed_along(): return lax.ppermute(x, 'site', [(i, (i + by) % size) for i in range(size)])  19.8 us
    all_gather x1, blocking collectives, local(): gram = lax.all_gather(whole[:kept], 'vec', axis=0)  17.1 us
    ppermute x4, starting transfers between devices, local(): lax.ppermute(current, 'vec', [(table[v][i], v) for v in range(devices)])  16.9 us
    ppermute x4, waiting for transfers between devices, local(): lax.ppermute(current, 'vec', [(table[v][i], v) for v in range(devices)])  8.82 us
  transfers between devices with their start and end apart: 16, of which 8 were waited for; matrix products, arithmetic and copies ran while one was open for 0% of the time, Pallas kernels for 58%

profile of v14, /device:TPU:1, one launch (start us, length us, event | category | flops | bytes accessed | tf_op | source)
XLA Modules:
  0.0 431.5 jit_solution(210234006302041329)
XLA Ops:
  8.4 1.4 backward.1
  9.8 4.4 %collective-permute-start.1 = (f32[8,64,128]{2,1,0:T(8,128)S(1)}, f32[8,64,128]{2,1,0:T(8,128)S(1)}, u32[]{:S(2)}, u32[]{:S(2)}) collective-permute-start(f32[8,64,128]{2,1,0:T(8,128)S(1)} %get-tuple-element.26), channel_id=1, source_target_pairs={{0,8},{8,16},{16,24},{24,32},{32,40},{40,48},{48,56},{56,64},{64,7... | collective-permute-start | bytes 786440 | tf_op jit(solution)/shard_map/ppermute | solution.py:335
  14.2 12.0 %collective-permute-start = (f32[8,64,128]{2,1,0:T(8,128)}, f32[8,64,128]{2,1,0:T(8,128)S(1)}, u32[]{:S(2)}, u32[]{:S(2)}) collective-permute-start(f32[8,64,128]{2,1,0:T(8,128)} %bitcast.1.x.rest_0_), channel_id=1, source_target_pairs={{0,504},{8,0},{16,8},{24,16},{32,24},{40,32},{48,40},{56,48},{64,5... | collective-permute-start | bytes 786440 | tf_op jit(solution)/shard_map/ppermute | solution.py:335
  27.8 3.1 prepare.1
  30.9 1.6 own_slice.5.own
  33.6 6.2 %collective-permute-start.2 = (f32[8,64,128]{2,1,0:T(8,128)S(1)}, f32[8,64,128]{2,1,0:T(8,128)S(1)}, u32[]{:S(2)}, u32[]{:S(2)}) collective-permute-start(f32[8,64,128]{2,1,0:T(8,128)S(1)} %get-tuple-element.31.x.rest_0_), channel_id=1, source_target_pairs={{0,504},{8,0},{16,8},{24,16},{32,24},{40,32},{48,40},{56,48},{64,5... | collective-permute-start | bytes 786440 | tf_op jit(solution)/shard_map/ppermute | solution.py:335
  39.8 1.9 collective-permute-start.3
  43.8 7.2 %collective-permute-done.3.received = f32[8,64,128]{2,1,0:T(8,128)S(1)} collective-permute-done((f32[8,64,128]{2,1,0:T(8,128)S(1)}, f32[8,64,128]{2,1,0:T(8,128)S(1)}, u32[]{:S(2)}, u32[]{:S(2)}) %collective-permute-start.3) | collective-permute-done | bytes 262176 | tf_op jit(solution)/shard_map/ppermute | solution.py:335
  51.0 1.4 next_slices.6
  52.4 1.9 collective-permute-start.4
  54.4 3.4 collective-permute-start.5
  59.5 5.2 %collective-permute-done.5.received = f32[8,64,128]{2,1,0:T(8,128)S(1)} collective-permute-done((f32[8,64,128]{2,1,0:T(8,128)S(1)}, f32[8,64,128]{2,1,0:T(8,128)S(1)}, u32[]{:S(2)}, u32[]{:S(2)}) %collective-permute-start.5) | collective-permute-done | bytes 262176 | tf_op jit(solution)/shard_map/ppermute | solution.py:335
  65.8 1.9 collective-permute-start.6
  67.8 3.4 collective-permute-start.7
  73.0 5.2 %collective-permute-done.7.received = f32[8,64,128]{2,1,0:T(8,128)S(1)} collective-permute-done((f32[8,64,128]{2,1,0:T(8,128)S(1)}, f32[8,64,128]{2,1,0:T(8,128)S(1)}, u32[]{:S(2)}, u32[]{:S(2)}) %collective-permute-start.7) | collective-permute-done | bytes 262176 | tf_op jit(solution)/shard_map/ppermute | solution.py:335
  78.2 1.6 next_slices.8
  79.9 1.9 collective-permute-start.8
  81.8 3.4 collective-permute-start.9
  85.1 4.7 %collective-permute-start.10 = (f32[8,64,128]{2,1,0:T(8,128)}, f32[8,64,128]{2,1,0:T(8,128)S(1)}, u32[]{:S(2)}, u32[]{:S(2)}) collective-permute-start(f32[8,64,128]{2,1,0:T(8,128)} %get-tuple-element.37.x.rest_0_.own), channel_id=1, source_target_pairs={{5,0},{4,1},{7,2},{6,3},{0,4},{1,5},{2,6},{3,7},{13,8},{12,9},{15,... | collective-permute-start | bytes 786440 | tf_op jit(solution)/shard_map/ppermute | solution.py:411
  89.8 8.0 %collective-permute-start.11 = (f32[8,64,128]{2,1,0:T(8,128)}, f32[8,64,128]{2,1,0:T(8,128)S(1)}, u32[]{:S(2)}, u32[]{:S(2)}) collective-permute-start(f32[8,64,128]{2,1,0:T(8,128)} %get-tuple-element.37.x.rest_0_.own), channel_id=1, source_target_pairs={{7,0},{6,1},{1,2},{0,3},{3,4},{2,5},{5,6},{4,7},{15,8},{14,9},{9,1... | collective-permute-start | bytes 786440 | tf_op jit(solution)/shard_map/ppermute | solution.py:411
  97.8 1.9 collective-permute-start.12
  99.7 2.3 collective-permute-start.13
  102.0 1.6 own_slice.9.own
  104.9 3.2 collective-permute-done.11.second
  108.1 5.6 %collective-permute-done.12.first = f32[8,64,128]{2,1,0:T(8,128)S(1)} collective-permute-done((f32[8,64,128]{2,1,0:T(8,128)}, f32[8,64,128]{2,1,0:T(8,128)S(1)}, u32[]{:S(2)}, u32[]{:S(2)}) %collective-permute-start.12) | collective-permute-done | bytes 262176 | tf_op jit(solution)/shard_map/ppermute | solution.py:411
  113.7 1.8 products.1
  115.6 24.9 %all_to_all.10.parts = f32[64,8,128]{2,1,0:T(8,128)S(1)} all-to-all(f32[64,8,128]{2,1,0:T(8,128)S(1)} %bitcast.12), channel_id=1, replica_groups=mesh['site'=64,'vec'=8] {'site'}, dimensions={0} | all-to-all | bytes 524288 | tf_op jit(solution)/shard_map/all_to_all | solution.py:427
  140.6 25.0 %all_to_all.11 = f32[64,8,128]{2,1,0:T(8,128)S(1)} all-to-all(f32[64,8,128]{2,1,0:T(8,128)S(1)} %sum_parts.1), channel_id=1, replica_groups=mesh['site'=64,'vec'=8] {'site'}, dimensions={0} | all-to-all | bytes 524288 | tf_op jit(solution)/shard_map/all_to_all | solution.py:431
  166.3 17.1 %all-gather.1 = f32[1280,128]{1,0:T(8,128)S(1)} all-gather(f32[160,128]{1,0:T(8,128)S(1)} %slice.6), channel_id=3, replica_groups=mesh['site'=64,'vec'=8] {'vec'}, dimensions={0}, use_global_device_ids=true | all-gather | bytes 737280 | tf_op jit(solution)/shard_map/all_gather | solution.py:434
  183.4 236.5 %inverse_factor.1 = (bf16[512,512]{1,0:T(8,128)(2,1)S(1)}, bf16[512,512]{1,0:T(8,128)(2,1)S(1)}) custom-call(f32[8,160,128]{2,1,0:T(8,128)S(1)} %bitcast.13), custom_call_target="tpu_custom_call" | custom-call | flops 7247757312 | bytes 2097152 | tf_op jit(solution)/shard_map/inverse_factor/pallas_call | solution.py:436
  419.9 1.3 basis.1
  422.5 2.2 projected.1
  (36 shorter events, 14.1 us)
Async XLA Ops:
  7.2 158.4 %all-gather.6.cloned.1.call-start = ((), (), s32[]{:S(2)}) async-start(), calls=%async_computation.2 | async-start | bytes 2359296 | tf_op jit(solution)/shard_map/all_gather | solution.py:425
  7.2 1.2 copy-start.1
  8.4 22.5 %copy-start.4 = (s32[8,8]{1,0:T(8,128)S(1)}, s32[8,8]{1,0:T(8,128)}, u32[]{:S(2)}) copy-start(s32[8,8]{1,0:T(8,128)} %near.21) | copy-start | bytes 772
  9.8 22.7 %collective-permute-start.1 = (f32[8,64,128]{2,1,0:T(8,128)S(1)}, f32[8,64,128]{2,1,0:T(8,128)S(1)}, u32[]{:S(2)}, u32[]{:S(2)}) collective-permute-start(f32[8,64,128]{2,1,0:T(8,128)S(1)} %get-tuple-element.26), channel_id=1, source_target_pairs={{0,8},{8,16},{16,24},{24,32},{32,40},{40,48},{48,56},{56,64},{64,7... | collective-permute-start | bytes 786440 | tf_op jit(solution)/shard_map/ppermute | solution.py:335
  14.2 18.3 %collective-permute-start = (f32[8,64,128]{2,1,0:T(8,128)}, f32[8,64,128]{2,1,0:T(8,128)S(1)}, u32[]{:S(2)}, u32[]{:S(2)}) collective-permute-start(f32[8,64,128]{2,1,0:T(8,128)} %bitcast.1.x.rest_0_), channel_id=1, source_target_pairs={{0,504},{8,0},{16,8},{24,16},{32,24},{40,32},{48,40},{56,48},{64,5... | collective-permute-start | bytes 786440 | tf_op jit(solution)/shard_map/ppermute | solution.py:335
  26.2 0.7 copy-start.3
  26.9 0.9 copy-start.5
  33.6 10.3 %collective-permute-start.2 = (f32[8,64,128]{2,1,0:T(8,128)S(1)}, f32[8,64,128]{2,1,0:T(8,128)S(1)}, u32[]{:S(2)}, u32[]{:S(2)}) collective-permute-start(f32[8,64,128]{2,1,0:T(8,128)S(1)} %get-tuple-element.31.x.rest_0_), channel_id=1, source_target_pairs={{0,504},{8,0},{16,8},{24,16},{32,24},{40,32},{48,40},{56,48},{64,5... | collective-permute-start | bytes 786440 | tf_op jit(solution)/shard_map/ppermute | solution.py:335
  39.8 11.2 %collective-permute-start.3 = (f32[8,64,128]{2,1,0:T(8,128)S(1)}, f32[8,64,128]{2,1,0:T(8,128)S(1)}, u32[]{:S(2)}, u32[]{:S(2)}) collective-permute-start(f32[8,64,128]{2,1,0:T(8,128)S(1)} %get-tuple-element.32), channel_id=1, source_target_pairs={{0,8},{8,16},{16,24},{24,32},{32,40},{40,48},{48,56},{56,64},{64,7... | collective-permute-start | bytes 786440 | tf_op jit(solution)/shard_map/ppermute | solution.py:335
  52.4 7.1 %collective-permute-start.4 = (f32[8,64,128]{2,1,0:T(8,128)S(1)}, f32[8,64,128]{2,1,0:T(8,128)S(1)}, u32[]{:S(2)}, u32[]{:S(2)}) collective-permute-start(f32[8,64,128]{2,1,0:T(8,128)S(1)} %get-tuple-element.33.x.rest_0_), channel_id=1, source_target_pairs={{0,504},{8,0},{16,8},{24,16},{32,24},{40,32},{48,40},{56,48},{64,5... | collective-permute-start | bytes 786440 | tf_op jit(solution)/shard_map/ppermute | solution.py:335
  54.4 10.4 %collective-permute-start.5 = (f32[8,64,128]{2,1,0:T(8,128)S(1)}, f32[8,64,128]{2,1,0:T(8,128)S(1)}, u32[]{:S(2)}, u32[]{:S(2)}) collective-permute-start(f32[8,64,128]{2,1,0:T(8,128)S(1)} %get-tuple-element.34), channel_id=1, source_target_pairs={{0,8},{8,16},{16,24},{24,32},{32,40},{40,48},{48,56},{56,64},{64,7... | collective-permute-start | bytes 786440 | tf_op jit(solution)/shard_map/ppermute | solution.py:335
  65.8 7.1 %collective-permute-start.6 = (f32[8,64,128]{2,1,0:T(8,128)S(1)}, f32[8,64,128]{2,1,0:T(8,128)S(1)}, u32[]{:S(2)}, u32[]{:S(2)}) collective-permute-start(f32[8,64,128]{2,1,0:T(8,128)S(1)} %get-tuple-element.35.x), channel_id=1, source_target_pairs={{0,504},{8,0},{16,8},{24,16},{32,24},{40,32},{48,40},{56,48},{64,5... | collective-permute-start | bytes 786440 | tf_op jit(solution)/shard_map/ppermute | solution.py:335
  67.8 10.4 %collective-permute-start.7 = (f32[8,64,128]{2,1,0:T(8,128)S(1)}, f32[8,64,128]{2,1,0:T(8,128)S(1)}, u32[]{:S(2)}, u32[]{:S(2)}) collective-permute-start(f32[8,64,128]{2,1,0:T(8,128)S(1)} %get-tuple-element.36), channel_id=1, source_target_pairs={{0,8},{8,16},{16,24},{24,32},{32,40},{40,48},{48,56},{56,64},{64,7... | collective-permute-start | bytes 786440 | tf_op jit(solution)/shard_map/ppermute | solution.py:335
  79.9 19.9 %collective-permute-start.8 = (f32[8,64,128]{2,1,0:T(8,128)}, f32[8,64,128]{2,1,0:T(8,128)S(1)}, u32[]{:S(2)}, u32[]{:S(2)}) collective-permute-start(f32[8,64,128]{2,1,0:T(8,128)} %get-tuple-element.37.x.rest_0_.own), channel_id=1, source_target_pairs={{0,504},{8,0},{16,8},{24,16},{32,24},{40,32},{48,40},{56,48},{64,5... | collective-permute-start | bytes 786440 | tf_op jit(solution)/shard_map/ppermute | solution.py:335
  81.8 21.8 %collective-permute-start.9 = (f32[8,64,128]{2,1,0:T(8,128)S(1)}, f32[8,64,128]{2,1,0:T(8,128)S(1)}, u32[]{:S(2)}, u32[]{:S(2)}) collective-permute-start(f32[8,64,128]{2,1,0:T(8,128)S(1)} %get-tuple-element.38), channel_id=1, source_target_pairs={{0,8},{8,16},{16,24},{24,32},{32,40},{40,48},{48,56},{56,64},{64,7... | collective-permute-start | bytes 786440 | tf_op jit(solution)/shard_map/ppermute | solution.py:335
  85.1 19.7 %collective-permute-start.10 = (f32[8,64,128]{2,1,0:T(8,128)}, f32[8,64,128]{2,1,0:T(8,128)S(1)}, u32[]{:S(2)}, u32[]{:S(2)}) collective-permute-start(f32[8,64,128]{2,1,0:T(8,128)} %get-tuple-element.37.x.rest_0_.own), channel_id=1, source_target_pairs={{5,0},{4,1},{7,2},{6,3},{0,4},{1,5},{2,6},{3,7},{13,8},{12,9},{15,... | collective-permute-start | bytes 786440 | tf_op jit(solution)/shard_map/ppermute | solution.py:411
  89.8 18.3 %collective-permute-start.11 = (f32[8,64,128]{2,1,0:T(8,128)}, f32[8,64,128]{2,1,0:T(8,128)S(1)}, u32[]{:S(2)}, u32[]{:S(2)}) collective-permute-start(f32[8,64,128]{2,1,0:T(8,128)} %get-tuple-element.37.x.rest_0_.own), channel_id=1, source_target_pairs={{7,0},{6,1},{1,2},{0,3},{3,4},{2,5},{5,6},{4,7},{15,8},{14,9},{9,1... | collective-permute-start | bytes 786440 | tf_op jit(solution)/shard_map/ppermute | solution.py:411
  97.8 15.9 %collective-permute-start.12 = (f32[8,64,128]{2,1,0:T(8,128)}, f32[8,64,128]{2,1,0:T(8,128)S(1)}, u32[]{:S(2)}, u32[]{:S(2)}) collective-permute-start(f32[8,64,128]{2,1,0:T(8,128)} %get-tuple-element.37.x.rest_0_.own), channel_id=1, source_target_pairs={{6,0},{7,1},{0,2},{1,3},{2,4},{3,5},{4,6},{5,7},{14,8},{15,9},{8,1... | collective-permute-start | bytes 786440 | tf_op jit(solution)/shard_map/ppermute | solution.py:411
  99.7 14.0 %collective-permute-start.13 = (f32[8,64,128]{2,1,0:T(8,128)}, f32[8,64,128]{2,1,0:T(8,128)S(1)}, u32[]{:S(2)}, u32[]{:S(2)}) collective-permute-start(f32[8,64,128]{2,1,0:T(8,128)} %get-tuple-element.37.x.rest_0_.own), channel_id=1, source_target_pairs={{1,0},{0,1},{3,2},{2,3},{5,4},{4,5},{7,6},{6,7},{9,8},{8,9},{11,10... | collective-permute-start | bytes 786440 | tf_op jit(solution)/shard_map/ppermute | solution.py:411
  115.5 305.7 %all-gather.8.cloned.1.call-start = ((), (), s32[]{:S(2)}) async-start(), calls=%async_computation.3 | async-start | bytes 1179648 | tf_op jit(solution)/shard_map/all_gather | solution.py:433
  183.4 236.5 %copy-start = (f32[4096,128]{1,0:T(8,128)S(1)}, f32[4096,128]{1,0:T(8,128)}, u32[]{:S(2)}) copy-start(f32[4096,128]{1,0:T(8,128)} %all-gather.6.cloned.1.call-done) | copy-start | bytes 6291460
  421.2 1.2 copy-start.2
Sparse Core Ops, SparseCore 0:
  115.7 22.0 all-gather.5
  166.4 24.2 all-gather.7
